TPU v7x, 32 devices: a whole 2x2x4 slice. The times are simulated.
32 devices in a mesh: tile: 8 (over y, x, core), frame: 4 (over z).
Axes of the slice: x: 2, y: 2, z: 4, core: 2. Of those that a mesh axis runs over, the one named last changes fastest.
Arguments:
- video: float32 [16, 16, 160, 128], P('frame', 'tile'), may hold values from -6 to 6
- norm_gain: float32 [2, 2, 128], replicated, may hold values from 0.1 to 1.9
- space_weight: float32 [2, 3, 3, 128, 128], replicated, may hold values from -0.1875 to 0.1875
- time_weight: float32 [2, 3, 128, 128], replicated, may hold values from -0.3125 to 0.3125
- down_weight: float32 [3, 3, 128, 256], replicated, may hold values from -0.1875 to 0.1875
- attn_gain: float32 [256], replicated, may hold values from 0.1 to 1.9
- w_query: float32 [256, 256], replicated, may hold values from -4 to 4
- w_key: float32 [256, 256], replicated, may hold values from -4 to 4
- w_value: float32 [256, 256], replicated, may hold values from -0.375 to 0.375
- w_out: float32 [256, 256], replicated, may hold values from -0.375 to 0.375
Outputs:
- encoded: float32 [32, 320, 256], P(('frame', 'tile'))
All inputs are finite; a program needn't handle non-finite values.
Results may differ from a plain program's by a relative error of at most 0.0003.
Values sent between devices are 32-bit elements; how exact they have to be, the bound alone decides.
No kernel may reach another device: no remote copies, remote signals or barrier semaphores. Data moves between devices by JAX's collectives and lax.ppermute only.
A program may use at most 64 MiB of HBM per device.

v0:
```python
import jax
import jax.numpy as jnp
from jax import lax
from jax.sharding import PartitionSpec as P

highest = lax.Precision.HIGHEST


def passed_along(shard, axis, by):
    size = lax.axis_size(axis)
    pairs = [(i, i + by) for i in range(size) if 0 <= i + by < size]
    return lax.ppermute(shard, axis, pairs)


def extended(cells, sides, width):
    for axis, dim in sides:
        count = lax.axis_size(axis)
        ends = count - 1
        head = lax.slice_in_dim(cells, 0, width, axis=dim)
        tail = lax.slice_in_dim(cells, cells.shape[dim] - width, cells.shape[dim], axis=dim)
        cells = jnp.concatenate(
            [
                lax.ppermute(tail, axis, [(i, (i + 1) % count) for i in range(ends)]),
                cells,
                lax.ppermute(head, axis, [((i + 1) % count, i) for i in range(ends)]),
            ],
            axis=dim,
        )
    return cells


def from_partner(shard, axis, apart):
    return lax.ppermute(shard, axis, [(i, i ^ 1 << apart) for i in range(lax.axis_size(axis))])


def norm(values, gain):
    return values * lax.rsqrt(jnp.mean(values * values, -1, keepdims=True) + 1e-06) * gain


def act(values, gain):
    return jax.nn.silu(norm(values, gain))


def conv_rows(inputs, kernel):
    return lax.conv_general_dilated(
        inputs,
        kernel,
        (1, 1),
        ((0, 0), (1, 1)),
        dimension_numbers=("NHWC", "HWIO", "NHWC"),
        precision=highest,
    )


def time_mix(inputs, kernel):
    earlier = passed_along(inputs[-2:], "frame", 1)
    opening = lax.axis_index("frame") == 0
    start = jnp.where(opening, jnp.concatenate([inputs[:1], inputs[:1]], 0), earlier)
    padded = jnp.concatenate([start, inputs], 0)
    count = inputs.shape[0]
    total = jnp.einsum("fhwc,cd->fhwd", padded[0:count], kernel[0], precision=highest)
    total = total + jnp.einsum("fhwc,cd->fhwd", padded[1 : count + 1], kernel[1], precision=highest)
    total = total + jnp.einsum("fhwc,cd->fhwd", padded[2 : count + 2], kernel[2], precision=highest)
    return total


def fold(carry, query, keys, values):
    best, total, accum = carry
    scores = jnp.dot(query, keys.T, precision=highest)
    new_best = jnp.maximum(best, jnp.max(scores, axis=1))
    factor = jnp.exp(best - new_best)
    weights = jnp.exp(scores - new_best[:, None])
    total = total * factor + jnp.sum(weights, axis=1)
    accum = accum * factor[:, None] + jnp.dot(weights, values, precision=highest)
    return (new_best, total, accum)


def local(
    video,
    norm_gain,
    space_weight,
    time_weight,
    down_weight,
    attn_gain,
    w_query,
    w_key,
    w_value,
    w_out,
):
    frames_dev, rows, width, chans = video.shape
    tiles = lax.axis_size("tile")
    state = video
    for block in range(2):
        wide = extended(act(state, norm_gain[block, 0]), (("tile", 1),), 1)
        mixed = conv_rows(wide, space_weight[block])
        state = state + time_mix(act(mixed, norm_gain[block, 1]), time_weight[block])
    upper = passed_along(state[:, -1:], "tile", 1)
    stacked = jnp.concatenate([upper, state], 1)
    lowered = lax.conv_general_dilated(
        stacked,
        down_weight,
        (2, 2),
        ((0, 0), (1, 0)),
        dimension_numbers=("NHWC", "HWIO", "NHWC"),
        precision=highest,
    )
    outer = lowered.shape[-1]
    group = tiles // frames_dev
    pieces = lowered.reshape(frames_dev * group, -1, outer)
    mine = lax.all_to_all(pieces, "tile", split_axis=0, concat_axis=0, tiled=True).reshape(
        -1, outer
    )
    normed = norm(mine, attn_gain)
    query = jnp.dot(normed, w_query, precision=highest) * float(outer) ** (-0.5)
    count = mine.shape[0]
    carry = (
        jnp.full((count,), -jnp.inf, jnp.float32),
        jnp.zeros((count,), jnp.float32),
        jnp.zeros((count, outer), jnp.float32),
    )
    levels = group.bit_length() - 1
    keys = jnp.dot(normed, w_key, precision=highest)
    values = jnp.dot(normed, w_value, precision=highest)
    carry = fold(carry, query, keys, values)
    for level in range(levels):
        got_keys, got_values = from_partner((keys, values), "tile", level)
        carry = fold(carry, query, got_keys, got_values)
        keys = jnp.concatenate([keys, got_keys], 0)
        values = jnp.concatenate([values, got_values], 0)
    best, total, accum = carry
    attended = accum / total[:, None]
    result = mine + jnp.dot(attended, w_out, precision=highest)
    return result[None]


def solution(mesh):
    in_specs = (P("frame", "tile", None, None), P(), P(), P(), P(), P(), P(), P(), P(), P())
    out_specs = P(("frame", "tile"), None, None)
    return jax.shard_map(local, mesh=mesh, in_specs=in_specs, out_specs=out_specs, check_vma=False)
```

profile of v0, /device:TPU:0, one launch (start us, length us, event | category | flops | bytes accessed | tf_op | source)
XLA Modules:
  0.0 101.9 jit_solution(15611979728672710645)
XLA Ops:
  0.0 0.8 slice_bitcast_fusion.2
  0.8 1.4 %multiply_reduce_fusion.3 = f32[4,2,160]{2,1,0:T(2,128)S(1)} fusion(f32[4,2,160,128]{3,2,1,0:T(8,128)} %param.10), kind=kLoop, calls=%fused_computation.49 | loop fusion | flops 326400 | bytes 660480 | tf_op jit(solution)/shard_map/reduce_sum | solution.py:37
  2.3 1.3 %divide_multiply_fusion.3 = f32[4,2,160,128]{3,2,1,0:T(8,128)S(1)} fusion(f32[4,2,160,128]{3,2,1,0:T(8,128)} %param.10, f32[128]{0:T(128)S(1)} %get-tuple-element.14, f32[4,2,160]{2,1,0:T(2,128)S(1)} %add_rsqrt_fusion.3), kind=kLoop, calls=%fused_computation.48 | loop fusion | flops 983040 | bytes 1316352 | tf_op jit(solution)/shard_map/jit(silu)/mul | solution.py:41
  3.7 2.4 %collective-permute-start = (f32[4,1,160,128]{3,2,1,0:T(8,128)S(1)}, f32[4,1,160,128]{3,2,1,0:T(8,128)S(1)}, u32[]{:S(2)}, u32[]{:S(2)}) collective-permute-start(f32[4,1,160,128]{3,2,1,0:T(8,128)S(1)} %get-tuple-element.9), channel_id=1, source_target_pairs={{0,4},{4,8},{8,12},{12,16},{16,20},{20,24},{24,28},{1,5},{5,9},{9,... | collective-permute-start | bytes 983048 | tf_op jit(solution)/shard_map/ppermute | solution.py:23
  6.1 1.3 %collective-permute-start.1 = (f32[4,1,160,128]{3,2,1,0:T(8,128)S(1)}, f32[4,1,160,128]{3,2,1,0:T(8,128)S(1)}, u32[]{:S(2)}, u32[]{:S(2)}) collective-permute-start(f32[4,1,160,128]{3,2,1,0:T(8,128)S(1)} %get-tuple-element.10), channel_id=1, source_target_pairs={{4,0},{8,4},{12,8},{16,12},{20,16},{24,20},{28,24},{5,1},{9,5},{13... | collective-permute-start | bytes 983048 | tf_op jit(solution)/shard_map/ppermute | solution.py:25
  7.4 4.3 %collective-permute-done.1 = f32[4,1,160,128]{3,2,1,0:T(8,128)S(1)} collective-permute-done((f32[4,1,160,128]{3,2,1,0:T(8,128)S(1)}, f32[4,1,160,128]{3,2,1,0:T(8,128)S(1)}, u32[]{:S(2)}, u32[]{:S(2)}) %collective-permute-start.1) | collective-permute-done | bytes 327712 | tf_op jit(solution)/shard_map/ppermute | solution.py:25
  11.7 0.1 maximum_bitcast_fusion
  11.8 0.8 copy.52
  12.7 0.2 pad.clone
  13.0 0.3 select_maximum_fusion.1
  13.3 0.9 copy-done.2
  14.2 5.3 %multiply_reduce_fusion.1 = (f32[2,32,21]{1,2,0:T(8,128)S(1)}, f32[2,32,21,128]{3,1,2,0:T(8,128)S(1)}) fusion(f32[2,3,3,128,128]{4,3,2,1,0:T(8,128)S(1)} %copy-done.2, f32[4,4,8,23,128]{4,1,3,2,0:T(4,128)S(1)} %select_maximum_fusion.1, pred[32,21]{0,1:T(8,128)(4,1)S(1)} %copy-done.10), kind=kOutput, calls=%fused_computation.37 | convolution fusion | flops 2378685184 | bytes 2793728 | tf_op jit(solution)/shard_map/conv_general_dilated | solution.py:45
  19.5 0.1 copy.32
  19.6 0.1 reshape.110
  19.7 0.5 copy.30
  20.3 0.3 divide_multiply_fusion.2
  20.6 3.5 %collective-permute-start.2 = (f32[2,2,160,128]{3,2,1,0:T(8,128)S(1)}, f32[2,2,160,128]{3,2,1,0:T(8,128)S(1)}, u32[]{:S(2)}, u32[]{:S(2)}) collective-permute-start(f32[2,2,160,128]{3,2,1,0:T(8,128)S(1)} %slice.130), channel_id=1, source_target_pairs={{0,1},{1,2},{2,3},{4,5},{5,6},{6,7},{8,9},{9,10},{10,11},{12,13},{... | collective-permute-start | bytes 983048 | tf_op jit(solution)/shard_map/ppermute | solution.py:12
  24.2 0.7 fusion.40
  24.9 3.8 %collective-permute-done.2 = f32[2,2,160,128]{3,2,1,0:T(8,128)S(1)} collective-permute-done((f32[2,2,160,128]{3,2,1,0:T(8,128)S(1)}, f32[2,2,160,128]{3,2,1,0:T(8,128)S(1)}, u32[]{:S(2)}, u32[]{:S(2)}) %collective-permute-start.2) | collective-permute-done | bytes 327712 | tf_op jit(solution)/shard_map/ppermute | solution.py:12
  28.7 0.7 fusion.22
  29.4 0.9 multiply_reduce_fusion.2
  30.3 0.3 divide_multiply_fusion.1
  30.6 7.2 %collective-permute-start.3 = (f32[4,1,160,128]{3,2,1,0:T(8,128)S(1)}, f32[4,1,160,128]{3,2,1,0:T(8,128)S(1)}, u32[]{:S(2)}, u32[]{:S(2)}) collective-permute-start(f32[4,1,160,128]{3,2,1,0:T(8,128)S(1)} %get-tuple-element.7), channel_id=1, source_target_pairs={{0,4},{4,8},{8,12},{12,16},{16,20},{20,24},{24,28},{1,5},{5,9},{9,... | collective-permute-start | bytes 983048 | tf_op jit(solution)/shard_map/ppermute | solution.py:23
  37.8 1.5 %collective-permute-start.4 = (f32[4,1,160,128]{3,2,1,0:T(8,128)S(1)}, f32[4,1,160,128]{3,2,1,0:T(8,128)S(1)}, u32[]{:S(2)}, u32[]{:S(2)}) collective-permute-start(f32[4,1,160,128]{3,2,1,0:T(8,128)S(1)} %get-tuple-element.8), channel_id=1, source_target_pairs={{4,0},{8,4},{12,8},{16,12},{20,16},{24,20},{28,24},{5,1},{9,5},{13... | collective-permute-start | bytes 983048 | tf_op jit(solution)/shard_map/ppermute | solution.py:25
  39.3 4.8 %collective-permute-done.4 = f32[4,1,160,128]{3,2,1,0:T(8,128)S(1)} collective-permute-done((f32[4,1,160,128]{3,2,1,0:T(8,128)S(1)}, f32[4,1,160,128]{3,2,1,0:T(8,128)S(1)}, u32[]{:S(2)}, u32[]{:S(2)}) %collective-permute-start.4) | collective-permute-done | bytes 327712 | tf_op jit(solution)/shard_map/ppermute | solution.py:25
  44.1 0.1 maximum_bitcast_fusion.1
  44.2 0.8 copy.53
  45.1 0.2 pad.2.clone
  45.3 0.3 select_maximum_fusion
  45.7 0.9 copy-done.3
  46.6 5.3 %multiply_reduce_fusion = (f32[2,32,21]{1,2,0:T(8,128)S(1)}, f32[2,32,21,128]{3,1,2,0:T(8,128)S(1)}) fusion(f32[2,3,3,128,128]{4,3,2,1,0:T(8,128)S(1)} %copy-done.3, f32[4,4,8,23,128]{4,1,3,2,0:T(4,128)S(1)} %select_maximum_fusion, pred[32,21]{0,1:T(8,128)(4,1)S(1)} %copy-done.10), kind=kOutput, calls=%fused_computation.36 | convolution fusion | flops 2378685184 | bytes 2793728 | tf_op jit(solution)/shard_map/conv_general_dilated | solution.py:45
  51.9 0.1 copy.38
  52.0 0.1 reshape.119
  52.1 0.5 copy.36
  52.7 0.3 divide_multiply_fusion
  53.0 4.4 %collective-permute-start.5 = (f32[2,2,160,128]{3,2,1,0:T(8,128)S(1)}, f32[2,2,160,128]{3,2,1,0:T(8,128)S(1)}, u32[]{:S(2)}, u32[]{:S(2)}) collective-permute-start(f32[2,2,160,128]{3,2,1,0:T(8,128)S(1)} %slice.137), channel_id=1, source_target_pairs={{0,1},{1,2},{2,3},{4,5},{5,6},{6,7},{8,9},{9,10},{10,11},{12,13},{... | collective-permute-start | bytes 983048 | tf_op jit(solution)/shard_map/ppermute | solution.py:12
  57.5 0.7 fusion.36
  58.1 3.9 %collective-permute-done.5 = f32[2,2,160,128]{3,2,1,0:T(8,128)S(1)} collective-permute-done((f32[2,2,160,128]{3,2,1,0:T(8,128)S(1)}, f32[2,2,160,128]{3,2,1,0:T(8,128)S(1)}, u32[]{:S(2)}, u32[]{:S(2)}) %collective-permute-start.5) | collective-permute-done | bytes 327712 | tf_op jit(solution)/shard_map/ppermute | solution.py:12
  62.0 0.7 fusion.21
  62.7 0.7 fusion.15
  63.4 8.4 %collective-permute-start.6 = (f32[4,1,160,128]{3,2,1,0:T(8,128)S(1)}, f32[4,1,160,128]{3,2,1,0:T(8,128)S(1)}, u32[]{:S(2)}, u32[]{:S(2)}) collective-permute-start(f32[4,1,160,128]{3,2,1,0:T(8,128)S(1)} %slice.138), channel_id=1, source_target_pairs={{0,4},{4,8},{8,12},{12,16},{16,20},{20,24},{24,28},{1,5},{5,9},{9,... | collective-permute-start | bytes 983048 | tf_op jit(solution)/shard_map/ppermute | solution.py:12
  71.8 1.0 collective-permute-done.6
  72.9 0.6 copy.54
  73.5 0.2 pad.4.clone
  73.7 0.3 select_maximum_fusion.2
  74.0 0.3 copy-done.11
  74.4 1.7 %convolution_select_fusion = f32[1,32,11,256]{3,1,2,0:T(8,128)S(1)} fusion(f32[3,3,128,256]{3,2,1,0:T(8,128)S(1)} %copy-done, f32[3,4,8,24,128]{4,1,3,2,0:T(4,128)S(1)} %select_maximum_fusion.2, pred[32,11]{0,1:T(8,128)(4,1)S(1)} %copy-done.11), kind=kOutput, calls=%fused_computation.19 | convolution fusion | flops 1245798400 | bytes 2720096 | tf_op jit(solution)/shard_map/conv_general_dilated | solution.py:99
  76.1 0.4 copy.42
  76.5 0.2 slice.140
  76.8 17.8 %all_to_all.5 = f32[8,40,256]{2,1,0:T(8,128)S(1)} all-to-all(f32[8,40,256]{2,1,0:T(8,128)S(1)} %bitcast.145), channel_id=1, replica_groups=mesh['tile'=8,'frame'=4] {'tile'}, dimensions={0} | all-to-all | bytes 655360 | tf_op jit(solution)/shard_map/all_to_all | solution.py:110
  94.6 0.1 multiply_reduce_fusion.4
  94.8 0.1 rsqrt.48
  94.9 0.1 fusion.33
  95.0 0.4 fusion.59
  95.4 0.4 fusion.58
  95.9 0.1 collective-permute-start.7
  95.9 0.4 convolution_multiply_fusion
  96.4 0.6 collective-permute-start.8
  96.9 0.7 fusion.56
  97.6 0.7 fusion.57
  98.4 0.2 fusion.31
  98.6 1.1 %fusion.17 = f32[320,256]{1,0:T(8,128)S(1)} fusion(f32[320,256]{1,0:T(8,128)S(1)} %fusion.59, f32[320,320]{0,1:T(8,128)S(1)} %get-tuple-element.23, f32[320]{0:T(512)S(1)} %get-tuple-element.22, f32[320]{0:T(512)S(1)} %get-tuple-element.6, f32[320]{0:T(512)S(1)} %get-tuple-element.11), kind=kOutput, calls=%fused_computation.25 | convolution fusion | flops 314839040 | bytes 1068800 | tf_op jit(solution)/shard_map/dot_general | solution.py:74
  99.7 1.1 %fusion.18 = f32[320,256]{1,0:T(8,128)S(1)} fusion(f32[320,256]{1,0:T(8,128)S(1)} %fusion.17, f32[320,256]{1,0:T(8,128)S(1)} %collective-permute-done.8, f32[320,320]{0,1:T(8,128)S(1)} %get-tuple-element.25, f32[320]{0:T(512)S(1)} %max.13, f32[320]{0:T(512)S(1)} %get-tuple-element.5), kind=kOutput, calls=%fused_computation.26 | convolution fusion | flops 314839040 | bytes 1395200 | tf_op jit(solution)/shard_map/dot_general | solution.py:74
  100.8 1.2 %fusion.16 = f32[1,320,256]{2,1,0:T(8,128)} fusion(f32[320,256]{1,0:T(8,128)S(1)} %bitcast.139, f32[320,256]{1,0:T(8,128)S(1)} %fusion.18, f32[256,256]{1,0:T(8,128)S(1)} %copy-done.9), kind=kOutput, calls=%fused_computation.21 | convolution fusion | flops 251740160 | bytes 1245184 | tf_op jit(solution)/shard_map/dot_general | solution.py:132
  (54 shorter events, 0.6 us)
Async XLA Ops:
  0.0 74.0 %copy-start = (f32[3,3,128,256]{3,2,1,0:T(8,128)S(1)}, f32[3,3,128,256]{3,2,1,0:T(8,128)}, u32[]{:S(2)}) copy-start(f32[3,3,128,256]{3,2,1,0:T(8,128)} %param.14) | copy-start | bytes 3538948
  3.7 3.7 %collective-permute-start = (f32[4,1,160,128]{3,2,1,0:T(8,128)S(1)}, f32[4,1,160,128]{3,2,1,0:T(8,128)S(1)}, u32[]{:S(2)}, u32[]{:S(2)}) collective-permute-start(f32[4,1,160,128]{3,2,1,0:T(8,128)S(1)} %get-tuple-element.9), channel_id=1, source_target_pairs={{0,4},{4,8},{8,12},{12,16},{16,20},{20,24},{24,28},{1,5},{5,9},{9,... | collective-permute-start | bytes 983048 | tf_op jit(solution)/shard_map/ppermute | solution.py:23
  6.1 5.6 %collective-permute-start.1 = (f32[4,1,160,128]{3,2,1,0:T(8,128)S(1)}, f32[4,1,160,128]{3,2,1,0:T(8,128)S(1)}, u32[]{:S(2)}, u32[]{:S(2)}) collective-permute-start(f32[4,1,160,128]{3,2,1,0:T(8,128)S(1)} %get-tuple-element.10), channel_id=1, source_target_pairs={{4,0},{8,4},{12,8},{16,12},{20,16},{24,20},{28,24},{5,1},{9,5},{13... | collective-permute-start | bytes 983048 | tf_op jit(solution)/shard_map/ppermute | solution.py:25
  12.9 1.3 %copy-start.2 = (f32[2,3,3,128,128]{4,3,2,1,0:T(8,128)S(1)}, f32[2,3,3,128,128]{4,3,2,1,0:T(8,128)}, u32[]{:S(2)}) copy-start(f32[2,3,3,128,128]{4,3,2,1,0:T(8,128)} %param.12) | copy-start | bytes 3538948
  12.9 1.3 %copy-start.10 = (pred[32,21]{0,1:T(8,128)(4,1)S(1)}, pred[32,21]{0,1:T(8,128)(4,1)}, u32[]{:S(2)}) copy-start(pred[32,21]{0,1:T(8,128)(4,1)} %constant.47) | copy-start | bytes 2020
  20.3 3.8 %copy-start.4 = (f32[2,3,128,128]{3,2,1,0:T(8,128)S(1)}, f32[2,3,128,128]{3,2,1,0:T(8,128)}, u32[]{:S(2)}) copy-start(f32[2,3,128,128]{3,2,1,0:T(8,128)} %param.13) | copy-start | bytes 1179652
  20.6 8.1 %collective-permute-start.2 = (f32[2,2,160,128]{3,2,1,0:T(8,128)S(1)}, f32[2,2,160,128]{3,2,1,0:T(8,128)S(1)}, u32[]{:S(2)}, u32[]{:S(2)}) collective-permute-start(f32[2,2,160,128]{3,2,1,0:T(8,128)S(1)} %slice.130), channel_id=1, source_target_pairs={{0,1},{1,2},{2,3},{4,5},{5,6},{6,7},{8,9},{9,10},{10,11},{12,13},{... | collective-permute-start | bytes 983048 | tf_op jit(solution)/shard_map/ppermute | solution.py:12
  24.8 4.6 %copy-start.1 = (f32[4,2,160,128]{3,2,1,0:T(8,128)S(1)}, f32[4,2,160,128]{3,2,1,0:T(8,128)}, u32[]{:S(2)}) copy-start(f32[4,2,160,128]{3,2,1,0:T(8,128)} %param.10) | copy-start | bytes 1966084
  30.6 8.7 %collective-permute-start.3 = (f32[4,1,160,128]{3,2,1,0:T(8,128)S(1)}, f32[4,1,160,128]{3,2,1,0:T(8,128)S(1)}, u32[]{:S(2)}, u32[]{:S(2)}) collective-permute-start(f32[4,1,160,128]{3,2,1,0:T(8,128)S(1)} %get-tuple-element.7), channel_id=1, source_target_pairs={{0,4},{4,8},{8,12},{12,16},{16,20},{20,24},{24,28},{1,5},{5,9},{9,... | collective-permute-start | bytes 983048 | tf_op jit(solution)/shard_map/ppermute | solution.py:23
  37.8 6.3 %collective-permute-start.4 = (f32[4,1,160,128]{3,2,1,0:T(8,128)S(1)}, f32[4,1,160,128]{3,2,1,0:T(8,128)S(1)}, u32[]{:S(2)}, u32[]{:S(2)}) collective-permute-start(f32[4,1,160,128]{3,2,1,0:T(8,128)S(1)} %get-tuple-element.8), channel_id=1, source_target_pairs={{4,0},{8,4},{12,8},{16,12},{20,16},{24,20},{28,24},{5,1},{9,5},{13... | collective-permute-start | bytes 983048 | tf_op jit(solution)/shard_map/ppermute | solution.py:25
  45.3 1.3 %copy-start.3 = (f32[2,3,3,128,128]{4,3,2,1,0:T(8,128)S(1)}, f32[2,3,3,128,128]{4,3,2,1,0:T(8,128)}, u32[]{:S(2)}) copy-start(f32[2,3,3,128,128]{4,3,2,1,0:T(8,128)} %param.12) | copy-start | bytes 3538948
  52.7 4.7 %copy-start.5 = (f32[2,3,128,128]{3,2,1,0:T(8,128)S(1)}, f32[2,3,128,128]{3,2,1,0:T(8,128)}, u32[]{:S(2)}) copy-start(f32[2,3,128,128]{3,2,1,0:T(8,128)} %param.13) | copy-start | bytes 1179652
  53.0 9.0 %collective-permute-start.5 = (f32[2,2,160,128]{3,2,1,0:T(8,128)S(1)}, f32[2,2,160,128]{3,2,1,0:T(8,128)S(1)}, u32[]{:S(2)}, u32[]{:S(2)}) collective-permute-start(f32[2,2,160,128]{3,2,1,0:T(8,128)S(1)} %slice.137), channel_id=1, source_target_pairs={{0,1},{1,2},{2,3},{4,5},{5,6},{6,7},{8,9},{9,10},{10,11},{12,13},{... | collective-permute-start | bytes 983048 | tf_op jit(solution)/shard_map/ppermute | solution.py:12
  63.4 9.4 %collective-permute-start.6 = (f32[4,1,160,128]{3,2,1,0:T(8,128)S(1)}, f32[4,1,160,128]{3,2,1,0:T(8,128)S(1)}, u32[]{:S(2)}, u32[]{:S(2)}) collective-permute-start(f32[4,1,160,128]{3,2,1,0:T(8,128)S(1)} %slice.138), channel_id=1, source_target_pairs={{0,4},{4,8},{8,12},{12,16},{16,20},{20,24},{24,28},{1,5},{5,9},{9,... | collective-permute-start | bytes 983048 | tf_op jit(solution)/shard_map/ppermute | solution.py:12
  73.7 0.7 copy-start.11
  76.5 18.3 %copy-start.12 = (f32[256]{0:T(256)S(1)}, f32[256]{0:T(256)}, u32[]{:S(2)}) copy-start(f32[256]{0:T(256)} %param.15) | copy-start | bytes 3076
  76.7 18.2 %copy-start.6 = (f32[256,256]{1,0:T(8,128)S(1)}, f32[256,256]{1,0:T(8,128)}, u32[]{:S(2)}) copy-start(f32[256,256]{1,0:T(8,128)} %param.18) | copy-start | bytes 786436
  76.8 18.6 %copy-start.7 = (f32[256,256]{1,0:T(8,128)S(1)}, f32[256,256]{1,0:T(8,128)}, u32[]{:S(2)}) copy-start(f32[256,256]{1,0:T(8,128)} %param.17) | copy-start | bytes 786436
  94.7 1.2 %copy-start.8 = (f32[256,256]{1,0:T(8,128)S(1)}, f32[256,256]{1,0:T(8,128)}, u32[]{:S(2)}) copy-start(f32[256,256]{1,0:T(8,128)} %param.16) | copy-start | bytes 786436
  95.9 1.8 %collective-permute-start.7 = (f32[320,256]{1,0:T(8,128)S(1)}, f32[320,256]{1,0:T(8,128)S(1)}, u32[]{:S(2)}, u32[]{:S(2)}) collective-permute-start(f32[320,256]{1,0:T(8,128)S(1)} %fusion.58), channel_id=1, source_target_pairs={{0,4},{4,0},{8,12},{12,8},{16,20},{20,16},{24,28},{28,24},{1,5},{5... | collective-permute-start | bytes 983048 | tf_op jit(solution)/shard_map/ppermute | solution.py:33
  96.4 3.3 %collective-permute-start.8 = (f32[320,256]{1,0:T(8,128)S(1)}, f32[320,256]{1,0:T(8,128)S(1)}, u32[]{:S(2)}, u32[]{:S(2)}) collective-permute-start(f32[320,256]{1,0:T(8,128)S(1)} %fusion.59), channel_id=1, source_target_pairs={{0,4},{4,0},{8,12},{12,8},{16,20},{20,16},{24,28},{28,24},{1,5},{5... | collective-permute-start | bytes 983048 | tf_op jit(solution)/shard_map/ppermute | solution.py:33
  98.5 2.2 %copy-start.9 = (f32[256,256]{1,0:T(8,128)S(1)}, f32[256,256]{1,0:T(8,128)}, u32[]{:S(2)}) copy-start(f32[256,256]{1,0:T(8,128)} %param.19) | copy-start | bytes 786436
where the time goes:
time: 102 us
  starting transfers between devices  29.3 us (29%)
  matrix products  22.6 us (22%)
  waiting for transfers between devices  17.8 us (17%)
  blocking collectives  17.8 us (17%)
  local copies, waits for them, and re-layouts  8.5 us (8%)
  other arithmetic  5.25 us (5%)
    all_to_all x1, blocking collectives, local(): lax.all_to_all(pieces, 'tile', split_axis=0, concat_axis=0, tiled=True)  17.8 us
    ppermute x3, starting transfers between devices, passed_along(): return lax.ppermute(shard, axis, pairs)  16.3 us
    conv_general_dilated x2, matrix products, conv_rows(): lax.conv_general_dilated(inputs, kernel, (1, 1), ((0, 0), (1, 1)), dimens...  10.6 us
    ppermute x2, starting transfers between devices, extended(): lax.ppermute(tail, axis, [(i, (i + 1) % count) for i in range(ends)])  9.63 us
    ppermute x2, waiting for transfers between devices, extended(): lax.ppermute(head, axis, [((i + 1) % count, i) for i in range(ends)])  9.07 us
    ppermute x3, waiting for transfers between devices, passed_along(): return lax.ppermute(shard, axis, pairs)  8.69 us
    unnamed x30, local copies, waits for them, and re-layouts  4.61 us
    ppermute x2, starting transfers between devices, extended(): lax.ppermute(head, axis, [((i + 1) % count, i) for i in range(ends)])  2.76 us
  transfers between devices with their start and end apart: 9, of which 5 were waited for; matrix products, arithmetic and copies ran while one was open for 4% of the time, Pallas kernels for 0%

commit v1 on v0

v1 whole, which is shorter than its diff:
```python
import functools

import jax
import jax.numpy as jnp
from jax import lax
from jax.experimental import pallas as pl
from jax.experimental.pallas import tpu as pltpu
from jax.sharding import PartitionSpec as P

F32, BF16 = jnp.float32, jnp.bfloat16
VM = pl.BlockSpec(memory_space=pltpu.VMEM)


def call(body, outs, *args, name, flops=0):
    outs = [jax.ShapeDtypeStruct(shape, kind) for shape, kind in outs]
    moved = sum(a.size * a.dtype.itemsize for a in args) + sum(o.size * o.dtype.itemsize for o in outs)
    return pl.pallas_call(
        body,
        out_shape=outs,
        in_specs=[VM] * len(args),
        out_specs=[VM] * len(outs),
        name=name,
        compiler_params=pltpu.CompilerParams(vmem_limit_bytes=28 << 20),
        cost_estimate=pl.CostEstimate(flops=flops, bytes_accessed=moved, transcendentals=0),
    )(*args)


def halves(values):
    high = values.astype(BF16)
    return high, (values - high.astype(F32)).astype(BF16)


def left_side(values):
    high, low = halves(values)
    return jnp.concatenate([high, low, high], -1)


def right_side(values):
    high, low = halves(values)
    return jnp.concatenate([high, high, low], 0)


def mul(left, right):
    return jnp.dot(left, right, preferred_element_type=F32)


def norm(values, gain):
    return values * lax.rsqrt(jnp.mean(values * values, -1, keepdims=True) + 1e-06) * gain


def act(values, gain):
    y = norm(values, gain)
    return y / (1.0 + jnp.exp(-y))


def taps(values):
    n, w, c = values.shape
    at = lax.broadcasted_iota(jnp.int32, values.shape, 1)
    before = jnp.where(at == 0, 0.0, pltpu.roll(values, 1, 1))
    after = jnp.where(at == w - 1, 0.0, pltpu.roll(values, w - 1, 1))
    return left_side(jnp.concatenate([before, values, after], -1).reshape(n * w, 3 * c))


def pack_space(space_ref, out_ref):
    c = space_ref.shape[-1]
    for kh in range(3):
        for kw in range(3):
            high, low = halves(space_ref[kh, kw])
            cols = slice((2 - kh) * c, (3 - kh) * c)
            out_ref[kw * c : (kw + 1) * c, cols] = high
            out_ref[(3 + kw) * c : (4 + kw) * c, cols] = high
            out_ref[(6 + kw) * c : (7 + kw) * c, cols] = low


def pack_time(time_ref, out_ref):
    c = time_ref.shape[-1]
    for k in range(3):
        out_ref[:, (2 - k) * c : (3 - k) * c] = right_side(time_ref[k])


def pack_down(down_ref, out_ref):
    for kh in range(3):
        out_ref[kh] = right_side(jnp.concatenate([down_ref[kh, kw] for kw in range(3)], 0))


def pack_attn(q_ref, k_ref, v_ref, o_ref, kv_out, q_out, o_out):
    d = q_ref.shape[0]
    kv_out[:, :d] = right_side(k_ref[...])
    kv_out[:, d:] = right_side(v_ref[...])
    q_out[...] = right_side(q_ref[...])
    o_out[...] = right_side(o_ref[...])


def is_even():
    return lax.rem(lax.axis_index("tile"), 2) == 0


def conv_near(block, x_ref, near_ref, gain_ref, weight_ref, out_ref):
    n, rows, w, c = x_ref.shape
    gain = gain_ref[block, 0]
    total = [None] * rows

    def add(row, part):
        total[row] = part if total[row] is None else total[row] + part

    for row in range(rows):
        left = taps(act(x_ref[:, row], gain))
        first, last = max(row - 1, 0), min(row + 1, rows - 1)
        product = mul(left, weight_ref[:, (first - row + 1) * c : (last - row + 2) * c])
        for at in range(first, last + 1):
            add(at, product[:, (at - first) * c : (at - first + 1) * c])
    for row in range(rows):
        out_ref[:, row] = total[row].reshape(n, w, c)
    even = is_even()
    col = pl.multiple_of(jnp.where(even, 0, 2 * c), c)
    row = jnp.where(even, rows - 1, 0)
    left = taps(act(near_ref[...], gain))
    product = mul(left, weight_ref[:, pl.ds(col, c)]).reshape(n, w, c)
    out_ref[:, row] = out_ref[:, row] + product


def conv_far(block, part_ref, far_ref, gain_ref, weight_ref, out_ref):
    n, rows, w, c = part_ref.shape
    even = is_even()
    tile = lax.axis_index("tile")
    inside = jnp.logical_and(tile > 0, tile < lax.axis_size("tile") - 1)
    col = pl.multiple_of(jnp.where(even, 2 * c, 0), c)
    row = jnp.where(even, 0, rows - 1)
    far = jnp.where(inside, far_ref[...], 0.0)
    left = taps(act(far, gain_ref[block, 0]))
    product = mul(left, weight_ref[:, pl.ds(col, c)]).reshape(n, w, c)
    gain = gain_ref[block, 1]
    out_ref[...] = act(part_ref[...], gain)
    out_ref[:, row] = act(part_ref[:, row] + product, gain)


def mix_own(x_ref, u_ref, weight_ref, *out_refs):
    n, rows, w, c = x_ref.shape
    total = [x_ref[f].reshape(rows * w, c) for f in range(n)]
    for f in range(n):
        left = left_side(u_ref[f].reshape(rows * w, c))
        wide = min(3, n - f)
        product = mul(left, weight_ref[:, : wide * c])
        for k in range(wide):
            total[f + k] = total[f + k] + product[:, k * c : (k + 1) * c]
    early_ref, late_refs = out_refs[0], out_refs[1:]
    for f in range(min(n, 2)):
        early_ref[f] = total[f].reshape(rows, w, c)
    if late_refs:
        for f in range(2, n):
            late_refs[0][f - 2] = total[f].reshape(rows, w, c)
        ends(late_refs)


def ends(refs):
    if len(refs) > 1:
        x_ref, near_ref, far_ref = refs
        rows = x_ref.shape[1]
        even = is_even()
        near_ref[...] = x_ref[:, jnp.where(even, rows - 1, 0)]
        far_ref[...] = x_ref[:, jnp.where(even, 0, rows - 1)]


def mix_earlier(x_ref, u_ref, got_ref, weight_ref, *out_refs):
    n, rows, w, c = x_ref.shape
    opening = lax.axis_index("frame") == 0
    first = u_ref[0].reshape(rows * w, c)
    before = jnp.where(opening, first, got_ref[0].reshape(rows * w, c))
    last = jnp.where(opening, first, got_ref[1].reshape(rows * w, c))
    near = mul(left_side(last), weight_ref[:, c:])
    far = mul(left_side(before), weight_ref[:, 2 * c :])
    out_ref = out_refs[0]
    out_ref[0] = x_ref[0] + (near[:, :c] + far).reshape(rows, w, c)
    out_ref[1] = x_ref[1] + near[:, c:].reshape(rows, w, c)
    ends(out_refs)


def pixels(ref, n, w):
    c = ref.shape[-1]
    even = ref[pl.ds(0, n * w // 2, stride=2), :]
    odd = ref[pl.ds(1, n * w // 2, stride=2), :]
    half = w // 2
    odd3 = odd.reshape(n, half, c)
    at = lax.broadcasted_iota(jnp.int32, odd3.shape, 1)
    before = jnp.where(at == 0, 0.0, pltpu.roll(odd3, 1, 1)).reshape(n * half, c)
    return left_side(jnp.concatenate([before, even, odd], -1))


def down_own(early_ref, late_ref, weight_ref, out_ref, flat_ref):
    refs = [early_ref] + ([late_ref] if late_ref is not None else [])
    _, rows, w, c = early_ref.shape
    at = 0
    for ref in refs:
        n = ref.shape[0]
        parts = []
        for row in range(rows):
            flat_ref[: n * w] = ref[:, row].reshape(n * w, c)
            parts.append(pixels(flat_ref.at[: n * w], n, w))
        for row in range(rows // 2):
            total = mul(parts[2 * row], weight_ref[1]) + mul(parts[2 * row + 1], weight_ref[2])
            if row:
                total = total + mul(parts[2 * row - 1], weight_ref[0])
            out_ref[at : at + n, row] = total.reshape(n, w // 2, -1)
        at += n


def down_above(part_ref, above_ref, weight_ref, out_ref, flat_ref):
    n, w, c = above_ref.shape
    above = jnp.where(lax.axis_index("tile") > 0, above_ref[...], 0.0)
    flat_ref[...] = above.reshape(n * w, c)
    product = mul(pixels(flat_ref, n, w), weight_ref[0])
    out_ref[...] = part_ref[...]
    out_ref[:, 0] = part_ref[:, 0] + product.reshape(n, w // 2, -1)


def keys_values(z_ref, gain_ref, weight_ref, k_ref, v_ref):
    d = z_ref.shape[-1]
    normed = norm(z_ref[...].reshape(-1, d), gain_ref[0])
    both = mul(left_side(normed), weight_ref[...])
    high, low = halves(both[:, :d])
    k_ref[:, :d] = high
    k_ref[:, d : 2 * d] = high
    k_ref[:, 2 * d :] = low
    v_ref[...] = right_side(both[:, d:]).reshape(v_ref.shape)


def attend(query_ref, gain_ref, wq_ref, wo_ref, *refs):
    out_ref = refs[-1]
    pieces = [(refs[i], refs[i + 1]) for i in range(0, len(refs) - 1, 2)]
    d = query_ref.shape[-1]
    mine = query_ref[...]
    query = mul(left_side(norm(mine, gain_ref[0])), wq_ref[...]) * float(d) ** (-0.5)
    left = left_side(query)
    scores = [
        lax.dot_general(left, k_ref[...], (((1,), (1,)), ((), ())), preferred_element_type=F32)
        for k_ref, _ in pieces
    ]
    best = functools.reduce(jnp.maximum, [jnp.max(s, -1, keepdims=True) for s in scores])
    total, mixed = 0.0, 0.0
    for s, (_, v_ref) in zip(scores, pieces):
        weights = jnp.exp(s - best)
        total = total + jnp.sum(weights, -1, keepdims=True)
        high, low = halves(weights)
        v = v_ref[...]
        mixed = mixed + (mul(high, v[0]) + mul(low, v[1]) + mul(high, v[2]))
    mixed = mixed / total
    out_ref[...] = mine + mul(left_side(mixed), wo_ref[...])


def local(
    video,
    norm_gain,
    space_weight,
    time_weight,
    down_weight,
    attn_gain,
    w_query,
    w_key,
    w_value,
    w_out,
):
    n, rows, w, c = video.shape
    tiles, spans = lax.axis_size("tile"), lax.axis_size("frame")
    tile = lax.axis_index("tile")
    even = lax.rem(tile, 2) == 0
    outer = down_weight.shape[-1]
    late = n > 2
    pairs = [(i, i ^ 1) for i in range(tiles)]
    across = [(i, (i + 1 if i % 2 else i - 1) % tiles) for i in range(tiles)]
    onward = [(i, (i + 1) % spans) for i in range(spans)]
    below = [(i, (i + 1) % tiles) for i in range(tiles)]

    def at_row(x, row):
        return lax.dynamic_index_in_dim(x, row, 1, keepdims=False)

    def pack(body, shape, *args, name):
        return call(body, [(shape, BF16)], *args, name=name)[0]

    near_row, far_row = jnp.where(even, rows - 1, 0), jnp.where(even, 0, rows - 1)
    far = lax.ppermute(at_row(video, far_row), "tile", across)
    near = lax.ppermute(at_row(video, near_row), "tile", pairs)
    space = [pack(pack_space, (9 * c, 3 * c), space_weight[j], name=f"pack_space{j}") for j in range(2)]
    times = [pack(pack_time, (3 * c, 3 * c), time_weight[j], name=f"pack_time{j}") for j in range(2)]
    down = pack(pack_down, (3, 9 * c, outer), down_weight, name="pack_down")
    wkv, wq, wo = call(
        pack_attn,
        [((3 * outer, 2 * outer), BF16), ((3 * outer, outer), BF16), ((3 * outer, outer), BF16)],
        w_query,
        w_key,
        w_value,
        w_out,
        name="pack_attn",
    )

    def conv(block, x, near, far, tag):
        shape = x.shape
        (part,) = call(functools.partial(conv_near, block), [(shape, F32)], x, near, norm_gain, space[block], name=f"near{tag}")
        (u,) = call(functools.partial(conv_far, block), [(shape, F32)], part, far, norm_gain, space[block], name=f"far{tag}")
        return u

    def mix(block, x, u):
        got = lax.ppermute(u[n - 2 :], "frame", onward)
        size = (2, rows, w, c)
        edge = (2, w, c)
        outs = [(size, F32)]
        if late:
            outs.append(((n - 2, rows, w, c), F32))
            if block == 0:
                outs += [((n - 2, w, c), F32)] * 2
        own = call(mix_own, outs, x, u, times[block], name=f"own{block}")
        outs = [(size, F32)] + ([(edge, F32)] * 2 if block == 0 else [])
        early = call(mix_earlier, outs, own[0], u, got, times[block], name=f"earlier{block}")
        return early, own[1:]

    u = conv(0, video, near, far, "0")
    early, behind = mix(0, video, u)
    pieces = []
    for tag, group in (("1b", behind), ("1a", early)):
        if group:
            x, near, far = group
            far = lax.ppermute(far, "tile", across)
            near = lax.ppermute(near, "tile", pairs)
            pieces.append(conv(1, x, near, far, tag))
    x = jnp.concatenate([early[0]] + ([behind[0]] if late else []), 0)
    u = jnp.concatenate(pieces[::-1], 0)
    early, behind = mix(1, x, u)
    x = jnp.concatenate([early[0]] + ([behind[0]] if late else []), 0)
    above = lax.ppermute(x[:, rows - 1], "tile", below)
    zshape = (n, rows // 2, w // 2, outer)

    def own_down(x_ref, weight_ref, out_ref, flat_ref):
        down_own(x_ref, None, weight_ref, out_ref, flat_ref)

    def piece(body, args, name):
        return pl.pallas_call(
            body,
            out_shape=jax.ShapeDtypeStruct(zshape, F32),
            in_specs=[VM] * len(args),
            out_specs=VM,
            scratch_shapes=[pltpu.VMEM((n * w, c), F32)],
            name=name,
            compiler_params=pltpu.CompilerParams(vmem_limit_bytes=28 << 20),
            cost_estimate=pl.CostEstimate(flops=0, bytes_accessed=1 << 20, transcendentals=0),
        )(*args)

    z = piece(own_down, (x, down), "down_own")
    z = piece(down_above, (z, above, down), "down_above")

    group = tiles // n
    tokens = z.reshape(n, -1, outer)
    count = tokens.shape[1]
    mine = tile // group

    def frame_of(index):
        return lax.dynamic_index_in_dim(tokens, index, 0, keepdims=False)

    held = [frame_of(mine)]
    for step in range(1, n):
        pairing = [(i, i ^ (step * group)) for i in range(tiles)]
        held.append(lax.ppermute(frame_of(mine ^ step), "tile", pairing))
    gain = attn_gain.reshape(1, outer)

    def project(z, tag):
        total = z.shape[0] * z.shape[1]
        return call(
            keys_values,
            [((total, 3 * outer), BF16), ((3, total, outer), BF16)],
            z,
            gain,
            wkv,
            name=f"kv{tag}",
        )

    frame = jnp.stack(held)[:, None]
    kv = project(frame.reshape(n, count, outer), "0")
    for level in range(group.bit_length() - 1):
        pairing = [(i, i ^ (1 << level)) for i in range(tiles)]
        got = lax.ppermute(frame, "tile", pairing)
        kv += project(got.reshape(-1, count, outer), str(level + 1))
        frame = jnp.concatenate([frame, got], 1)
    frame = frame.reshape(tiles, group, count // group, outer)
    order = jnp.arange(tiles) ^ tile
    query = lax.dynamic_index_in_dim(frame, tile % group, 1, keepdims=False)[order]
    query = query.reshape(-1, outer)
    (result,) = call(attend, [(query.shape, F32)], query, gain, wq, wo, *kv, name="attend")
    return result[None]


def solution(mesh):
    in_specs = (P("frame", "tile", None, None), P(), P(), P(), P(), P(), P(), P(), P(), P())
    out_specs = P(("frame", "tile"), None, None)
    return jax.shard_map(local, mesh=mesh, in_specs=in_specs, out_specs=out_specs, check_vma=False)
```

time: 102 us -> 57.1 us (0.56)
  matrix products: 22.6 us -> 0 us
  blocking collectives: 17.8 us -> 0 us
  starting transfers between devices: 29.3 us -> 15.4 us
  Pallas kernels: 0 us -> 13.7 us
  waiting for transfers between devices: 17.8 us -> 22.8 us
  other arithmetic: 5.25 us -> 0.26 us
  local copies, waits for them, and re-layouts: 8.5 us -> 4.27 us
    all_to_all x1 -> x0, blocking collectives: 17.8 us -> none  [local(): lax.all_to_all(pieces, 'tile', split_axis=0, concat_axis=0, tiled=True)]
    ppermute x9 -> x13, starting transfers between devices: 29.3 us -> 15.4 us  [the longest x2 3.73 us: local(): far = lax.ppermute(far, 'tile', across)]
    pallas_call x0 -> x21, Pallas kernels: none -> 13.7 us  [the longest x19 12.7 us: call(): pl.pallas_call(body, out_shape=outs, in_specs=[VM] * len(args), out_specs...]
    conv_general_dilated x3 -> x0, matrix products: 12.3 us -> none  [the longest x2 10.6 us: conv_rows(): lax.conv_general_dilated(inputs, kernel, (1, 1), ((0, 0), (1, 1)), dimens...]
    dot_general x14 -> x0, matrix products: 10.2 us -> none  [the longest x2 2.17 us: fold(): jnp.dot(weights, values, precision=highest)]
    ppermute x9 -> x13, waiting for transfers between devices: 17.8 us -> 22.8 us  [the longest x2 7.27 us: local(): far = lax.ppermute(far, 'tile', across)]
    unnamed x30 -> x20, local copies, waits for them, and re-layouts: 4.61 us -> 2.25 us
    mul x5 -> x0, other arithmetic: 2.21 us -> none  [the longest x4 2.09 us: act(): return jax.nn.silu(norm(values, gain))]
  transfers between devices with their start and end apart: 9 -> 13, of which waited for: 5 -> 10; matrix products, arithmetic and copies ran while one was open for 4% -> 0% of each run, Pallas kernels for 0% -> 14%
where the time goes in v1:
time: 57.1 us; the launch traced here: 56.9 us
  waiting for transfers between devices  22.8 us (40%)
  starting transfers between devices  15.4 us (27%)
  Pallas kernels  13.7 us (24%)
  local copies, waits for them, and re-layouts  4.27 us (7%)
    pallas_call x19, Pallas kernels, call(): pl.pallas_call(body, out_shape=outs, in_specs=[VM] * len(args), out_specs...  12.7 us
    ppermute x2, waiting for transfers between devices, local(): far = lax.ppermute(far, 'tile', across)  7.27 us
    ppermute x1, waiting for transfers between devices, local(): above = lax.ppermute(x[:, rows - 1], 'tile', below)  5.15 us
    ppermute x1, waiting for transfers between devices, local(): far = lax.ppermute(at_row(video, far_row), 'tile', across)  4.68 us
    ppermute x2, starting transfers between devices, local(): far = lax.ppermute(far, 'tile', across)  3.73 us
    ppermute x2, starting transfers between devices, mix(): got = lax.ppermute(u[n - 2:], 'frame', onward)  3.58 us
    ppermute x3, starting transfers between devices, local(): held.append(lax.ppermute(frame_of(mine ^ step), 'tile', pairing))  3.55 us
    ppermute x1, starting transfers between devices, local(): far = lax.ppermute(at_row(video, far_row), 'tile', across)  3.54 us
  transfers between devices with their start and end apart: 13, of which 10 were waited for; matrix products, arithmetic and copies ran while one was open for 0% of the time, Pallas kernels for 14%

profile of v1, /device:TPU:0, one launch (start us, length us, event | category | flops | bytes accessed | tf_op | source)
XLA Modules:
  0.0 56.9 jit_solution(10624418912858605332)
XLA Ops:
  0.0 1.2 %dynamic-slice_bitcast_fusion.1 = (f32[4,160,128]{2,1,0:T(8,128)S(1)}, f32[4,160,128]{2,1,0:T(8,128)S(1)}) fusion(f32[4,2,160,128]{3,2,1,0:T(8,128)} %x_ref.3, s32[]{:T(128)S(6)} %select_n.49, s32[]{:T(128)S(6)} %select_n.48), kind=kLoop, calls=%fused_computation.13 | loop fusion | bytes 1310728 | tf_op jit(solution)/shard_map/jit(dynamic_index_in_dim)/squeeze | solution.py:274
  1.2 0.6 collective-permute-start
  1.8 3.5 %collective-permute-start.1 = (f32[4,160,128]{2,1,0:T(8,128)S(1)}, f32[4,160,128]{2,1,0:T(8,128)S(1)}, u32[]{:S(2)}, u32[]{:S(2)}) collective-permute-start(f32[4,160,128]{2,1,0:T(8,128)S(1)} %get-tuple-element.39), channel_id=1, source_target_pairs={{0,28},{4,8},{8,4},{12,16},{16,12},{20,24},{24,20},{28,0},{1,29},{... | collective-permute-start | bytes 983048 | tf_op jit(solution)/shard_map/ppermute | solution.py:280
  5.3 0.1 slice_bitcast_fusion
  5.4 0.0 copy-start
  5.4 0.0 copy-start.6
  5.4 0.1 pack_space0.1.weight_ref
  5.6 0.0 collective-permute-done.near_ref
  5.6 0.9 %copy-done = f32[4,2,160,128]{3,2,1,0:T(8,128)S(1)} copy-done((f32[4,2,160,128]{3,2,1,0:T(8,128)S(1)}, f32[4,2,160,128]{3,2,1,0:T(8,128)}, u32[]{:S(2)}) %copy-start) | copy-done | bytes 655384
  6.5 0.0 copy-done.6
  6.5 1.6 %near0.1.part_ref = f32[4,2,160,128]{3,2,1,0:T(8,128)S(1)} custom-call(f32[4,2,160,128]{3,2,1,0:T(8,128)S(1)} %copy-done, f32[4,160,128]{2,1,0:T(8,128)S(1)} %collective-permute-done.near_ref, f32[2,2,128]{2,1,0:T(2,128)S(1)} %copy-done.6, bf16[1152,384]{1,0:T(8,128)(2,1)S(1)} %pack_space0.1.weight_ref), custom_call_target="tpu_custom_call" | custom-call | bytes 2525184 | tf_op jit(solution)/shard_map/near0/pallas_call | solution.py:17
  8.1 0.0 copy-start.9
  8.1 4.7 %collective-permute-done.1.far_ref = f32[4,160,128]{2,1,0:T(8,128)S(1)} collective-permute-done((f32[4,160,128]{2,1,0:T(8,128)S(1)}, f32[4,160,128]{2,1,0:T(8,128)S(1)}, u32[]{:S(2)}, u32[]{:S(2)}) %collective-permute-start.1) | collective-permute-done | bytes 327712 | tf_op jit(solution)/shard_map/ppermute | solution.py:280
  12.8 0.9 %far0.1.u_ref = f32[4,2,160,128]{3,2,1,0:T(8,128)S(1)} custom-call(f32[4,2,160,128]{3,2,1,0:T(8,128)S(1)} %near0.1.part_ref, f32[4,160,128]{2,1,0:T(8,128)S(1)} %collective-permute-done.1.far_ref, f32[2,2,128]{2,1,0:T(2,128)S(1)} %copy-done.6, bf16[1152,384]{1,0:T(8,128)(2,1)S(1)} %pack_space0.1.weight_ref), custom_call_target="tpu_custom_call" | custom-call | bytes 2525184 | tf_op jit(solution)/shard_map/far0/pallas_call | solution.py:17
  13.7 1.9 %collective-permute-start.2 = (f32[2,2,160,128]{3,2,1,0:T(8,128)S(1)}, f32[2,2,160,128]{3,2,1,0:T(8,128)S(1)}, u32[]{:S(2)}, u32[]{:S(2)}) collective-permute-start(f32[2,2,160,128]{3,2,1,0:T(8,128)S(1)} %slice.26), channel_id=1, source_target_pairs={{0,1},{1,2},{2,3},{3,0},{4,5},{5,6},{6,7},{7,4},{8,9},{9,10},{10,1... | collective-permute-start | bytes 983048 | tf_op jit(solution)/shard_map/ppermute | solution.py:302
  15.6 0.0 copy-done.9
  15.7 0.7 %own0.1 = (f32[2,2,160,128]{3,2,1,0:T(8,128)S(1)}, f32[2,2,160,128]{3,2,1,0:T(8,128)S(1)}, f32[2,160,128]{2,1,0:T(8,128)S(1)}, f32[2,160,128]{2,1,0:T(8,128)S(1)}) custom-call(f32[4,2,160,128]{3,2,1,0:T(8,128)S(1)} %copy-done, f32[4,2,160,128]{3,2,1,0:T(8,128)S(1)} %far0.1.u_ref, bf16[384,384]{1,0:T(8,128)(2,1)S(1)} %pack_time0.1.weight_ref), custom_call_target="tpu_custom_call" | custom-call | bytes 2588672 | tf_op jit(solution)/shard_map/own0/pallas_call | solution.py:17
  16.4 0.1 collective-permute-start.5
  16.4 1.8 %collective-permute-start.6 = (f32[2,160,128]{2,1,0:T(8,128)S(1)}, f32[2,160,128]{2,1,0:T(8,128)S(1)}, u32[]{:S(2)}, u32[]{:S(2)}) collective-permute-start(f32[2,160,128]{2,1,0:T(8,128)S(1)} %get-tuple-element.27), channel_id=1, source_target_pairs={{0,28},{4,8},{8,4},{12,16},{16,12},{20,24},{24,20},{28,0},{1,29},{... | collective-permute-start | bytes 491528 | tf_op jit(solution)/shard_map/ppermute | solution.py:321
  18.2 0.1 pack_space1.1.weight_ref
  18.3 0.0 collective-permute-done.5.near_ref
  18.3 0.9 %near1b.1.part_ref = f32[2,2,160,128]{3,2,1,0:T(8,128)S(1)} custom-call(f32[2,2,160,128]{3,2,1,0:T(8,128)S(1)} %get-tuple-element.23.x_ref, f32[2,160,128]{2,1,0:T(8,128)S(1)} %collective-permute-done.5.near_ref, f32[2,2,128]{2,1,0:T(2,128)S(1)} %copy-done.6, bf16[1152,384]{1,0:T(8,128)(2,1)S(1)} %pack_space1.1.weight_ref), custom_call_target="tpu_custom_call" | custom-call | bytes 1705984 | tf_op jit(solution)/shard_map/near1b/pallas_call | solution.py:17
  19.3 3.6 %collective-permute-done.6.far_ref = f32[2,160,128]{2,1,0:T(8,128)S(1)} collective-permute-done((f32[2,160,128]{2,1,0:T(8,128)S(1)}, f32[2,160,128]{2,1,0:T(8,128)S(1)}, u32[]{:S(2)}, u32[]{:S(2)}) %collective-permute-start.6) | collective-permute-done | bytes 163872 | tf_op jit(solution)/shard_map/ppermute | solution.py:321
  22.9 0.6 %far1b.1 = f32[2,2,160,128]{3,2,1,0:T(8,128)S(1)} custom-call(f32[2,2,160,128]{3,2,1,0:T(8,128)S(1)} %near1b.1.part_ref, f32[2,160,128]{2,1,0:T(8,128)S(1)} %collective-permute-done.6.far_ref, f32[2,2,128]{2,1,0:T(2,128)S(1)} %copy-done.6, bf16[1152,384]{1,0:T(8,128)(2,1)S(1)} %pack_space1.1.weight_ref), custom_call_target="tpu_custom_call" | custom-call | bytes 1705984 | tf_op jit(solution)/shard_map/far1b/pallas_call | solution.py:17
  23.5 1.6 %collective-permute-start.7 = (f32[2,2,160,128]{3,2,1,0:T(8,128)S(1)}, f32[2,2,160,128]{3,2,1,0:T(8,128)S(1)}, u32[]{:S(2)}, u32[]{:S(2)}) collective-permute-start(f32[2,2,160,128]{3,2,1,0:T(8,128)S(1)} %far1b.1), channel_id=1, source_target_pairs={{0,1},{1,2},{2,3},{3,0},{4,5},{5,6},{6,7},{7,4},{8,9},{9,10},{10,1... | collective-permute-start | bytes 983048 | tf_op jit(solution)/shard_map/ppermute | solution.py:302
  25.1 0.5 collective-permute-done.2.got_ref
  25.6 0.4 earlier0.1
  26.0 0.1 collective-permute-start.3
  26.1 2.0 %collective-permute-start.4 = (f32[2,160,128]{2,1,0:T(8,128)S(1)}, f32[2,160,128]{2,1,0:T(8,128)S(1)}, u32[]{:S(2)}, u32[]{:S(2)}) collective-permute-start(f32[2,160,128]{2,1,0:T(8,128)S(1)} %get-tuple-element.25), channel_id=1, source_target_pairs={{0,28},{4,8},{8,4},{12,16},{16,12},{20,24},{24,20},{28,0},{1,29},{... | collective-permute-start | bytes 491528 | tf_op jit(solution)/shard_map/ppermute | solution.py:321
  28.2 0.0 collective-permute-done.3.near_ref
  28.2 0.9 %near1a.1.part_ref = f32[2,2,160,128]{3,2,1,0:T(8,128)S(1)} custom-call(f32[2,2,160,128]{3,2,1,0:T(8,128)S(1)} %get-tuple-element.22.x_ref, f32[2,160,128]{2,1,0:T(8,128)S(1)} %collective-permute-done.3.near_ref, f32[2,2,128]{2,1,0:T(2,128)S(1)} %copy-done.6, bf16[1152,384]{1,0:T(8,128)(2,1)S(1)} %pack_space1.1.weight_ref), custom_call_target="tpu_custom_call" | custom-call | bytes 1705984 | tf_op jit(solution)/shard_map/near1a/pallas_call | solution.py:17
  29.1 3.6 %collective-permute-done.4.far_ref = f32[2,160,128]{2,1,0:T(8,128)S(1)} collective-permute-done((f32[2,160,128]{2,1,0:T(8,128)S(1)}, f32[2,160,128]{2,1,0:T(8,128)S(1)}, u32[]{:S(2)}, u32[]{:S(2)}) %collective-permute-start.4) | collective-permute-done | bytes 163872 | tf_op jit(solution)/shard_map/ppermute | solution.py:321
  32.8 0.6 %far1a.1 = f32[2,2,160,128]{3,2,1,0:T(8,128)S(1)} custom-call(f32[2,2,160,128]{3,2,1,0:T(8,128)S(1)} %near1a.1.part_ref, f32[2,160,128]{2,1,0:T(8,128)S(1)} %collective-permute-done.4.far_ref, f32[2,2,128]{2,1,0:T(2,128)S(1)} %copy-done.6, bf16[1152,384]{1,0:T(8,128)(2,1)S(1)} %pack_space1.1.weight_ref), custom_call_target="tpu_custom_call" | custom-call | bytes 1705984 | tf_op jit(solution)/shard_map/far1a/pallas_call | solution.py:17
  33.4 0.6 %own1.1 = (f32[2,2,160,128]{3,2,1,0:T(8,128)S(1)}, f32[2,2,160,128]{3,2,1,0:T(8,128)S(1)}) custom-call(f32[4,2,160,128]{3,2,1,0:T(8,128)S(1)} %pad_maximum_fusion.1.x_ref, f32[4,2,160,128]{3,2,1,0:T(8,128)S(1)} %pad_maximum_fusion.2.u_ref, bf16[384,384]{1,0:T(8,128)(2,1)S(1)} %pack_time1.1.weight_ref), custom_call_target="tpu_custom_call" | custom-call | bytes 2260992 | tf_op jit(solution)/shard_map/own1/pallas_call | solution.py:17
  34.0 1.1 %collective-permute-done.7.got_ref = f32[2,2,160,128]{3,2,1,0:T(8,128)S(1)} collective-permute-done((f32[2,2,160,128]{3,2,1,0:T(8,128)S(1)}, f32[2,2,160,128]{3,2,1,0:T(8,128)S(1)}, u32[]{:S(2)}, u32[]{:S(2)}) %collective-permute-start.7) | collective-permute-done | bytes 327712 | tf_op jit(solution)/shard_map/ppermute | solution.py:302
  35.1 0.3 earlier1.1
  35.5 0.2 collective-permute-start.8
  35.8 0.0 copy-start.1
  35.8 1.3 %copy-done.1 = f32[3,3,128,256]{3,2,1,0:T(8,128)S(1)} copy-done((f32[3,3,128,256]{3,2,1,0:T(8,128)S(1)}, f32[3,3,128,256]{3,2,1,0:T(8,128)}, u32[]{:S(2)}) %copy-start.1) | copy-done | bytes 1179672
  37.1 0.2 pack_down.1.weight_ref
  37.4 0.6 %down_own.1.part_ref = f32[4,1,80,256]{3,2,1,0:T(8,128)S(1)} custom-call(f32[4,2,160,128]{3,2,1,0:T(8,128)S(1)} %pad_maximum_fusion.x_ref, bf16[3,1152,256]{2,1,0:T(8,128)(2,1)S(1)} %pack_down.1.weight_ref), custom_call_target="tpu_custom_call" | custom-call | bytes 1048576 | tf_op jit(solution)/shard_map/down_own/pallas_call | solution.py:335
  38.0 5.1 %collective-permute-done.8.above_ref = f32[4,160,128]{2,1,0:T(8,128)S(1)} collective-permute-done((f32[4,160,128]{2,1,0:T(8,128)S(1)}, f32[4,160,128]{2,1,0:T(8,128)S(1)}, u32[]{:S(2)}, u32[]{:S(2)}) %collective-permute-start.8) | collective-permute-done | bytes 327712 | tf_op jit(solution)/shard_map/ppermute | solution.py:328
  43.1 0.4 down_above.1
  43.5 0.0 copy-start.2
  43.5 0.0 copy-start.3
  43.6 0.0 copy-start.4
  43.6 0.0 copy-start.5
  43.6 0.0 copy-start.7
  43.6 0.1 collective-permute-start.11
  43.7 2.3 %collective-permute-start.10 = (f32[80,256]{1,0:T(8,128)S(1)}, f32[80,256]{1,0:T(8,128)S(1)}, u32[]{:S(2)}, u32[]{:S(2)}) collective-permute-start(f32[80,256]{1,0:T(8,128)S(1)} %get-tuple-element.47), channel_id=1, source_target_pairs={{0,16},{4,20},{8,24},{12,28},{16,0},{20,4},{24,8},{28,12},{1,17},{... | collective-permute-start | bytes 245768 | tf_op jit(solution)/shard_map/ppermute | solution.py:360
  46.0 1.2 %collective-permute-start.9 = (f32[80,256]{1,0:T(8,128)S(1)}, f32[80,256]{1,0:T(8,128)S(1)}, u32[]{:S(2)}, u32[]{:S(2)}) collective-permute-start(f32[80,256]{1,0:T(8,128)S(1)} %get-tuple-element.48), channel_id=1, source_target_pairs={{0,8},{4,12},{8,0},{12,4},{16,24},{20,28},{24,16},{28,20},{1,9},{5... | collective-permute-start | bytes 245768 | tf_op jit(solution)/shard_map/ppermute | solution.py:360
  47.2 2.0 %collective-permute-done.11 = f32[80,256]{1,0:T(8,128)S(1)} collective-permute-done((f32[80,256]{1,0:T(8,128)S(1)}, f32[80,256]{1,0:T(8,128)S(1)}, u32[]{:S(2)}, u32[]{:S(2)}) %collective-permute-start.11) | collective-permute-done | bytes 81952 | tf_op jit(solution)/shard_map/ppermute | solution.py:360
  49.1 0.1 collective-permute-done.10
  49.3 1.1 %collective-permute-done.9 = f32[80,256]{1,0:T(8,128)S(1)} collective-permute-done((f32[80,256]{1,0:T(8,128)S(1)}, f32[80,256]{1,0:T(8,128)S(1)}, u32[]{:S(2)}, u32[]{:S(2)}) %collective-permute-start.9) | collective-permute-done | bytes 81952 | tf_op jit(solution)/shard_map/ppermute | solution.py:360
  50.5 0.1 collective-permute-start.12
  50.6 0.0 copy-done.2
  50.6 0.0 copy-done.3
  50.6 0.2 pack_attn.1
  50.9 0.5 kv0.1
  51.4 0.8 %collective-permute-done.12 = f32[4,1,80,256]{3,2,0,1:T(8,128)S(1)} collective-permute-done((f32[4,1,80,256]{3,2,0,1:T(8,128)S(1)}, f32[4,1,80,256]{3,2,0,1:T(8,128)S(1)}, u32[]{:S(2)}, u32[]{:S(2)}) %collective-permute-start.12) | collective-permute-done | bytes 327712 | tf_op jit(solution)/shard_map/ppermute | solution.py:378
  52.2 0.1 copy.17
  52.3 0.5 kv1.1
  52.8 0.6 %gather_fusion = f32[8,40,256]{2,1,0:T(8,128)S(1)} fusion(f32[8,40,256]{2,1,0:T(8,128)S(1)} %dynamic-slice_bitcast_fusion, s32[1024]{0:T(1024)S(1)} %pad_clamp_fusion), kind=kCustom, calls=%fused_computation | custom fusion | bytes 655392 | tf_op jit(solution)/shard_map/gather | solution.py:383
  53.4 3.5 %attend.1 = f32[320,256]{1,0:T(8,128)} custom-call(f32[320,256]{1,0:T(8,128)S(1)} %bitcast.39, f32[1,256]{1,0:T(1,128)S(1)} %bitcast.42, bf16[768,256]{1,0:T(8,128)(2,1)S(1)} %get-tuple-element.30.wq_ref, bf16[768,256]{1,0:T(8,128)(2,1)S(1)} %get-tuple-element.31.wo_ref, bf16[320,768]{1,0:T(8,128)(2,1)S(1)} %get-tuple-element.33.refs_0_, ...), custom_call_target="tpu_custom_call" | custom-call | bytes 3408896 | tf_op jit(solution)/shard_map/attend/pallas_call | solution.py:17
  (19 shorter events, 0.5 us)
Async XLA Ops:
  0.0 5.3 %copy-start.8 = (f32[2,3,3,128,128]{4,3,2,1,0:T(8,128)S(1)}, f32[2,3,3,128,128]{4,3,2,1,0:T(8,128)}, u32[]{:S(2)}) copy-start(f32[2,3,3,128,128]{4,3,2,1,0:T(8,128)} %param.12) | copy-start | bytes 3538948
  1.2 4.3 %collective-permute-start = (f32[4,160,128]{2,1,0:T(8,128)S(1)}, f32[4,160,128]{2,1,0:T(8,128)S(1)}, u32[]{:S(2)}, u32[]{:S(2)}) collective-permute-start(f32[4,160,128]{2,1,0:T(8,128)S(1)} %get-tuple-element.40), channel_id=1, source_target_pairs={{0,4},{4,0},{8,12},{12,8},{16,20},{20,16},{24,28},{28,24},{1,5},{5... | collective-permute-start | bytes 983048 | tf_op jit(solution)/shard_map/ppermute | solution.py:281
  1.8 11.0 %collective-permute-start.1 = (f32[4,160,128]{2,1,0:T(8,128)S(1)}, f32[4,160,128]{2,1,0:T(8,128)S(1)}, u32[]{:S(2)}, u32[]{:S(2)}) collective-permute-start(f32[4,160,128]{2,1,0:T(8,128)S(1)} %get-tuple-element.39), channel_id=1, source_target_pairs={{0,28},{4,8},{8,4},{12,16},{16,12},{20,24},{24,20},{28,0},{1,29},{... | collective-permute-start | bytes 983048 | tf_op jit(solution)/shard_map/ppermute | solution.py:280
  5.4 1.1 %copy-start = (f32[4,2,160,128]{3,2,1,0:T(8,128)S(1)}, f32[4,2,160,128]{3,2,1,0:T(8,128)}, u32[]{:S(2)}) copy-start(f32[4,2,160,128]{3,2,1,0:T(8,128)} %x_ref.3) | copy-start | bytes 1966084
  5.4 1.1 %copy-start.6 = (f32[2,2,128]{2,1,0:T(2,128)S(1)}, f32[2,2,128]{2,1,0:T(2,128)}, u32[]{:S(2)}) copy-start(f32[2,2,128]{2,1,0:T(2,128)} %gain_ref.11) | copy-start | bytes 6148
  8.1 7.6 %copy-start.9 = (f32[2,3,128,128]{3,2,1,0:T(8,128)S(1)}, f32[2,3,128,128]{3,2,1,0:T(8,128)}, u32[]{:S(2)}) copy-start(f32[2,3,128,128]{3,2,1,0:T(8,128)} %param.13) | copy-start | bytes 1179652
  13.7 12.0 %collective-permute-start.2 = (f32[2,2,160,128]{3,2,1,0:T(8,128)S(1)}, f32[2,2,160,128]{3,2,1,0:T(8,128)S(1)}, u32[]{:S(2)}, u32[]{:S(2)}) collective-permute-start(f32[2,2,160,128]{3,2,1,0:T(8,128)S(1)} %slice.26), channel_id=1, source_target_pairs={{0,1},{1,2},{2,3},{3,0},{4,5},{5,6},{6,7},{7,4},{8,9},{9,10},{10,1... | collective-permute-start | bytes 983048 | tf_op jit(solution)/shard_map/ppermute | solution.py:302
  16.4 2.0 %collective-permute-start.5 = (f32[2,160,128]{2,1,0:T(8,128)S(1)}, f32[2,160,128]{2,1,0:T(8,128)S(1)}, u32[]{:S(2)}, u32[]{:S(2)}) collective-permute-start(f32[2,160,128]{2,1,0:T(8,128)S(1)} %get-tuple-element.26), channel_id=1, source_target_pairs={{0,4},{4,0},{8,12},{12,8},{16,20},{20,16},{24,28},{28,24},{1,5},{5... | collective-permute-start | bytes 491528 | tf_op jit(solution)/shard_map/ppermute | solution.py:322
  16.4 6.5 %collective-permute-start.6 = (f32[2,160,128]{2,1,0:T(8,128)S(1)}, f32[2,160,128]{2,1,0:T(8,128)S(1)}, u32[]{:S(2)}, u32[]{:S(2)}) collective-permute-start(f32[2,160,128]{2,1,0:T(8,128)S(1)} %get-tuple-element.27), channel_id=1, source_target_pairs={{0,28},{4,8},{8,4},{12,16},{16,12},{20,24},{24,20},{28,0},{1,29},{... | collective-permute-start | bytes 491528 | tf_op jit(solution)/shard_map/ppermute | solution.py:321
  23.5 11.6 %collective-permute-start.7 = (f32[2,2,160,128]{3,2,1,0:T(8,128)S(1)}, f32[2,2,160,128]{3,2,1,0:T(8,128)S(1)}, u32[]{:S(2)}, u32[]{:S(2)}) collective-permute-start(f32[2,2,160,128]{3,2,1,0:T(8,128)S(1)} %far1b.1), channel_id=1, source_target_pairs={{0,1},{1,2},{2,3},{3,0},{4,5},{5,6},{6,7},{7,4},{8,9},{9,10},{10,1... | collective-permute-start | bytes 983048 | tf_op jit(solution)/shard_map/ppermute | solution.py:302
  26.0 2.1 %collective-permute-start.3 = (f32[2,160,128]{2,1,0:T(8,128)S(1)}, f32[2,160,128]{2,1,0:T(8,128)S(1)}, u32[]{:S(2)}, u32[]{:S(2)}) collective-permute-start(f32[2,160,128]{2,1,0:T(8,128)S(1)} %get-tuple-element.24), channel_id=1, source_target_pairs={{0,4},{4,0},{8,12},{12,8},{16,20},{20,16},{24,28},{28,24},{1,5},{5... | collective-permute-start | bytes 491528 | tf_op jit(solution)/shard_map/ppermute | solution.py:322
  26.1 6.7 %collective-permute-start.4 = (f32[2,160,128]{2,1,0:T(8,128)S(1)}, f32[2,160,128]{2,1,0:T(8,128)S(1)}, u32[]{:S(2)}, u32[]{:S(2)}) collective-permute-start(f32[2,160,128]{2,1,0:T(8,128)S(1)} %get-tuple-element.25), channel_id=1, source_target_pairs={{0,28},{4,8},{8,4},{12,16},{16,12},{20,24},{24,20},{28,0},{1,29},{... | collective-permute-start | bytes 491528 | tf_op jit(solution)/shard_map/ppermute | solution.py:321
  35.5 7.6 %collective-permute-start.8 = (f32[4,160,128]{2,1,0:T(8,128)S(1)}, f32[4,160,128]{2,1,0:T(8,128)S(1)}, u32[]{:S(2)}, u32[]{:S(2)}) collective-permute-start(f32[4,160,128]{2,1,0:T(8,128)S(1)} %fusion.1), channel_id=1, source_target_pairs={{0,4},{4,8},{8,12},{12,16},{16,20},{20,24},{24,28},{28,0},{1,5},{5... | collective-permute-start | bytes 983048 | tf_op jit(solution)/shard_map/ppermute | solution.py:328
  35.8 1.3 %copy-start.1 = (f32[3,3,128,256]{3,2,1,0:T(8,128)S(1)}, f32[3,3,128,256]{3,2,1,0:T(8,128)}, u32[]{:S(2)}) copy-start(f32[3,3,128,256]{3,2,1,0:T(8,128)} %down_ref.1) | copy-start | bytes 3538948
  43.5 7.0 %copy-start.2 = (f32[256,256]{1,0:T(8,128)S(1)}, f32[256,256]{1,0:T(8,128)}, u32[]{:S(2)}) copy-start(f32[256,256]{1,0:T(8,128)} %q_ref.1) | copy-start | bytes 786436
  43.5 7.0 %copy-start.3 = (f32[256,256]{1,0:T(8,128)S(1)}, f32[256,256]{1,0:T(8,128)}, u32[]{:S(2)}) copy-start(f32[256,256]{1,0:T(8,128)} %k_ref.1) | copy-start | bytes 786436
  43.6 7.0 %copy-start.4 = (f32[256,256]{1,0:T(8,128)S(1)}, f32[256,256]{1,0:T(8,128)}, u32[]{:S(2)}) copy-start(f32[256,256]{1,0:T(8,128)} %v_ref.1) | copy-start | bytes 786436
  43.6 7.0 %copy-start.5 = (f32[256,256]{1,0:T(8,128)S(1)}, f32[256,256]{1,0:T(8,128)}, u32[]{:S(2)}) copy-start(f32[256,256]{1,0:T(8,128)} %o_ref.1) | copy-start | bytes 786436
  43.6 7.2 %copy-start.7 = (f32[256]{0:T(256)S(1)}, f32[256]{0:T(256)}, u32[]{:S(2)}) copy-start(f32[256]{0:T(256)} %param.15) | copy-start | bytes 3076
  43.6 5.5 %collective-permute-start.11 = (f32[80,256]{1,0:T(8,128)S(1)}, f32[80,256]{1,0:T(8,128)S(1)}, u32[]{:S(2)}, u32[]{:S(2)}) collective-permute-start(f32[80,256]{1,0:T(8,128)S(1)} %get-tuple-element.46), channel_id=1, source_target_pairs={{0,24},{4,28},{8,16},{12,20},{16,8},{20,12},{24,0},{28,4},{1,25},{... | collective-permute-start | bytes 245768 | tf_op jit(solution)/shard_map/ppermute | solution.py:360
  43.7 5.6 %collective-permute-start.10 = (f32[80,256]{1,0:T(8,128)S(1)}, f32[80,256]{1,0:T(8,128)S(1)}, u32[]{:S(2)}, u32[]{:S(2)}) collective-permute-start(f32[80,256]{1,0:T(8,128)S(1)} %get-tuple-element.47), channel_id=1, source_target_pairs={{0,16},{4,20},{8,24},{12,28},{16,0},{20,4},{24,8},{28,12},{1,17},{... | collective-permute-start | bytes 245768 | tf_op jit(solution)/shard_map/ppermute | solution.py:360
  46.0 4.4 %collective-permute-start.9 = (f32[80,256]{1,0:T(8,128)S(1)}, f32[80,256]{1,0:T(8,128)S(1)}, u32[]{:S(2)}, u32[]{:S(2)}) collective-permute-start(f32[80,256]{1,0:T(8,128)S(1)} %get-tuple-element.48), channel_id=1, source_target_pairs={{0,8},{4,12},{8,0},{12,4},{16,24},{20,28},{24,16},{28,20},{1,9},{5... | collective-permute-start | bytes 245768 | tf_op jit(solution)/shard_map/ppermute | solution.py:360
  50.5 1.7 %collective-permute-start.12 = (f32[4,1,80,256]{3,2,0,1:T(8,128)S(1)}, f32[4,1,80,256]{3,2,0,1:T(8,128)S(1)}, u32[]{:S(2)}, u32[]{:S(2)}) collective-permute-start(f32[4,1,80,256]{3,2,0,1:T(8,128)S(1)} %get-tuple-element.44), channel_id=1, source_target_pairs={{0,4},{4,0},{8,12},{12,8},{16,20},{20,16},{24,28},{28,24},{1,5},{5... | collective-permute-start | bytes 983048 | tf_op jit(solution)/shard_map/ppermute | solution.py:378

commit v2 on v0

v2 whole, which is shorter than its diff:
```python
import functools

import jax
import jax.numpy as jnp
from jax import lax
from jax.experimental import pallas as pl
from jax.experimental.pallas import tpu as pltpu
from jax.sharding import PartitionSpec as P

F32, BF16 = jnp.float32, jnp.bfloat16
VM = pl.BlockSpec(memory_space=pltpu.VMEM)


def call(body, outs, *args, name, flops=0):
    outs = [jax.ShapeDtypeStruct(shape, kind) for shape, kind in outs]
    moved = sum(a.size * a.dtype.itemsize for a in args) + sum(o.size * o.dtype.itemsize for o in outs)
    return pl.pallas_call(
        body,
        out_shape=outs,
        in_specs=[VM] * len(args),
        out_specs=[VM] * len(outs),
        name=name,
        compiler_params=pltpu.CompilerParams(vmem_limit_bytes=28 << 20),
        cost_estimate=pl.CostEstimate(flops=flops, bytes_accessed=moved, transcendentals=0),
    )(*args)


def halves(values):
    high = values.astype(BF16)
    return high, (values - high.astype(F32)).astype(BF16)


def left_side(values):
    high, low = halves(values)
    return jnp.concatenate([high, low, high], -1)


def right_side(values):
    high, low = halves(values)
    return jnp.concatenate([high, high, low], 0)


def mul(left, right):
    return jnp.dot(left, right, preferred_element_type=F32)


def norm(values, gain):
    return values * lax.rsqrt(jnp.mean(values * values, -1, keepdims=True) + 1e-06) * gain


def act(values, gain):
    y = norm(values, gain)
    return y / (1.0 + jnp.exp(-y))


def taps(values):
    n, w, c = values.shape
    at = lax.broadcasted_iota(jnp.int32, values.shape, 1)
    before = jnp.where(at == 0, 0.0, pltpu.roll(values, 1, 1))
    after = jnp.where(at == w - 1, 0.0, pltpu.roll(values, w - 1, 1))
    return left_side(jnp.concatenate([before, values, after], -1).reshape(n * w, 3 * c))


def is_even():
    return lax.rem(lax.axis_index("tile"), 2) == 0


def pack_space(space_ref, out_ref):
    c = space_ref.shape[-1]
    for kh in range(3):
        at = jnp.where(is_even(), kh, 2 - kh)
        for kw in range(3):
            high, low = halves(space_ref[at, kw])
            cols = slice((2 - kh) * c, (3 - kh) * c)
            out_ref[kw * c : (kw + 1) * c, cols] = high
            out_ref[(3 + kw) * c : (4 + kw) * c, cols] = high
            out_ref[(6 + kw) * c : (7 + kw) * c, cols] = low


def pack_time(time_ref, *out_refs):
    c = time_ref.shape[-1]
    for block, out_ref in enumerate(out_refs):
        for k in range(3):
            out_ref[:, (2 - k) * c : (3 - k) * c] = right_side(time_ref[block, k])


def pack_down(down_ref, out_ref):
    for kh in range(3):
        out_ref[kh] = right_side(jnp.concatenate([down_ref[kh, kw] for kw in range(3)], 0))


def pack_attn(q_ref, k_ref, v_ref, o_ref, kv_out, q_out, o_out):
    d = q_ref.shape[0]
    kv_out[:, :d] = right_side(k_ref[...])
    kv_out[:, d:] = right_side(v_ref[...])
    q_out[...] = right_side(q_ref[...])
    o_out[...] = right_side(o_ref[...])


def conv_near(block, far_ref, near_ref, partner_ref, gain_ref, weight_ref, u_ref, part_ref):
    n, rest, w, c = near_ref.shape
    rows = rest + 1
    gain = gain_ref[block, 0]
    total = [None] * rows

    def add(row, part):
        total[row] = part if total[row] is None else total[row] + part

    for row in range(rows + 1):
        if row == rows:
            values = partner_ref[...]
        else:
            values = near_ref[:, row - 1] if row else far_ref[...]
        left = taps(act(values, gain))
        first, last = max(row - 1, 0), min(row + 1, rows - 1)
        product = mul(left, weight_ref[:, (first - row + 1) * c : (last - row + 2) * c])
        for at in range(first, last + 1):
            add(at, product[:, (at - first) * c : (at - first + 1) * c])
    part_ref[...] = total[0].reshape(n, w, c)
    for row in range(1, rows):
        u_ref[:, row - 1] = act(total[row], gain_ref[block, 1]).reshape(n, w, c)


def conv_far(block, part_ref, beyond_ref, gain_ref, weight_ref, u_ref):
    n, w, c = part_ref.shape
    tile = lax.axis_index("tile")
    inside = jnp.logical_and(tile > 0, tile < lax.axis_size("tile") - 1)
    beyond = jnp.where(inside, beyond_ref[...], 0.0)
    left = taps(act(beyond, gain_ref[block, 0]))
    product = mul(left, weight_ref[:, 2 * c :]).reshape(n, w, c)
    u_ref[...] = act(part_ref[...] + product, gain_ref[block, 1])


def mix_own(groups, x_refs, u_refs, weight_ref, out_refs):
    places = [(g, f) for g in range(groups) for f in range(x_refs[g].shape[0])]
    c = x_refs[0].shape[-1]
    shape = x_refs[0].shape[1:]
    total = [x_refs[g][f].reshape(-1, c) for g, f in places]
    for at, (g, f) in enumerate(places):
        left = left_side(u_refs[g][f].reshape(-1, c))
        wide = min(3, len(places) - at)
        product = mul(left, weight_ref[:, : wide * c])
        for k in range(wide):
            total[at + k] = total[at + k] + product[:, k * c : (k + 1) * c]
    for at, (g, f) in enumerate(places):
        out_refs[g][f] = total[at].reshape(shape)


def mix_earlier(x_ref, u_ref, got_ref, weight_ref, out_ref):
    c = x_ref.shape[-1]
    shape = x_ref.shape[1:]
    opening = lax.axis_index("frame") == 0
    first = u_ref[0].reshape(-1, c)
    before = jnp.where(opening, first, got_ref[0].reshape(-1, c))
    last = jnp.where(opening, first, got_ref[1].reshape(-1, c))
    near = mul(left_side(last), weight_ref[:, c:])
    far = mul(left_side(before), weight_ref[:, 2 * c :])
    out_ref[0] = x_ref[0] + (near[:, :c] + far).reshape(shape)
    out_ref[1] = x_ref[1] + near[:, c:].reshape(shape)


def pixels(ref, n, w):
    c = ref.shape[-1]
    half = w // 2
    even = ref[pl.ds(0, n * half, stride=2), :]
    odd = ref[pl.ds(1, n * half, stride=2), :]
    odd3 = odd.reshape(n, half, c)
    at = lax.broadcasted_iota(jnp.int32, odd3.shape, 1)
    before = jnp.where(at == 0, 0.0, pltpu.roll(odd3, 1, 1)).reshape(n * half, c)
    return left_side(jnp.concatenate([before, even, odd], -1))


def down_rows(groups, far_refs, near_refs, weight_ref, out_refs, flat_ref, held_ref):
    rows = near_refs[0].shape[1] + 1
    w, c = far_refs[0].shape[1:]
    even = is_even()

    def held(g, row):
        return near_refs[g][:, row - 1] if row else far_refs[g][...]

    start = 0
    for g in range(groups):
        n = far_refs[g].shape[0]
        parts = []
        for row in range(rows):
            values = jnp.where(even, held(g, row), held(g, rows - 1 - row))
            flat_ref[: n * w] = values.reshape(n * w, c)
            parts.append(pixels(flat_ref.at[: n * w], n, w))
        for row in range(rows // 2 + 1):
            total = None
            for kh in range(3):
                at = 2 * row - 1 + kh
                if 0 <= at < rows:
                    product = mul(parts[at], weight_ref[kh])
                    total = product if total is None else total + product
            held_ref[start : start + n, row] = total.reshape(n, w // 2, -1)
        start += n
    mine = lax.axis_index("tile") // (lax.axis_size("tile") // start)
    for step in range(start):
        out_refs[step][...] = held_ref[mine ^ step]


def attend(count, *refs):
    pieces = refs[:count]
    gain_ref, wkv_ref, wq_ref, wo_ref, out_ref, z_ref, query_ref, k_ref, v_ref = refs[count:]
    rows, w, d = pieces[0].shape
    rows -= 1
    tile = lax.axis_index("tile")
    for m in range(count):
        z_ref[tile ^ m] = pieces[m][:rows].reshape(rows * w, d)
    for m in range(count):
        at = (tile ^ m) + 1
        z_ref[at, :w] = z_ref[at, :w] + pieces[m][rows]
    gain = gain_ref[0]
    size = rows * w
    step = min(count, 8)
    for at in range(0, count, step):
        normed = norm(z_ref[at : at + step].reshape(step * size, d), gain)
        both = mul(left_side(normed), wkv_ref[...])
        tokens = slice(at * size, (at + step) * size)
        high, low = halves(both[:, :d])
        k_ref[tokens, :d] = high
        k_ref[tokens, d : 2 * d] = high
        k_ref[tokens, 2 * d :] = low
        high, low = halves(both[:, d:])
        v_ref[0, tokens] = high
        v_ref[1, tokens] = low
    part = out_ref.shape[0] // count
    for block in range(size // part):

        @pl.when(lax.rem(tile, size // part) == block)
        def _():
            for b in range(count):
                query_ref[b * part : (b + 1) * part] = z_ref[b, block * part : (block + 1) * part]

    mine = query_ref[...]
    query = mul(left_side(norm(mine, gain)), wq_ref[...]) * float(d) ** (-0.5)
    scores = lax.dot_general(
        left_side(query), k_ref[...], (((1,), (1,)), ((), ())), preferred_element_type=F32
    )
    weights = jnp.exp(scores - jnp.max(scores, -1, keepdims=True))
    total = jnp.sum(weights, -1, keepdims=True)
    high, low = halves(weights)
    mixed = mul(high, v_ref[0]) + mul(low, v_ref[0]) + mul(high, v_ref[1])
    out_ref[...] = mine + mul(left_side(mixed / total), wo_ref[...])


def local(
    video,
    norm_gain,
    space_weight,
    time_weight,
    down_weight,
    attn_gain,
    w_query,
    w_key,
    w_value,
    w_out,
):
    n, rows, w, c = video.shape
    tiles, spans = lax.axis_size("tile"), lax.axis_size("frame")
    even = lax.rem(lax.axis_index("tile"), 2) == 0
    outer = down_weight.shape[-1]
    if n == 3:
        raise ValueError("three frames")
    pairs = [(i, i ^ 1) for i in range(tiles)]
    across = [(i, (i + 1 if i % 2 else i - 1) % tiles) for i in range(tiles)]
    onward = [(i, (i + 1) % spans) for i in range(spans)]
    early, late = slice(0, 2), slice(2, n)
    ranges = [early, late] if n > 2 else [early]
    groups = len(ranges)

    def row(j):
        at = jnp.where(even, j, rows - 1 - j)
        return lax.dynamic_index_in_dim(video, at, 1, keepdims=False)

    def fold(x):
        return lax.ppermute(x, "tile", pairs)

    def cross(x):
        return lax.ppermute(x, "tile", across)

    def shift(x):
        return lax.ppermute(x[-2:], "frame", onward)

    far_all = row(0)
    near_all = jnp.stack([row(j) for j in range(1, rows)], 1)
    far = [far_all[r] for r in ranges]
    near = [near_all[r] for r in ranges]
    beyond = [None] * groups
    for g in reversed(range(groups)):
        beyond[g] = cross(far[g])
    partner_all = fold(near_all[:, -1])
    partner = [partner_all[r] for r in ranges]

    space = [
        call(pack_space, [((9 * c, 3 * c), BF16)], space_weight[j], name=f"pack_space{j}")[0] for j in range(2)
    ]
    times = call(pack_time, [((3 * c, 3 * c), BF16)] * 2, time_weight, name="pack_time")
    (down,) = call(pack_down, [((3, 9 * c, outer), BF16)], down_weight, name="pack_down")
    wkv, wq, wo = call(
        pack_attn,
        [((3 * outer, 2 * outer), BF16), ((3 * outer, outer), BF16), ((3 * outer, outer), BF16)],
        w_query,
        w_key,
        w_value,
        w_out,
        name="pack_attn",
    )

    def near_conv(block, g, far, near, partner):
        return call(
            functools.partial(conv_near, block),
            [(near.shape, F32), (far.shape, F32)],
            far,
            near,
            partner,
            norm_gain,
            space[block],
            name=f"near{block}{g}",
        )

    def far_conv(block, g, part, beyond):
        return call(
            functools.partial(conv_far, block),
            [(part.shape, F32)],
            part,
            beyond,
            norm_gain,
            space[block],
            name=f"far{block}{g}",
        )[0]

    def mix(block, x, u, tag):
        def body(*refs):
            mix_own(groups, refs[:groups], refs[groups : 2 * groups], refs[2 * groups], refs[2 * groups + 1 :])

        return call(body, [(a.shape, F32) for a in x], *x, *u, times[block], name=f"own{block}{tag}")

    def mix_in(block, x, u, got, tag):
        return call(mix_earlier, [(x.shape, F32)], x, u, got, times[block], name=f"earlier{block}{tag}")[0]

    last = groups - 1
    for block in range(2):
        u_near, part = [None] * groups, [None] * groups
        for g in reversed(range(groups)):
            u_near[g], part[g] = near_conv(block, g, far[g], near[g], partner[g])
            if g == last:
                got_near = shift(u_near[g])
        near = list(mix(block, near, u_near, "near"))
        u_far = [None] * groups
        for g in reversed(range(groups)):
            u_far[g] = far_conv(block, g, part[g], beyond[g])
            if g == last:
                got_far = shift(u_far[g])
        far = list(mix(block, far, u_far, "far"))
        if block == 0:
            partner, beyond = [None] * groups, [None] * groups
        for g in reversed(range(groups)):
            if g == 0:
                near[0] = mix_in(block, near[0], u_near[0], got_near, "near")
                far[0] = mix_in(block, far[0], u_far[0], got_far, "far")
            if block == 0:
                partner[g] = fold(near[g][:, -1])
                beyond[g] = cross(far[g])

    piece = (rows // 2 + 1, w // 2, outer)

    def down_body(*refs):
        fars, nears, refs = refs[:groups], refs[groups : 2 * groups], refs[2 * groups :]
        down_rows(groups, fars, nears, refs[0], refs[1 : 1 + n], *refs[1 + n :])

    def staged(body, outs, args, scratch, limit, name):
        return pl.pallas_call(
            body,
            out_shape=outs,
            in_specs=[VM] * len(args),
            out_specs=jax.tree.map(lambda _: VM, outs),
            scratch_shapes=[pltpu.VMEM(*s) for s in scratch],
            name=name,
            compiler_params=pltpu.CompilerParams(vmem_limit_bytes=limit << 20),
            cost_estimate=pl.CostEstimate(flops=1 << 20, bytes_accessed=1 << 20, transcendentals=0),
        )(*args)

    held = list(
        staged(
            down_body,
            [jax.ShapeDtypeStruct(piece, F32)] * n,
            (*far, *near, down),
            [((max(2, n - 2) * w, c), F32), ((n, *piece), F32)],
            28,
            "down",
        )
    )
    group = tiles // n
    held = [
        lax.ppermute(x, "tile", [(i, i ^ (step * group)) for i in range(tiles)]) if step else x
        for step, x in enumerate(held)
    ]
    pieces = {step * group: x for step, x in enumerate(held)}
    for level in range(group.bit_length() - 1):
        by = 1 << level
        pairing = [(i, i ^ by) for i in range(tiles)]
        pieces.update({m + by: lax.ppermute(x, "tile", pairing) for m, x in list(pieces.items())})
    size = (rows // 2) * (w // 2)
    total = tiles * size
    result = staged(
        functools.partial(attend, tiles),
        jax.ShapeDtypeStruct((total // group, outer), F32),
        (*[pieces[m] for m in range(tiles)], attn_gain.reshape(1, outer), wkv, wq, wo),
        [
            ((tiles + 1, size, outer), F32),
            ((total // group, outer), F32),
            ((total, 3 * outer), BF16),
            ((2, total, outer), BF16),
        ],
        28 if total < 2048 else 60,
        "attend",
    )
    return result[None]


def solution(mesh):
    in_specs = (P("frame", "tile", None, None), P(), P(), P(), P(), P(), P(), P(), P(), P())
    out_specs = P(("frame", "tile"), None, None)
    return jax.shard_map(local, mesh=mesh, in_specs=in_specs, out_specs=out_specs, check_vma=False)
```

time: 102 us -> 59.5 us (0.58)
  matrix products: 22.6 us -> 0 us
  blocking collectives: 17.8 us -> 0 us
  Pallas kernels: 0 us -> 14.8 us
  starting transfers between devices: 29.3 us -> 17.5 us
  waiting for transfers between devices: 17.8 us -> 23.5 us
  other arithmetic: 5.25 us -> 0 us
  local copies, waits for them, and re-layouts: 8.5 us -> 3.29 us
    all_to_all x1 -> x0, blocking collectives: 17.8 us -> none  [local(): lax.all_to_all(pieces, 'tile', split_axis=0, concat_axis=0, tiled=True)]
    pallas_call x0 -> x23, Pallas kernels: none -> 14.8 us  [the longest x21 9.74 us: call(): pl.pallas_call(body, out_shape=outs, in_specs=[VM] * len(args), out_specs...]
    conv_general_dilated x3 -> x0, matrix products: 12.3 us -> none  [the longest x2 10.6 us: conv_rows(): lax.conv_general_dilated(inputs, kernel, (1, 1), ((0, 0), (1, 1)), dimens...]
    ppermute x9 -> x18, starting transfers between devices: 29.3 us -> 17.5 us  [the longest x4 7.51 us: cross(): return lax.ppermute(x, 'tile', across)]
    dot_general x14 -> x0, matrix products: 10.2 us -> none  [the longest x2 2.17 us: fold(): jnp.dot(weights, values, precision=highest)]
    ppermute x9 -> x18, waiting for transfers between devices: 17.8 us -> 23.5 us  [the longest x4 9.34 us: shift(): return lax.ppermute(x[-2:], 'frame', onward)]
    unnamed x30 -> x18, local copies, waits for them, and re-layouts: 4.61 us -> 0.9 us
    mul x5 -> x0, other arithmetic: 2.21 us -> none  [the longest x4 2.09 us: act(): return jax.nn.silu(norm(values, gain))]
  transfers between devices with their start and end apart: 9 -> 18, of which waited for: 5 -> 9; matrix products, arithmetic and copies ran while one was open for 4% -> 2% of each run, Pallas kernels for 0% -> 16%
where the time goes in v2:
time: 59.5 us; the launch traced here: 59.4 us
  waiting for transfers between devices  23.5 us (39%)
  starting transfers between devices  17.5 us (29%)
  Pallas kernels  14.8 us (25%)
  local copies, waits for them, and re-layouts  3.29 us (6%)
    pallas_call x21, Pallas kernels, call(): pl.pallas_call(body, out_shape=outs, in_specs=[VM] * len(args), out_specs...  9.74 us
    ppermute x4, waiting for transfers between devices, shift(): return lax.ppermute(x[-2:], 'frame', onward)  9.34 us
    ppermute x3, waiting for transfers between devices, local(): lax.ppermute(x, 'tile', [(i, i ^ step * group) for i in range(tiles)])  7.67 us
    ppermute x4, starting transfers between devices, cross(): return lax.ppermute(x, 'tile', across)  7.51 us
    ppermute x4, waiting for transfers between devices, cross(): return lax.ppermute(x, 'tile', across)  5.59 us
    pallas_call x2, Pallas kernels, staged(): pl.pallas_call(body, out_shape=outs, in_specs=[VM] * len(args), out_specs...  5.06 us
    ppermute x4, starting transfers between devices, shift(): return lax.ppermute(x[-2:], 'frame', onward)  4.77 us
    ppermute x3, starting transfers between devices, local(): lax.ppermute(x, 'tile', [(i, i ^ step * group) for i in range(tiles)])  3.95 us
  transfers between devices with their start and end apart: 18, of which 9 were waited for; matrix products, arithmetic and copies ran while one was open for 2% of the time, Pallas kernels for 16%

profile of v2, /device:TPU:0, one launch (start us, length us, event | category | flops | bytes accessed | tf_op | source)
XLA Modules:
  0.0 59.4 jit_solution(5188768119873383485)
XLA Ops:
  0.0 1.1 %dynamic-slice_bitcast_fusion = f32[4,160,128]{2,1,0:T(8,128)S(1)} fusion(f32[4,2,160,128]{3,2,1,0:T(8,128)} %param.10, s32[]{:T(128)S(6)} %select_n.11), kind=kLoop, calls=%fused_computation.2 | loop fusion | bytes 655364 | tf_op jit(solution)/shard_map/jit(dynamic_index_in_dim)/squeeze | solution.py:275
  1.1 0.6 collective-permute-start
  1.7 1.2 %constant_dynamic-slice_fusion = (f32[2,1,160,128]{3,2,1,0:T(8,128)S(1)}, f32[2,1,160,128]{3,2,1,0:T(8,128)S(1)}, f32[2,160,128]{2,1,0:T(8,128)S(1)}, f32[2,160,128]{2,1,0:T(8,128)S(1)}) fusion(f32[4,2,160,128]{3,2,1,0:T(8,128)} %param.10, s32[]{:T(128)S(6)} %add.3, s32[]{:T(128)S(6)} %select_n.11, s32[]{:T(128)S(6)} %select_n.10), kind=kLoop, calls=%fused_computation.5 | loop fusion | bytes 1310732 | tf_op jit(solution)/shard_map/slice | solution.py:289
  2.9 3.6 %collective-permute-start.1 = (f32[2,160,128]{2,1,0:T(8,128)S(1)}, f32[2,160,128]{2,1,0:T(8,128)S(1)}, u32[]{:S(2)}, u32[]{:S(2)}) collective-permute-start(f32[2,160,128]{2,1,0:T(8,128)S(1)} %get-tuple-element.59.far_ref.refs_0_), channel_id=1, source_target_pairs={{0,28},{4,8},{8,4},{12,16},{16,12},{20,24},{24,20},{28,0},{1,29},{... | collective-permute-start | bytes 491528 | tf_op jit(solution)/shard_map/ppermute | solution.py:281
  6.5 0.1 collective-permute-start.2
  6.5 0.1 slice_bitcast_fusion
  6.6 0.0 copy-start.1
  6.6 0.0 copy-start.6
  6.7 0.1 pack_space0.1.weight_ref
  6.8 0.8 %copy-done.1 = f32[2,3,128,128]{3,2,1,0:T(8,128)S(1)} copy-done((f32[2,3,128,128]{3,2,1,0:T(8,128)S(1)}, f32[2,3,128,128]{3,2,1,0:T(8,128)}, u32[]{:S(2)}) %copy-start.1) | copy-done | bytes 393240
  7.6 0.1 pack_time.1
  7.7 0.0 collective-permute-done
  7.8 1.1 %near01.1 = (f32[2,1,160,128]{3,2,1,0:T(8,128)S(1)}, f32[2,160,128]{2,1,0:T(8,128)S(1)}) custom-call(f32[2,160,128]{2,1,0:T(8,128)S(1)} %get-tuple-element.60.far_ref.refs_1_, f32[2,1,160,128]{3,2,1,0:T(8,128)S(1)} %get-tuple-element.57.near_ref.refs_1_, f32[2,160,128]{2,1,0:T(8,128)S(1)} %get-tuple-element.61.partner_ref, f32[2,2,128]{2,1,0:T(2,128)S(1)} %copy-done.6, ...), custom_call_target="tpu_custom_call" | custom-call | bytes 1705984 | tf_op jit(solution)/shard_map/near01/pallas_call | solution.py:17
  8.8 5.1 %collective-permute-done.2.beyond_ref = f32[2,160,128]{2,1,0:T(8,128)S(1)} collective-permute-done((f32[2,160,128]{2,1,0:T(8,128)S(1)}, f32[2,160,128]{2,1,0:T(8,128)S(1)}, u32[]{:S(2)}, u32[]{:S(2)}) %collective-permute-start.2) | collective-permute-done | bytes 163872 | tf_op jit(solution)/shard_map/ppermute | solution.py:281
  13.9 0.6 far01.1.refs_3_
  14.5 1.9 %collective-permute-start.3 = (f32[2,160,128]{2,1,0:T(8,128)S(1)}, f32[2,160,128]{2,1,0:T(8,128)S(1)}, u32[]{:S(2)}, u32[]{:S(2)}) collective-permute-start(f32[2,160,128]{2,1,0:T(8,128)S(1)} %far01.1.refs_3_), channel_id=1, source_target_pairs={{0,1},{1,2},{2,3},{3,0},{4,5},{5,6},{6,7},{7,4},{8,9},{9,10},{10,1... | collective-permute-start | bytes 491528 | tf_op jit(solution)/shard_map/ppermute | solution.py:284
  16.4 1.6 %collective-permute-start.4 = (f32[2,1,160,128]{3,2,1,0:T(8,128)S(1)}, f32[2,1,160,128]{3,2,1,0:T(8,128)S(1)}, u32[]{:S(2)}, u32[]{:S(2)}) collective-permute-start(f32[2,1,160,128]{3,2,1,0:T(8,128)S(1)} %get-tuple-element.36.refs_3_), channel_id=1, source_target_pairs={{0,1},{1,2},{2,3},{3,0},{4,5},{5,6},{6,7},{7,4},{8,9},{9,10},{10,1... | collective-permute-start | bytes 491528 | tf_op jit(solution)/shard_map/ppermute | solution.py:284
  17.9 1.0 %near00.1 = (f32[2,1,160,128]{3,2,1,0:T(8,128)S(1)}, f32[2,160,128]{2,1,0:T(8,128)S(1)}) custom-call(f32[2,160,128]{2,1,0:T(8,128)S(1)} %get-tuple-element.59.far_ref.refs_0_, f32[2,1,160,128]{3,2,1,0:T(8,128)S(1)} %get-tuple-element.58.near_ref.refs_0_, f32[2,160,128]{2,1,0:T(8,128)S(1)} %get-tuple-element.62.partner_ref, f32[2,2,128]{2,1,0:T(2,128)S(1)} %copy-done.6, ...), custom_call_target="tpu_custom_call" | custom-call | bytes 1705984 | tf_op jit(solution)/shard_map/near00/pallas_call | solution.py:17
  19.0 0.0 collective-permute-done.1.beyond_ref
  19.0 0.6 far00.1.refs_2_.u_ref
  19.6 0.4 own0far.1
  20.0 0.4 own0near.1
  20.4 0.1 collective-permute-start.7
  20.5 1.8 %collective-permute-start.8 = (f32[2,160,128]{2,1,0:T(8,128)S(1)}, f32[2,160,128]{2,1,0:T(8,128)S(1)}, u32[]{:S(2)}, u32[]{:S(2)}) collective-permute-start(f32[2,160,128]{2,1,0:T(8,128)S(1)} %get-tuple-element.34.far_ref.refs_1_), channel_id=1, source_target_pairs={{0,28},{4,8},{8,4},{12,16},{16,12},{20,24},{24,20},{28,0},{1,29},{... | collective-permute-start | bytes 491528 | tf_op jit(solution)/shard_map/ppermute | solution.py:281
  22.2 4.1 %collective-permute-done.4.got_ref = f32[2,1,160,128]{3,2,1,0:T(8,128)S(1)} collective-permute-done((f32[2,1,160,128]{3,2,1,0:T(8,128)S(1)}, f32[2,1,160,128]{3,2,1,0:T(8,128)S(1)}, u32[]{:S(2)}, u32[]{:S(2)}) %collective-permute-start.4) | collective-permute-done | bytes 163872 | tf_op jit(solution)/shard_map/ppermute | solution.py:284
  26.4 0.2 earlier0near.1.near_ref.refs_0_
  26.6 0.1 collective-permute-start.5
  26.7 0.2 earlier0far.1.far_ref.refs_0_
  26.9 2.1 %collective-permute-start.6 = (f32[2,160,128]{2,1,0:T(8,128)S(1)}, f32[2,160,128]{2,1,0:T(8,128)S(1)}, u32[]{:S(2)}, u32[]{:S(2)}) collective-permute-start(f32[2,160,128]{2,1,0:T(8,128)S(1)} %earlier0far.1.far_ref.refs_0_), channel_id=1, source_target_pairs={{0,28},{4,8},{8,4},{12,16},{16,12},{20,24},{24,20},{28,0},{1,29},{... | collective-permute-start | bytes 491528 | tf_op jit(solution)/shard_map/ppermute | solution.py:281
  29.0 0.1 pack_space1.1.weight_ref
  29.1 0.0 copy-start
  29.1 1.0 %near11.1 = (f32[2,1,160,128]{3,2,1,0:T(8,128)S(1)}, f32[2,160,128]{2,1,0:T(8,128)S(1)}) custom-call(f32[2,160,128]{2,1,0:T(8,128)S(1)} %get-tuple-element.34.far_ref.refs_1_, f32[2,1,160,128]{3,2,1,0:T(8,128)S(1)} %get-tuple-element.39.near_ref.refs_1_, f32[2,160,128]{2,1,0:T(8,128)S(1)} %collective-permute-done.7.partner_ref, f32[2,2,128]{2,1,0:T(2,128)S(1)} %copy-done.6, ...), custom_call_target="tpu_custom_call" | custom-call | bytes 1705984 | tf_op jit(solution)/shard_map/near11/pallas_call | solution.py:17
  30.2 0.0 collective-permute-done.8.beyond_ref
  30.2 0.6 far11.1.refs_3_
  30.8 0.1 collective-permute-start.9
  30.9 1.3 %collective-permute-start.10 = (f32[2,1,160,128]{3,2,1,0:T(8,128)S(1)}, f32[2,1,160,128]{3,2,1,0:T(8,128)S(1)}, u32[]{:S(2)}, u32[]{:S(2)}) collective-permute-start(f32[2,1,160,128]{3,2,1,0:T(8,128)S(1)} %get-tuple-element.45.refs_3_), channel_id=1, source_target_pairs={{0,1},{1,2},{2,3},{3,0},{4,5},{5,6},{6,7},{7,4},{8,9},{9,10},{10,1... | collective-permute-start | bytes 491528 | tf_op jit(solution)/shard_map/ppermute | solution.py:284
  32.1 0.2 pack_down.1.refs_4_
  32.4 0.0 collective-permute-done.5.partner_ref
  32.4 1.0 %near10.1 = (f32[2,1,160,128]{3,2,1,0:T(8,128)S(1)}, f32[2,160,128]{2,1,0:T(8,128)S(1)}) custom-call(f32[2,160,128]{2,1,0:T(8,128)S(1)} %earlier0far.1.far_ref.refs_0_, f32[2,1,160,128]{3,2,1,0:T(8,128)S(1)} %earlier0near.1.near_ref.refs_0_, f32[2,160,128]{2,1,0:T(8,128)S(1)} %collective-permute-done.5.partner_ref, f32[2,2,128]{2,1,0:T(2,128)S(1)} %copy-done.6, ...), custom_call_target="tpu_custom_call" | custom-call | bytes 1705984 | tf_op jit(solution)/shard_map/near10/pallas_call | solution.py:17
  33.4 0.5 collective-permute-done.6.beyond_ref
  33.9 0.6 far10.1.refs_2_.u_ref
  34.5 0.4 own1far.1
  34.9 0.4 own1near.1
  35.3 3.7 %collective-permute-done.9.got_ref = f32[2,160,128]{2,1,0:T(8,128)S(1)} collective-permute-done((f32[2,160,128]{2,1,0:T(8,128)S(1)}, f32[2,160,128]{2,1,0:T(8,128)S(1)}, u32[]{:S(2)}, u32[]{:S(2)}) %collective-permute-start.9) | collective-permute-done | bytes 163872 | tf_op jit(solution)/shard_map/ppermute | solution.py:284
  39.0 0.2 earlier1far.1.refs_0_
  39.2 1.5 %collective-permute-done.10.got_ref = f32[2,1,160,128]{3,2,1,0:T(8,128)S(1)} collective-permute-done((f32[2,1,160,128]{3,2,1,0:T(8,128)S(1)}, f32[2,1,160,128]{3,2,1,0:T(8,128)S(1)}, u32[]{:S(2)}, u32[]{:S(2)}) %collective-permute-start.10) | collective-permute-done | bytes 163872 | tf_op jit(solution)/shard_map/ppermute | solution.py:284
  40.8 0.2 earlier1near.1.refs_2_
  41.0 0.0 copy-start.2
  41.0 0.0 copy-start.3
  41.0 0.0 copy-start.4
  41.0 0.0 copy-start.5
  41.0 0.0 copy-start.7
  41.1 0.9 %down.1 = (f32[2,80,256]{2,1,0:T(8,128)S(1)}, f32[2,80,256]{2,1,0:T(8,128)S(1)}, f32[2,80,256]{2,1,0:T(8,128)S(1)}, f32[2,80,256]{2,1,0:T(8,128)S(1)}) custom-call(f32[2,160,128]{2,1,0:T(8,128)S(1)} %earlier1far.1.refs_0_, f32[2,160,128]{2,1,0:T(8,128)S(1)} %get-tuple-element.43.refs_1_, f32[2,1,160,128]{3,2,1,0:T(8,128)S(1)} %earlier1near.1.refs_2_, ...), custom_call_target="tpu_custom_call" | custom-call | flops 1048576 | bytes 1048576 | tf_op jit(solution)/shard_map/down/pallas_call | solution.py:374
  42.0 2.4 %collective-permute-start.12 = (f32[2,80,256]{2,1,0:T(8,128)S(1)}, f32[2,80,256]{2,1,0:T(8,128)S(1)}, u32[]{:S(2)}, u32[]{:S(2)}) collective-permute-start(f32[2,80,256]{2,1,0:T(8,128)S(1)} %get-tuple-element.49), channel_id=1, source_target_pairs={{0,8},{4,12},{8,0},{12,4},{16,24},{20,28},{24,16},{28,20},{1,9},{5... | collective-permute-start | bytes 491528 | tf_op jit(solution)/shard_map/ppermute | solution.py:397
  44.4 0.7 %collective-permute-start.14 = (f32[2,80,256]{2,1,0:T(8,128)S(1)}, f32[2,80,256]{2,1,0:T(8,128)S(1)}, u32[]{:S(2)}, u32[]{:S(2)}) collective-permute-start(f32[2,80,256]{2,1,0:T(8,128)S(1)} %get-tuple-element.50), channel_id=1, source_target_pairs={{0,16},{4,20},{8,24},{12,28},{16,0},{20,4},{24,8},{28,12},{1,17},{... | collective-permute-start | bytes 491528 | tf_op jit(solution)/shard_map/ppermute | solution.py:397
  45.1 0.8 %collective-permute-start.16 = (f32[2,80,256]{2,1,0:T(8,128)S(1)}, f32[2,80,256]{2,1,0:T(8,128)S(1)}, u32[]{:S(2)}, u32[]{:S(2)}) collective-permute-start(f32[2,80,256]{2,1,0:T(8,128)S(1)} %get-tuple-element.51), channel_id=1, source_target_pairs={{0,24},{4,28},{8,16},{12,20},{16,8},{20,12},{24,0},{28,4},{1,25},{... | collective-permute-start | bytes 491528 | tf_op jit(solution)/shard_map/ppermute | solution.py:397
  45.9 0.0 collective-permute-start.11
  45.9 3.5 %collective-permute-done.12.refs_2_ = f32[2,80,256]{2,1,0:T(8,128)S(1)} collective-permute-done((f32[2,80,256]{2,1,0:T(8,128)S(1)}, f32[2,80,256]{2,1,0:T(8,128)S(1)}, u32[]{:S(2)}, u32[]{:S(2)}) %collective-permute-start.12) | collective-permute-done | bytes 163872 | tf_op jit(solution)/shard_map/ppermute | solution.py:397
  49.4 4.2 %collective-permute-done.14.refs_4_ = f32[2,80,256]{2,1,0:T(8,128)S(1)} collective-permute-done((f32[2,80,256]{2,1,0:T(8,128)S(1)}, f32[2,80,256]{2,1,0:T(8,128)S(1)}, u32[]{:S(2)}, u32[]{:S(2)}) %collective-permute-start.14) | collective-permute-done | bytes 163872 | tf_op jit(solution)/shard_map/ppermute | solution.py:397
  53.6 0.5 collective-permute-start.17
  54.1 0.2 pack_attn.1
  54.3 0.6 %collective-permute-done.15.refs_5_ = f32[2,80,256]{2,1,0:T(8,128)S(1)} collective-permute-done((f32[2,80,256]{2,1,0:T(8,128)S(1)}, f32[2,80,256]{2,1,0:T(8,128)S(1)}, u32[]{:S(2)}, u32[]{:S(2)}) %collective-permute-start.15) | collective-permute-done | bytes 163872 | tf_op jit(solution)/shard_map/ppermute | solution.py:404
  55.0 0.2 collective-permute-done.17.refs_7_
  55.2 4.2 %attend.1 = f32[320,256]{1,0:T(8,128)} custom-call(f32[2,80,256]{2,1,0:T(8,128)S(1)} %get-tuple-element.48.refs_0_, f32[2,80,256]{2,1,0:T(8,128)S(1)} %collective-permute-done.11.refs_1_, f32[2,80,256]{2,1,0:T(8,128)S(1)} %collective-permute-done.12.refs_2_, f32[2,80,256]{2,1,0:T(8,128)S(1)} %collective-permute-done.13.refs_3_, ...), custom_call_target="tpu_custom_call" | custom-call | flops 1048576 | bytes 1048576 | tf_op jit(solution)/shard_map/attend/pallas_call | solution.py:374
  (17 shorter events, 0.1 us)
Async XLA Ops:
  0.0 6.5 %copy-start.8 = (f32[2,3,3,128,128]{4,3,2,1,0:T(8,128)S(1)}, f32[2,3,3,128,128]{4,3,2,1,0:T(8,128)}, u32[]{:S(2)}) copy-start(f32[2,3,3,128,128]{4,3,2,1,0:T(8,128)} %param.12) | copy-start | bytes 3538948
  1.1 6.6 %collective-permute-start = (f32[4,160,128]{2,1,0:T(8,128)S(1)}, f32[4,160,128]{2,1,0:T(8,128)S(1)}, u32[]{:S(2)}, u32[]{:S(2)}) collective-permute-start(f32[4,160,128]{2,1,0:T(8,128)S(1)} %dynamic-slice_bitcast_fusion), channel_id=1, source_target_pairs={{0,4},{4,0},{8,12},{12,8},{16,20},{20,16},{24,28},{28,24},{1,5},{5... | collective-permute-start | bytes 983048 | tf_op jit(solution)/shard_map/ppermute | solution.py:278
  2.9 16.1 %collective-permute-start.1 = (f32[2,160,128]{2,1,0:T(8,128)S(1)}, f32[2,160,128]{2,1,0:T(8,128)S(1)}, u32[]{:S(2)}, u32[]{:S(2)}) collective-permute-start(f32[2,160,128]{2,1,0:T(8,128)S(1)} %get-tuple-element.59.far_ref.refs_0_), channel_id=1, source_target_pairs={{0,28},{4,8},{8,4},{12,16},{16,12},{20,24},{24,20},{28,0},{1,29},{... | collective-permute-start | bytes 491528 | tf_op jit(solution)/shard_map/ppermute | solution.py:281
  6.5 7.4 %collective-permute-start.2 = (f32[2,160,128]{2,1,0:T(8,128)S(1)}, f32[2,160,128]{2,1,0:T(8,128)S(1)}, u32[]{:S(2)}, u32[]{:S(2)}) collective-permute-start(f32[2,160,128]{2,1,0:T(8,128)S(1)} %get-tuple-element.60.far_ref.refs_1_), channel_id=1, source_target_pairs={{0,28},{4,8},{8,4},{12,16},{16,12},{20,24},{24,20},{28,0},{1,29},{... | collective-permute-start | bytes 491528 | tf_op jit(solution)/shard_map/ppermute | solution.py:281
  6.6 1.0 %copy-start.1 = (f32[2,3,128,128]{3,2,1,0:T(8,128)S(1)}, f32[2,3,128,128]{3,2,1,0:T(8,128)}, u32[]{:S(2)}) copy-start(f32[2,3,128,128]{3,2,1,0:T(8,128)} %time_ref.1) | copy-start | bytes 1179652
  6.6 1.1 %copy-start.6 = (f32[2,2,128]{2,1,0:T(2,128)S(1)}, f32[2,2,128]{2,1,0:T(2,128)}, u32[]{:S(2)}) copy-start(f32[2,2,128]{2,1,0:T(2,128)} %gain_ref.15) | copy-start | bytes 6148
  14.5 12.2 %collective-permute-start.3 = (f32[2,160,128]{2,1,0:T(8,128)S(1)}, f32[2,160,128]{2,1,0:T(8,128)S(1)}, u32[]{:S(2)}, u32[]{:S(2)}) collective-permute-start(f32[2,160,128]{2,1,0:T(8,128)S(1)} %far01.1.refs_3_), channel_id=1, source_target_pairs={{0,1},{1,2},{2,3},{3,0},{4,5},{5,6},{6,7},{7,4},{8,9},{9,10},{10,1... | collective-permute-start | bytes 491528 | tf_op jit(solution)/shard_map/ppermute | solution.py:284
  16.4 10.0 %collective-permute-start.4 = (f32[2,1,160,128]{3,2,1,0:T(8,128)S(1)}, f32[2,1,160,128]{3,2,1,0:T(8,128)S(1)}, u32[]{:S(2)}, u32[]{:S(2)}) collective-permute-start(f32[2,1,160,128]{3,2,1,0:T(8,128)S(1)} %get-tuple-element.36.refs_3_), channel_id=1, source_target_pairs={{0,1},{1,2},{2,3},{3,0},{4,5},{5,6},{6,7},{7,4},{8,9},{9,10},{10,1... | collective-permute-start | bytes 491528 | tf_op jit(solution)/shard_map/ppermute | solution.py:284
  20.4 8.7 %collective-permute-start.7 = (f32[2,160,128]{2,1,0:T(8,128)S(1)}, f32[2,160,128]{2,1,0:T(8,128)S(1)}, u32[]{:S(2)}, u32[]{:S(2)}) collective-permute-start(f32[2,160,128]{2,1,0:T(8,128)S(1)} %bitcast.20), channel_id=1, source_target_pairs={{0,4},{4,0},{8,12},{12,8},{16,20},{20,16},{24,28},{28,24},{1,5},{5... | collective-permute-start | bytes 491528 | tf_op jit(solution)/shard_map/ppermute | solution.py:278
  20.5 9.7 %collective-permute-start.8 = (f32[2,160,128]{2,1,0:T(8,128)S(1)}, f32[2,160,128]{2,1,0:T(8,128)S(1)}, u32[]{:S(2)}, u32[]{:S(2)}) collective-permute-start(f32[2,160,128]{2,1,0:T(8,128)S(1)} %get-tuple-element.34.far_ref.refs_1_), channel_id=1, source_target_pairs={{0,28},{4,8},{8,4},{12,16},{16,12},{20,24},{24,20},{28,0},{1,29},{... | collective-permute-start | bytes 491528 | tf_op jit(solution)/shard_map/ppermute | solution.py:281
  26.6 5.8 %collective-permute-start.5 = (f32[2,160,128]{2,1,0:T(8,128)S(1)}, f32[2,160,128]{2,1,0:T(8,128)S(1)}, u32[]{:S(2)}, u32[]{:S(2)}) collective-permute-start(f32[2,160,128]{2,1,0:T(8,128)S(1)} %bitcast.19), channel_id=1, source_target_pairs={{0,4},{4,0},{8,12},{12,8},{16,20},{20,16},{24,28},{28,24},{1,5},{5... | collective-permute-start | bytes 491528 | tf_op jit(solution)/shard_map/ppermute | solution.py:278
  26.9 7.0 %collective-permute-start.6 = (f32[2,160,128]{2,1,0:T(8,128)S(1)}, f32[2,160,128]{2,1,0:T(8,128)S(1)}, u32[]{:S(2)}, u32[]{:S(2)}) collective-permute-start(f32[2,160,128]{2,1,0:T(8,128)S(1)} %earlier0far.1.far_ref.refs_0_), channel_id=1, source_target_pairs={{0,28},{4,8},{8,4},{12,16},{16,12},{20,24},{24,20},{28,0},{1,29},{... | collective-permute-start | bytes 491528 | tf_op jit(solution)/shard_map/ppermute | solution.py:281
  29.1 3.0 %copy-start = (f32[3,3,128,256]{3,2,1,0:T(8,128)S(1)}, f32[3,3,128,256]{3,2,1,0:T(8,128)}, u32[]{:S(2)}) copy-start(f32[3,3,128,256]{3,2,1,0:T(8,128)} %down_ref.1) | copy-start | bytes 3538948
  30.8 8.2 %collective-permute-start.9 = (f32[2,160,128]{2,1,0:T(8,128)S(1)}, f32[2,160,128]{2,1,0:T(8,128)S(1)}, u32[]{:S(2)}, u32[]{:S(2)}) collective-permute-start(f32[2,160,128]{2,1,0:T(8,128)S(1)} %far11.1.refs_3_), channel_id=1, source_target_pairs={{0,1},{1,2},{2,3},{3,0},{4,5},{5,6},{6,7},{7,4},{8,9},{9,10},{10,1... | collective-permute-start | bytes 491528 | tf_op jit(solution)/shard_map/ppermute | solution.py:284
  30.9 9.9 %collective-permute-start.10 = (f32[2,1,160,128]{3,2,1,0:T(8,128)S(1)}, f32[2,1,160,128]{3,2,1,0:T(8,128)S(1)}, u32[]{:S(2)}, u32[]{:S(2)}) collective-permute-start(f32[2,1,160,128]{3,2,1,0:T(8,128)S(1)} %get-tuple-element.45.refs_3_), channel_id=1, source_target_pairs={{0,1},{1,2},{2,3},{3,0},{4,5},{5,6},{6,7},{7,4},{8,9},{9,10},{10,1... | collective-permute-start | bytes 491528 | tf_op jit(solution)/shard_map/ppermute | solution.py:284
  41.0 13.1 %copy-start.2 = (f32[256,256]{1,0:T(8,128)S(1)}, f32[256,256]{1,0:T(8,128)}, u32[]{:S(2)}) copy-start(f32[256,256]{1,0:T(8,128)} %q_ref.1) | copy-start | bytes 786436
  41.0 13.1 %copy-start.3 = (f32[256,256]{1,0:T(8,128)S(1)}, f32[256,256]{1,0:T(8,128)}, u32[]{:S(2)}) copy-start(f32[256,256]{1,0:T(8,128)} %k_ref.1) | copy-start | bytes 786436
  41.0 13.1 %copy-start.4 = (f32[256,256]{1,0:T(8,128)S(1)}, f32[256,256]{1,0:T(8,128)}, u32[]{:S(2)}) copy-start(f32[256,256]{1,0:T(8,128)} %v_ref.1) | copy-start | bytes 786436
  41.0 13.1 %copy-start.5 = (f32[256,256]{1,0:T(8,128)S(1)}, f32[256,256]{1,0:T(8,128)}, u32[]{:S(2)}) copy-start(f32[256,256]{1,0:T(8,128)} %o_ref.1) | copy-start | bytes 786436
  41.0 14.2 %copy-start.7 = (f32[256]{0:T(256)S(1)}, f32[256]{0:T(256)}, u32[]{:S(2)}) copy-start(f32[256]{0:T(256)} %param.15) | copy-start | bytes 3076
  42.0 7.5 %collective-permute-start.12 = (f32[2,80,256]{2,1,0:T(8,128)S(1)}, f32[2,80,256]{2,1,0:T(8,128)S(1)}, u32[]{:S(2)}, u32[]{:S(2)}) collective-permute-start(f32[2,80,256]{2,1,0:T(8,128)S(1)} %get-tuple-element.49), channel_id=1, source_target_pairs={{0,8},{4,12},{8,0},{12,4},{16,24},{20,28},{24,16},{28,20},{1,9},{5... | collective-permute-start | bytes 491528 | tf_op jit(solution)/shard_map/ppermute | solution.py:397
  44.4 9.2 %collective-permute-start.14 = (f32[2,80,256]{2,1,0:T(8,128)S(1)}, f32[2,80,256]{2,1,0:T(8,128)S(1)}, u32[]{:S(2)}, u32[]{:S(2)}) collective-permute-start(f32[2,80,256]{2,1,0:T(8,128)S(1)} %get-tuple-element.50), channel_id=1, source_target_pairs={{0,16},{4,20},{8,24},{12,28},{16,0},{20,4},{24,8},{28,12},{1,17},{... | collective-permute-start | bytes 491528 | tf_op jit(solution)/shard_map/ppermute | solution.py:397
  45.1 8.5 %collective-permute-start.16 = (f32[2,80,256]{2,1,0:T(8,128)S(1)}, f32[2,80,256]{2,1,0:T(8,128)S(1)}, u32[]{:S(2)}, u32[]{:S(2)}) collective-permute-start(f32[2,80,256]{2,1,0:T(8,128)S(1)} %get-tuple-element.51), channel_id=1, source_target_pairs={{0,24},{4,28},{8,16},{12,20},{16,8},{20,12},{24,0},{28,4},{1,25},{... | collective-permute-start | bytes 491528 | tf_op jit(solution)/shard_map/ppermute | solution.py:397
  45.9 8.4 %collective-permute-start.11 = (f32[2,80,256]{2,1,0:T(8,128)S(1)}, f32[2,80,256]{2,1,0:T(8,128)S(1)}, u32[]{:S(2)}, u32[]{:S(2)}) collective-permute-start(f32[2,80,256]{2,1,0:T(8,128)S(1)} %get-tuple-element.48.refs_0_), channel_id=1, source_target_pairs={{0,4},{4,0},{8,12},{12,8},{16,20},{20,16},{24,28},{28,24},{1,5},{5... | collective-permute-start | bytes 491528 | tf_op jit(solution)/shard_map/ppermute | solution.py:404
  49.4 4.9 %collective-permute-start.13 = (f32[2,80,256]{2,1,0:T(8,128)S(1)}, f32[2,80,256]{2,1,0:T(8,128)S(1)}, u32[]{:S(2)}, u32[]{:S(2)}) collective-permute-start(f32[2,80,256]{2,1,0:T(8,128)S(1)} %collective-permute-done.12.refs_2_), channel_id=1, source_target_pairs={{0,4},{4,0},{8,12},{12,8},{16,20},{20,16},{24,28},{28,24},{1,5},{5... | collective-permute-start | bytes 491528 | tf_op jit(solution)/shard_map/ppermute | solution.py:404
  53.6 1.4 %collective-permute-start.15 = (f32[2,80,256]{2,1,0:T(8,128)S(1)}, f32[2,80,256]{2,1,0:T(8,128)S(1)}, u32[]{:S(2)}, u32[]{:S(2)}) collective-permute-start(f32[2,80,256]{2,1,0:T(8,128)S(1)} %collective-permute-done.14.refs_4_), channel_id=1, source_target_pairs={{0,4},{4,0},{8,12},{12,8},{16,20},{20,16},{24,28},{28,24},{1,5},{5... | collective-permute-start | bytes 491528 | tf_op jit(solution)/shard_map/ppermute | solution.py:404
  53.6 1.6 %collective-permute-start.17 = (f32[2,80,256]{2,1,0:T(8,128)S(1)}, f32[2,80,256]{2,1,0:T(8,128)S(1)}, u32[]{:S(2)}, u32[]{:S(2)}) collective-permute-start(f32[2,80,256]{2,1,0:T(8,128)S(1)} %collective-permute-done.16.refs_6_), channel_id=1, source_target_pairs={{0,4},{4,0},{8,12},{12,8},{16,20},{20,16},{24,28},{28,24},{1,5},{5... | collective-permute-start | bytes 491528 | tf_op jit(solution)/shard_map/ppermute | solution.py:404

commit v3 on v2

v3 whole, which is shorter than its diff:
```python
import functools

import jax
import jax.numpy as jnp
from jax import lax
from jax.experimental import pallas as pl
from jax.experimental.pallas import tpu as pltpu
from jax.sharding import PartitionSpec as P


F32, BF16 = jnp.float32, jnp.bfloat16

VM = pl.BlockSpec(memory_space=pltpu.VMEM)


def call(body, outs, *args, flops=0):
    return called(body, outs, *args, flops=flops)


def called(body, outs, *args, flops):
    outs = [jax.ShapeDtypeStruct(shape, kind) for shape, kind in outs]
    moved = sum(a.size * a.dtype.itemsize for a in args) + sum(o.size * o.dtype.itemsize for o in outs)
    return pl.pallas_call(
        body,
        out_shape=outs,
        in_specs=[VM] * len(args),
        out_specs=[VM] * len(outs),
        compiler_params=pltpu.CompilerParams(vmem_limit_bytes=28 << 20),
        cost_estimate=pl.CostEstimate(flops=flops, bytes_accessed=moved, transcendentals=0),
    )(*args)


def halves(values):
    high = values.astype(BF16)
    return high, (values - high.astype(F32)).astype(BF16)


def left_side(values):
    high, low = halves(values)
    return jnp.concatenate([high, low, high], -1)


def right_side(values):
    high, low = halves(values)
    return jnp.concatenate([high, high, low], 0)


def mul(left, right):
    return jnp.dot(left, right, preferred_element_type=F32)


def norm(values, gain):
    return values * lax.rsqrt(jnp.mean(values * values, -1, keepdims=True) + 1e-06) * gain


def act(values, gain):
    y = norm(values, gain)
    return y / (1.0 + jnp.exp(-y))


def taps(values):
    n, w, c = values.shape
    at = lax.broadcasted_iota(jnp.int32, values.shape, 1)
    before = jnp.where(at == 0, 0.0, pltpu.roll(values, 1, 1))
    after = jnp.where(at == w - 1, 0.0, pltpu.roll(values, w - 1, 1))
    return halves(jnp.concatenate([before, values, after], -1).reshape(n * w, 3 * c))


def is_even():
    return lax.rem(lax.axis_index("tile"), 2) == 0


def pack_space(space_ref, pair_ref, above_ref, below_ref):
    c = space_ref.shape[-1]
    even = is_even()
    for kh in range(3):
        at = jnp.where(even, kh, 2 - kh)
        high, low = halves(jnp.concatenate([space_ref[at, kw] for kw in range(3)], 0))
        three = jnp.concatenate([high, high, low], 0)
        for row in range(2):
            to = row + 1 - kh
            if 0 <= to < 2:
                pair_ref[row * 9 * c : (row + 1) * 9 * c, to * c : (to + 1) * c] = three
        if kh != 1:
            edge_ref = above_ref if kh == 0 else below_ref
            edge_ref[: 3 * c, :c] = high
            edge_ref[: 3 * c, c:] = low
            edge_ref[3 * c :, :c] = high
            edge_ref[3 * c :, c:] = jnp.zeros_like(low)


def pack_time(time_ref, *out_refs):
    c = time_ref.shape[-1]
    for block, out_ref in enumerate(out_refs):
        for k in range(3):
            out_ref[:, (2 - k) * c : (3 - k) * c] = right_side(time_ref[block, k])


def pack_down(down_ref, own_ref, next_ref):
    def rows(kh):
        return right_side(jnp.concatenate([down_ref[kh, kw] for kw in range(3)], 0))

    size = next_ref.shape[0]
    next_ref[...] = rows(0)
    own_ref[:size] = rows(1)
    own_ref[size:] = rows(2)


def pack_attn(q_ref, k_ref, v_ref, o_ref, qk_out, vo_out):
    d = q_ref.shape[0]
    both = lax.dot_general(
        left_side(q_ref[...] * float(d) ** (-0.5)),
        jnp.concatenate([*halves(k_ref[...])[:1] * 2, halves(k_ref[...])[1]], 1),
        (((1,), (1,)), ((), ())),
        preferred_element_type=F32,
    )
    qk_out[...] = right_side(both)
    vo_out[...] = right_side(mul(left_side(v_ref[...]), right_side(o_ref[...])))


def edge(values, weight_ref):
    n, w, c = values.shape
    both = mul(jnp.concatenate(taps(values), -1), weight_ref[...])
    return (both[:, :c] + both[:, c:]).reshape(n, w, c)


def conv_near(block, far_ref, near_ref, partner_ref, gain_ref, pair_ref, above_ref, below_ref, u_ref, part_ref):
    n, rest, w, c = near_ref.shape
    rows = rest + 1
    gain = gain_ref[block, 0]
    source = [act(near_ref[:, row - 1] if row else far_ref[...], gain) for row in range(rows)]
    total = []
    for row in range(0, rows, 2):
        left = []
        for values in source[row : row + 2]:
            high, low = taps(values)
            left += [high, low, high]
        both = mul(jnp.concatenate(left, -1), pair_ref[...])
        total += [both[:, :c].reshape(n, w, c), both[:, c:].reshape(n, w, c)]
    total[-1] = total[-1] + edge(act(partner_ref[...], gain), below_ref)
    for row in range(2, rows, 2):
        total[row] = total[row] + edge(source[row - 1], above_ref)
        total[row - 1] = total[row - 1] + edge(source[row], below_ref)
    part_ref[...] = total[0]
    for row in range(1, rows):
        u_ref[:, row - 1] = act(total[row], gain_ref[block, 1])


def conv_far(block, part_ref, beyond_ref, gain_ref, above_ref, u_ref):
    tile = lax.axis_index("tile")
    inside = jnp.logical_and(tile > 0, tile < lax.axis_size("tile") - 1)
    beyond = jnp.where(inside, beyond_ref[...], 0.0)
    product = edge(act(beyond, gain_ref[block, 0]), above_ref)
    u_ref[...] = act(part_ref[...] + product, gain_ref[block, 1])


def mix_own(groups, x_refs, u_refs, weight_ref, out_refs):
    places = [(g, f) for g in range(groups) for f in range(x_refs[g].shape[0])]
    c = x_refs[0].shape[-1]
    shape = x_refs[0].shape[1:]
    total = [x_refs[g][f].reshape(-1, c) for g, f in places]
    for at, (g, f) in enumerate(places):
        left = left_side(u_refs[g][f].reshape(-1, c))
        wide = min(3, len(places) - at)
        product = mul(left, weight_ref[:, : wide * c])
        for k in range(wide):
            total[at + k] = total[at + k] + product[:, k * c : (k + 1) * c]
    for at, (g, f) in enumerate(places):
        out_refs[g][f] = total[at].reshape(shape)


def mix_earlier(x_ref, u_ref, got_ref, weight_ref, out_ref):
    c = x_ref.shape[-1]
    shape = x_ref.shape[1:]
    opening = lax.axis_index("frame") == 0
    first = u_ref[0].reshape(-1, c)
    before = jnp.where(opening, first, got_ref[0].reshape(-1, c))
    last = jnp.where(opening, first, got_ref[1].reshape(-1, c))
    near = mul(left_side(last), weight_ref[:, c:])
    far = mul(left_side(before), weight_ref[:, 2 * c :])
    out_ref[0] = x_ref[0] + (near[:, :c] + far).reshape(shape)
    out_ref[1] = x_ref[1] + near[:, c:].reshape(shape)


def pixels(ref, n, w):
    c = ref.shape[-1]
    half = w // 2
    even = ref[pl.ds(0, n * half, stride=2), :]
    odd = ref[pl.ds(1, n * half, stride=2), :]
    odd3 = odd.reshape(n, half, c)
    at = lax.broadcasted_iota(jnp.int32, odd3.shape, 1)
    before = jnp.where(at == 0, 0.0, pltpu.roll(odd3, 1, 1)).reshape(n * half, c)
    return left_side(jnp.concatenate([before, even, odd], -1))


def down_rows(far_ref, near_ref, own_ref, next_ref, out_ref, flat_ref):
    n, rest, w, c = near_ref.shape
    rows = rest + 1
    even = is_even()

    def held(row):
        return near_ref[:, row - 1] if row else far_ref[...]

    parts = []
    for row in range(rows):
        flat_ref[: n * w] = jnp.where(even, held(row), held(rows - 1 - row)).reshape(n * w, c)
        parts.append(pixels(flat_ref.at[: n * w], n, w))
    for row in range(rows // 2 + 1):
        total = mul(parts[2 * row - 1], next_ref[...]) if row else 0.0
        if row < rows // 2:
            total = total + mul(jnp.concatenate(parts[2 * row : 2 * row + 2], -1), own_ref[...])
        out_ref[:, row] = total.reshape(n, w // 2, -1)


def spread_out(refs, out_refs):
    frames = len(out_refs)
    mine = lax.axis_index("tile") // (lax.axis_size("tile") // frames)
    start = 0
    for ref in refs:
        for f in range(ref.shape[0]):
            for step in range(frames):

                @pl.when(mine ^ step == start + f)
                def _():
                    out_refs[step][...] = ref[f]

        start += ref.shape[0]


def attend(count, *refs):
    held = refs[:count]
    gain_ref, qk_ref, vo_ref, out_ref, z_ref, query_ref, k_ref, v_ref = refs[count:]
    places = [(ref, i) for ref in held for i in range(ref.shape[0])]
    count = len(places)
    _, rows, w, d = held[0].shape
    rows -= 1
    tile = lax.axis_index("tile")
    for m, (ref, i) in enumerate(places):
        z_ref[tile ^ m] = ref[i, :rows].reshape(rows * w, d)
    for m, (ref, i) in enumerate(places):
        at = (tile ^ m) + 1
        z_ref[at, :w] = z_ref[at, :w] + ref[i, rows]
    gain = gain_ref[0]
    size = rows * w
    step = min(count, 8)
    for at in range(0, count, step):
        high, low = halves(norm(z_ref[at : at + step].reshape(step * size, d), gain))
        tokens = slice(at * size, (at + step) * size)
        k_ref[tokens, :d] = high
        k_ref[tokens, d : 2 * d] = high
        k_ref[tokens, 2 * d :] = low
        v_ref[at * size : (at + step) * size] = high
        v_ref[(count + at) * size : (count + at + step) * size] = high
        v_ref[(2 * count + at) * size : (2 * count + at + step) * size] = low
    part = out_ref.shape[0] // count
    for block in range(size // part):

        @pl.when(lax.rem(tile, size // part) == block)
        def _():
            for b in range(count):
                query_ref[b * part : (b + 1) * part] = z_ref[b, block * part : (block + 1) * part]

    mine = query_ref[...]
    query = mul(left_side(norm(mine, gain)), qk_ref[...])
    scores = lax.dot_general(
        left_side(query), k_ref[...], (((1,), (1,)), ((), ())), preferred_element_type=F32
    )
    weights = jnp.exp(scores - jnp.max(scores, -1, keepdims=True))
    total = jnp.sum(weights, -1, keepdims=True)
    mixed = mul(left_side(weights), v_ref[...])
    out_ref[...] = mine + mul(left_side(mixed / total), vo_ref[...])


def local(
    video,
    norm_gain,
    space_weight,
    time_weight,
    down_weight,
    attn_gain,
    w_query,
    w_key,
    w_value,
    w_out,
):
    n, rows, w, c = video.shape
    tiles, spans = lax.axis_size("tile"), lax.axis_size("frame")
    even = lax.rem(lax.axis_index("tile"), 2) == 0
    outer = down_weight.shape[-1]
    if n == 3:
        raise ValueError("three frames")
    pairs = [(i, i ^ 1) for i in range(tiles)]
    across = [(i, (i + 1 if i % 2 else i - 1) % tiles) for i in range(tiles)]
    onward = [(i, (i + 1) % spans) for i in range(spans)]
    early, late = slice(0, 2), slice(2, n)
    ranges = [early, late] if n > 2 else [early]
    groups = len(ranges)

    def fold(x):
        return lax.ppermute(x, "tile", pairs)

    def cross(x):
        return lax.ppermute(x, "tile", across)

    def shift(x):
        return lax.ppermute(x[-2:], "frame", onward)

    far, near, beyond = [None] * groups, [None] * groups, [None] * groups

    def load(ranges, rows_of):
        def body(video_ref, *refs):
            outs, sem = refs[:-1], refs[-1]
            even = is_even()
            copies = []
            for out, r, j in zip(outs, ranges, rows_of):
                at = jnp.where(even, j, rows - 1 - j)
                copies.append(pltpu.make_async_copy(video_ref.at[r, at], out, sem.at[len(copies)]))
                copies[-1].start()
            for copy in copies:
                copy.wait()

        outs = [jax.ShapeDtypeStruct((r.stop - r.start, w, c), F32) for r in ranges]
        return pl.pallas_call(
            body,
            out_shape=outs,
            in_specs=[pl.BlockSpec(memory_space=pl.ANY)],
            out_specs=[VM] * len(outs),
            scratch_shapes=[pltpu.SemaphoreType.DMA((len(outs),))],
            compiler_params=pltpu.CompilerParams(vmem_limit_bytes=28 << 20),
            cost_estimate=pl.CostEstimate(flops=0, bytes_accessed=1 << 18, transcendentals=0),
        )(video)

    far, beyond = [None] * groups, [None] * groups
    far[-1:] = load(ranges[-1:], [0])
    rest = load(ranges[:-1] + [slice(0, n)] * (rows - 1), [0] * (groups - 1) + list(range(1, rows)))
    far[:-1] = rest[: groups - 1]
    for g in reversed(range(groups)):
        beyond[g] = cross(far[g])
    near_all = jnp.stack(rest[groups - 1 :], 1)
    near = [near_all[r] for r in ranges]
    partner_all = fold(near_all[:, -1])
    partner = [partner_all[r] for r in ranges]

    wide = [((18 * c, 2 * c), BF16), ((6 * c, 2 * c), BF16), ((6 * c, 2 * c), BF16)]
    space = [call(pack_space, wide, space_weight[j]) for j in range(2)]
    times = call(pack_time, [((3 * c, 3 * c), BF16)] * 2, time_weight)
    down = call(pack_down, [((18 * c, outer), BF16), ((9 * c, outer), BF16)], down_weight)
    attention = call(pack_attn, [((3 * outer, outer), BF16)] * 2, w_query, w_key, w_value, w_out)

    def near_conv(block, far, near, partner):
        return call(
            functools.partial(conv_near, block),
            [(near.shape, F32), (far.shape, F32)],
            far,
            near,
            partner,
            norm_gain,
            *space[block],
        )

    def far_conv(block, part, beyond):
        return call(
            functools.partial(conv_far, block), [(part.shape, F32)], part, beyond, norm_gain, space[block][1]
        )[0]

    def mix(block, x, u):
        def body(*refs):
            mix_own(groups, refs[:groups], refs[groups : 2 * groups], refs[2 * groups], refs[2 * groups + 1 :])

        return call(body, [(a.shape, F32) for a in x], *x, *u, times[block])

    def mix_in(block, x, u, got):
        return call(mix_earlier, [(x.shape, F32)], x, u, got, times[block])[0]

    last = groups - 1
    for block in range(2):
        u_near, part = [None] * groups, [None] * groups
        for g in reversed(range(groups)):
            u_near[g], part[g] = near_conv(block, far[g], near[g], partner[g])
            if g == last:
                got_near = shift(u_near[g])
        near = list(mix(block, near, u_near))
        u_far = [None] * groups
        for g in reversed(range(groups)):
            u_far[g] = far_conv(block, part[g], beyond[g])
            if g == last:
                got_far = shift(u_far[g])
        far = list(mix(block, far, u_far))
        if block == 0:
            partner, beyond = [None] * groups, [None] * groups
        for g in reversed(range(groups)):
            if g == 0:
                near[0] = mix_in(block, near[0], u_near[0], got_near)
                far[0] = mix_in(block, far[0], u_far[0], got_far)
            if block == 0:
                partner[g] = fold(near[g][:, -1])
                beyond[g] = cross(far[g])

    piece = (rows // 2 + 1, w // 2, outer)

    def staged(body, outs, args, scratch, limit):
        return pl.pallas_call(
            body,
            out_shape=outs,
            in_specs=[VM] * len(args),
            out_specs=jax.tree.map(lambda _: VM, outs),
            scratch_shapes=[pltpu.VMEM(*s) for s in scratch],
            compiler_params=pltpu.CompilerParams(vmem_limit_bytes=limit << 20),
            cost_estimate=pl.CostEstimate(flops=1 << 20, bytes_accessed=1 << 20, transcendentals=0),
        )(*args)

    rowed = []
    for g in range(groups):
        count = far[g].shape[0]
        rowed.append(
            staged(
                down_rows,
                jax.ShapeDtypeStruct((count, *piece), F32),
                (far[g], near[g], *down),
                [((count * w, c), F32)],
                28,
            )
        )

    def spread_body(*refs):
        spread_out(refs[:groups], refs[groups:])

    held = call(spread_body, [(piece, F32)] * n, *rowed)
    group = tiles // n
    held = [
        lax.ppermute(x, "tile", [(i, i ^ (step * group)) for i in range(tiles)]) if step else x
        for step, x in enumerate(held)
    ]
    held = [x[None] for x in held]
    for level in range(group.bit_length() - 1):
        pairing = [(i, i ^ (1 << level)) for i in range(tiles)]
        got = [lax.ppermute(x, "tile", pairing) for x in held]
        if level < group.bit_length() - 2:
            held = [jnp.concatenate(both, 0) for both in zip(held, got)]
    pieces = []
    for both in zip(held, got):
        pieces += both
    size = (rows // 2) * (w // 2)
    total = tiles * size
    result = staged(
        functools.partial(attend, len(pieces)),
        jax.ShapeDtypeStruct((total // group, outer), F32),
        (*pieces, attn_gain.reshape(1, outer), *attention),
        [
            ((tiles + 1, size, outer), F32),
            ((total // group, outer), F32),
            ((total, 3 * outer), BF16),
            ((3 * total, outer), BF16),
        ],
        28 if total < 2048 else 60,
    )
    return result[None]


def solution(mesh):
    in_specs = (P("frame", "tile", None, None), P(), P(), P(), P(), P(), P(), P(), P(), P())
    out_specs = P(("frame", "tile"), None, None)
    return jax.shard_map(local, mesh=mesh, in_specs=in_specs, out_specs=out_specs, check_vma=False)
```

time: 59.5 us -> 57.3 us (0.963)
  local copies, waits for them, and re-layouts: 3.29 us -> 1.79 us
  Pallas kernels: 14.8 us -> 14 us
    slice x1, local copies, waits for them, and re-layouts: 1.2 us -> 0.02 us  [local(): near = [near_all[r] for r in ranges]]
    squeeze x2 -> x1, local copies, waits for them, and re-layouts: 1.17 us -> 0.1 us  [local(): space = [call(pack_space, wide, space_weight[j]) for j in range(2)]]
    ppermute x4, waiting for transfers between devices: 5.59 us -> 6.45 us  [cross(): return lax.ppermute(x, 'tile', across)]
    pallas_call x2 -> x3, Pallas kernels: 5.06 us -> 4.21 us  [staged(): pl.pallas_call(body, out_shape=outs, in_specs=[VM] * len(args), out_specs...]
    unnamed x18 -> x20, local copies, waits for them, and re-layouts: 0.9 us -> 1.65 us
    pallas_call x21 -> x24, Pallas kernels: 9.74 us -> 9.76 us  [the longest x22 9.52 us: called(): pl.pallas_call(body, out_shape=outs, in_specs=[VM] * len(args), out_specs...]
  transfers between devices with their start and end apart: 18 -> 18, of which waited for: 9 -> 9; matrix products, arithmetic and copies ran while one was open for 2% -> 0% of each run, Pallas kernels for 16% -> 16%
where the time goes in v3:
time: 57.3 us; the launch traced here: 57.1 us
  waiting for transfers between devices  23.7 us (41%)
  starting transfers between devices  17.3 us (30%)
  Pallas kernels  14 us (24%)
  local copies, waits for them, and re-layouts  1.79 us (3%)
    pallas_call x22, Pallas kernels, called(): pl.pallas_call(body, out_shape=outs, in_specs=[VM] * len(args), out_specs...  9.52 us
    ppermute x4, waiting for transfers between devices, shift(): return lax.ppermute(x[-2:], 'frame', onward)  8.92 us
    ppermute x3, waiting for transfers between devices, local(): lax.ppermute(x, 'tile', [(i, i ^ step * group) for i in range(tiles)])  7.63 us
    ppermute x4, starting transfers between devices, cross(): return lax.ppermute(x, 'tile', across)  7.47 us
    ppermute x4, waiting for transfers between devices, cross(): return lax.ppermute(x, 'tile', across)  6.45 us
    ppermute x4, starting transfers between devices, shift(): return lax.ppermute(x[-2:], 'frame', onward)  4.71 us
    pallas_call x3, Pallas kernels, staged(): pl.pallas_call(body, out_shape=outs, in_specs=[VM] * len(args), out_specs...  4.21 us
    ppermute x3, starting transfers between devices, local(): lax.ppermute(x, 'tile', [(i, i ^ step * group) for i in range(tiles)])  3.9 us
  transfers between devices with their start and end apart: 18, of which 9 were waited for; matrix products, arithmetic and copies ran while one was open for 0% of the time, Pallas kernels for 16%

profile of v3, /device:TPU:0, one launch (start us, length us, event | category | flops | bytes accessed | tf_op | source)
XLA Modules:
  0.0 57.1 jit_solution(10400695297820554906)
XLA Ops:
  0.0 1.1 %copy-done = f32[4,2,160,128]{3,2,1,0:T(8,128)S(1)} copy-done((f32[4,2,160,128]{3,2,1,0:T(8,128)S(1)}, f32[4,2,160,128]{3,2,1,0:T(8,128)}, u32[]{:S(2)}) %copy-start) | copy-done | bytes 655384
  1.1 0.2 shard_map.100
  1.2 0.6 collective-permute-start
  1.8 3.5 %collective-permute-start.1 = (f32[2,160,128]{2,1,0:T(8,128)S(1)}, f32[2,160,128]{2,1,0:T(8,128)S(1)}, u32[]{:S(2)}, u32[]{:S(2)}) collective-permute-start(f32[2,160,128]{2,1,0:T(8,128)S(1)} %get-tuple-element.39.far_ref.refs_0_), channel_id=1, source_target_pairs={{0,28},{4,8},{8,4},{12,16},{16,12},{20,24},{24,20},{28,0},{1,29},{... | collective-permute-start | bytes 491528 | tf_op jit(solution)/shard_map/ppermute | solution.py:303
  5.4 0.1 shard_map.101.far_ref.refs_1_
  5.5 0.0 copy-start.2
  5.5 0.1 collective-permute-start.2
  5.6 0.1 slice_bitcast_fusion
  5.7 0.0 copy-start.7
  5.7 0.3 shard_map.102
  5.9 0.5 copy-done.2
  6.5 0.1 shard_map.107
  6.6 0.9 %shard_map.105 = (f32[2,1,160,128]{3,2,1,0:T(8,128)S(1)}, f32[2,160,128]{2,1,0:T(8,128)S(1)}) custom-call(f32[2,160,128]{2,1,0:T(8,128)S(1)} %shard_map.101.far_ref.refs_1_, f32[2,1,160,128]{3,2,1,0:T(8,128)S(1)} %get-tuple-element.77.near_ref.refs_1_, f32[2,160,128]{2,1,0:T(8,128)S(1)} %get-tuple-element.75.partner_ref, f32[2,2,128]{2,1,0:T(2,128)S(1)} %copy-done.7, ...), custom_call_target="tpu_custom_call" | custom-call | bytes 2787328 | tf_op jit(solution)/shard_map/pallas_call | solution.py:23
  7.6 5.4 %collective-permute-done.2.beyond_ref = f32[2,160,128]{2,1,0:T(8,128)S(1)} collective-permute-done((f32[2,160,128]{2,1,0:T(8,128)S(1)}, f32[2,160,128]{2,1,0:T(8,128)S(1)}, u32[]{:S(2)}, u32[]{:S(2)}) %collective-permute-start.2) | collective-permute-done | bytes 163872 | tf_op jit(solution)/shard_map/ppermute | solution.py:303
  12.9 0.5 shard_map.106.refs_3_
  13.4 1.8 %collective-permute-start.3 = (f32[2,160,128]{2,1,0:T(8,128)S(1)}, f32[2,160,128]{2,1,0:T(8,128)S(1)}, u32[]{:S(2)}, u32[]{:S(2)}) collective-permute-start(f32[2,160,128]{2,1,0:T(8,128)S(1)} %shard_map.106.refs_3_), channel_id=1, source_target_pairs={{0,1},{1,2},{2,3},{3,0},{4,5},{5,6},{6,7},{7,4},{8,9},{9,10},{10,1... | collective-permute-start | bytes 491528 | tf_op jit(solution)/shard_map/ppermute | solution.py:306
  15.2 1.6 %collective-permute-start.4 = (f32[2,1,160,128]{3,2,1,0:T(8,128)S(1)}, f32[2,1,160,128]{3,2,1,0:T(8,128)S(1)}, u32[]{:S(2)}, u32[]{:S(2)}) collective-permute-start(f32[2,1,160,128]{3,2,1,0:T(8,128)S(1)} %get-tuple-element.50.refs_3_), channel_id=1, source_target_pairs={{0,1},{1,2},{2,3},{3,0},{4,5},{5,6},{6,7},{7,4},{8,9},{9,10},{10,1... | collective-permute-start | bytes 491528 | tf_op jit(solution)/shard_map/ppermute | solution.py:306
  16.8 0.9 %shard_map.103 = (f32[2,1,160,128]{3,2,1,0:T(8,128)S(1)}, f32[2,160,128]{2,1,0:T(8,128)S(1)}) custom-call(f32[2,160,128]{2,1,0:T(8,128)S(1)} %get-tuple-element.39.far_ref.refs_0_, f32[2,1,160,128]{3,2,1,0:T(8,128)S(1)} %get-tuple-element.78.near_ref.refs_0_, f32[2,160,128]{2,1,0:T(8,128)S(1)} %get-tuple-element.76.partner_ref, f32[2,2,128]{2,1,0:T(2,128)S(1)} %copy-done.7, ...), custom_call_target="tpu_custom_call" | custom-call | bytes 2787328 | tf_op jit(solution)/shard_map/pallas_call | solution.py:23
  17.8 0.4 shard_map.110
  18.2 0.1 collective-permute-start.7
  18.2 0.0 collective-permute-done.1.beyond_ref
  18.3 0.5 shard_map.104.refs_2_.u_ref
  18.8 0.4 shard_map.108
  19.2 1.8 %collective-permute-start.8 = (f32[2,160,128]{2,1,0:T(8,128)S(1)}, f32[2,160,128]{2,1,0:T(8,128)S(1)}, u32[]{:S(2)}, u32[]{:S(2)}) collective-permute-start(f32[2,160,128]{2,1,0:T(8,128)S(1)} %get-tuple-element.48.far_ref.refs_1_), channel_id=1, source_target_pairs={{0,28},{4,8},{8,4},{12,16},{16,12},{20,24},{24,20},{28,0},{1,29},{... | collective-permute-start | bytes 491528 | tf_op jit(solution)/shard_map/ppermute | solution.py:303
  21.0 0.3 shard_map.112
  21.2 4.0 %collective-permute-done.4.got_ref = f32[2,1,160,128]{3,2,1,0:T(8,128)S(1)} collective-permute-done((f32[2,1,160,128]{3,2,1,0:T(8,128)S(1)}, f32[2,1,160,128]{3,2,1,0:T(8,128)S(1)}, u32[]{:S(2)}, u32[]{:S(2)}) %collective-permute-start.4) | collective-permute-done | bytes 163872 | tf_op jit(solution)/shard_map/ppermute | solution.py:306
  25.3 0.2 shard_map.111.near_ref.refs_0_
  25.5 0.1 collective-permute-start.5
  25.6 0.0 collective-permute-done.3.got_ref
  25.6 0.2 shard_map.109.far_ref.refs_0_
  25.8 2.0 %collective-permute-start.6 = (f32[2,160,128]{2,1,0:T(8,128)S(1)}, f32[2,160,128]{2,1,0:T(8,128)S(1)}, u32[]{:S(2)}, u32[]{:S(2)}) collective-permute-start(f32[2,160,128]{2,1,0:T(8,128)S(1)} %shard_map.109.far_ref.refs_0_), channel_id=1, source_target_pairs={{0,28},{4,8},{8,4},{12,16},{16,12},{20,24},{24,20},{28,0},{1,29},{... | collective-permute-start | bytes 491528 | tf_op jit(solution)/shard_map/ppermute | solution.py:303
  27.8 0.0 collective-permute-done.7.partner_ref
  27.8 0.9 %shard_map.115 = (f32[2,1,160,128]{3,2,1,0:T(8,128)S(1)}, f32[2,160,128]{2,1,0:T(8,128)S(1)}) custom-call(f32[2,160,128]{2,1,0:T(8,128)S(1)} %get-tuple-element.48.far_ref.refs_1_, f32[2,1,160,128]{3,2,1,0:T(8,128)S(1)} %get-tuple-element.56.near_ref.refs_1_, f32[2,160,128]{2,1,0:T(8,128)S(1)} %collective-permute-done.7.partner_ref, ...), custom_call_target="tpu_custom_call" | custom-call | bytes 2787328 | tf_op jit(solution)/shard_map/pallas_call | solution.py:23
  28.8 0.5 shard_map.116.refs_3_
  29.3 0.1 collective-permute-start.9
  29.3 1.3 %collective-permute-start.10 = (f32[2,1,160,128]{3,2,1,0:T(8,128)S(1)}, f32[2,1,160,128]{3,2,1,0:T(8,128)S(1)}, u32[]{:S(2)}, u32[]{:S(2)}) collective-permute-start(f32[2,1,160,128]{3,2,1,0:T(8,128)S(1)} %get-tuple-element.61.refs_3_), channel_id=1, source_target_pairs={{0,1},{1,2},{2,3},{3,0},{4,5},{5,6},{6,7},{7,4},{8,9},{9,10},{10,1... | collective-permute-start | bytes 491528 | tf_op jit(solution)/shard_map/ppermute | solution.py:306
  30.6 0.2 shard_map.121
  30.9 0.9 %shard_map.113 = (f32[2,1,160,128]{3,2,1,0:T(8,128)S(1)}, f32[2,160,128]{2,1,0:T(8,128)S(1)}) custom-call(f32[2,160,128]{2,1,0:T(8,128)S(1)} %shard_map.109.far_ref.refs_0_, f32[2,1,160,128]{3,2,1,0:T(8,128)S(1)} %shard_map.111.near_ref.refs_0_, f32[2,160,128]{2,1,0:T(8,128)S(1)} %collective-permute-done.5.partner_ref, f32[2,2,128]{2,1,0:T(2,128)S(1)} %copy-done.7, ...), custom_call_target="tpu_custom_call" | custom-call | bytes 2787328 | tf_op jit(solution)/shard_map/pallas_call | solution.py:23
  31.8 1.1 %collective-permute-done.6.beyond_ref = f32[2,160,128]{2,1,0:T(8,128)S(1)} collective-permute-done((f32[2,160,128]{2,1,0:T(8,128)S(1)}, f32[2,160,128]{2,1,0:T(8,128)S(1)}, u32[]{:S(2)}, u32[]{:S(2)}) %collective-permute-start.6) | collective-permute-done | bytes 163872 | tf_op jit(solution)/shard_map/ppermute | solution.py:303
  32.8 0.5 shard_map.114.refs_2_.u_ref
  33.3 0.4 shard_map.117
  33.8 0.4 shard_map.119
  34.2 3.4 %collective-permute-done.9.got_ref = f32[2,160,128]{2,1,0:T(8,128)S(1)} collective-permute-done((f32[2,160,128]{2,1,0:T(8,128)S(1)}, f32[2,160,128]{2,1,0:T(8,128)S(1)}, u32[]{:S(2)}, u32[]{:S(2)}) %collective-permute-start.9) | collective-permute-done | bytes 163872 | tf_op jit(solution)/shard_map/ppermute | solution.py:306
  37.5 0.2 shard_map.118.far_ref
  37.8 1.5 %collective-permute-done.10.got_ref = f32[2,1,160,128]{3,2,1,0:T(8,128)S(1)} collective-permute-done((f32[2,1,160,128]{3,2,1,0:T(8,128)S(1)}, f32[2,1,160,128]{3,2,1,0:T(8,128)S(1)}, u32[]{:S(2)}, u32[]{:S(2)}) %collective-permute-start.10) | collective-permute-done | bytes 163872 | tf_op jit(solution)/shard_map/ppermute | solution.py:306
  39.3 0.2 shard_map.120.near_ref
  39.5 0.5 shard_map.122.refs_0_
  40.0 0.0 copy-start.3
  40.0 0.0 copy-start.4
  40.0 0.0 copy-start.5
  40.1 0.0 copy-start.6
  40.1 0.5 shard_map.123.refs_1_
  40.6 0.0 copy-start.8
  40.6 0.1 shard_map.124
  40.7 2.4 %collective-permute-start.12 = (f32[2,80,256]{2,1,0:T(8,128)S(1)}, f32[2,80,256]{2,1,0:T(8,128)S(1)}, u32[]{:S(2)}, u32[]{:S(2)}) collective-permute-start(f32[2,80,256]{2,1,0:T(8,128)S(1)} %get-tuple-element.68), channel_id=1, source_target_pairs={{0,8},{4,12},{8,0},{12,4},{16,24},{20,28},{24,16},{28,20},{1,9},{5... | collective-permute-start | bytes 491528 | tf_op jit(solution)/shard_map/ppermute | solution.py:431
  43.1 0.8 %collective-permute-start.14 = (f32[2,80,256]{2,1,0:T(8,128)S(1)}, f32[2,80,256]{2,1,0:T(8,128)S(1)}, u32[]{:S(2)}, u32[]{:S(2)}) collective-permute-start(f32[2,80,256]{2,1,0:T(8,128)S(1)} %get-tuple-element.69), channel_id=1, source_target_pairs={{0,16},{4,20},{8,24},{12,28},{16,0},{20,4},{24,8},{28,12},{1,17},{... | collective-permute-start | bytes 491528 | tf_op jit(solution)/shard_map/ppermute | solution.py:431
  43.8 0.7 %collective-permute-start.16 = (f32[2,80,256]{2,1,0:T(8,128)S(1)}, f32[2,80,256]{2,1,0:T(8,128)S(1)}, u32[]{:S(2)}, u32[]{:S(2)}) collective-permute-start(f32[2,80,256]{2,1,0:T(8,128)S(1)} %get-tuple-element.70), channel_id=1, source_target_pairs={{0,24},{4,28},{8,16},{12,20},{16,8},{20,12},{24,0},{28,4},{1,25},{... | collective-permute-start | bytes 491528 | tf_op jit(solution)/shard_map/ppermute | solution.py:431
  44.6 3.5 %collective-permute-done.12 = f32[2,80,256]{2,1,0:T(8,128)S(1)} collective-permute-done((f32[2,80,256]{2,1,0:T(8,128)S(1)}, f32[2,80,256]{2,1,0:T(8,128)S(1)}, u32[]{:S(2)}, u32[]{:S(2)}) %collective-permute-start.12) | collective-permute-done | bytes 163872 | tf_op jit(solution)/shard_map/ppermute | solution.py:431
  48.1 4.1 %collective-permute-done.14 = f32[2,80,256]{2,1,0:T(8,128)S(1)} collective-permute-done((f32[2,80,256]{2,1,0:T(8,128)S(1)}, f32[2,80,256]{2,1,0:T(8,128)S(1)}, u32[]{:S(2)}, u32[]{:S(2)}) %collective-permute-start.14) | collective-permute-done | bytes 163872 | tf_op jit(solution)/shard_map/ppermute | solution.py:431
  52.2 0.5 collective-permute-start.17
  52.8 0.4 shard_map.125
  53.2 0.4 collective-permute-done.15.refs_5_
  53.6 0.2 collective-permute-done.17.refs_7_
  53.9 3.2 %shard_map.126 = f32[320,256]{1,0:T(8,128)} custom-call(f32[1,2,80,256]{3,2,1,0:T(8,128)S(1)} %bitcast.19, f32[1,2,80,256]{3,2,1,0:T(8,128)S(1)} %collective-permute-done.11.refs_1_, f32[1,2,80,256]{3,2,1,0:T(8,128)S(1)} %bitcast.21, f32[1,2,80,256]{3,2,1,0:T(8,128)S(1)} %collective-permute-done.13.refs_3_, f32[1,2,80,256]{3,2,1,0:T(8,128)S(1)} %bitcast.23, ...), custom_call_target="tpu_custom_call" | custom-call | flops 1048576 | bytes 1048576 | tf_op jit(solution)/shard_map/pallas_call | solution.py:402
  (22 shorter events, 0.1 us)
Async XLA Ops:
  0.0 1.1 %copy-start = (f32[4,2,160,128]{3,2,1,0:T(8,128)S(1)}, f32[4,2,160,128]{3,2,1,0:T(8,128)}, u32[]{:S(2)}) copy-start(f32[4,2,160,128]{3,2,1,0:T(8,128)} %video_ref.3) | copy-start | bytes 1966084
  1.1 4.5 %copy-start.9 = (f32[2,3,3,128,128]{4,3,2,1,0:T(8,128)S(1)}, f32[2,3,3,128,128]{4,3,2,1,0:T(8,128)}, u32[]{:S(2)}) copy-start(f32[2,3,3,128,128]{4,3,2,1,0:T(8,128)} %param.12) | copy-start | bytes 3538948
  1.2 5.3 %collective-permute-start = (f32[4,160,128]{2,1,0:T(8,128)S(1)}, f32[4,160,128]{2,1,0:T(8,128)S(1)}, u32[]{:S(2)}, u32[]{:S(2)}) collective-permute-start(f32[4,160,128]{2,1,0:T(8,128)S(1)} %get-tuple-element.40), channel_id=1, source_target_pairs={{0,4},{4,0},{8,12},{12,8},{16,20},{20,16},{24,28},{28,24},{1,5},{5... | collective-permute-start | bytes 983048 | tf_op jit(solution)/shard_map/ppermute | solution.py:300
  1.8 16.4 %collective-permute-start.1 = (f32[2,160,128]{2,1,0:T(8,128)S(1)}, f32[2,160,128]{2,1,0:T(8,128)S(1)}, u32[]{:S(2)}, u32[]{:S(2)}) collective-permute-start(f32[2,160,128]{2,1,0:T(8,128)S(1)} %get-tuple-element.39.far_ref.refs_0_), channel_id=1, source_target_pairs={{0,28},{4,8},{8,4},{12,16},{16,12},{20,24},{24,20},{28,0},{1,29},{... | collective-permute-start | bytes 491528 | tf_op jit(solution)/shard_map/ppermute | solution.py:303
  5.5 1.0 %copy-start.2 = (f32[2,3,128,128]{3,2,1,0:T(8,128)S(1)}, f32[2,3,128,128]{3,2,1,0:T(8,128)}, u32[]{:S(2)}) copy-start(f32[2,3,128,128]{3,2,1,0:T(8,128)} %time_ref.1) | copy-start | bytes 1179652
  5.5 7.5 %collective-permute-start.2 = (f32[2,160,128]{2,1,0:T(8,128)S(1)}, f32[2,160,128]{2,1,0:T(8,128)S(1)}, u32[]{:S(2)}, u32[]{:S(2)}) collective-permute-start(f32[2,160,128]{2,1,0:T(8,128)S(1)} %shard_map.101.far_ref.refs_1_), channel_id=1, source_target_pairs={{0,28},{4,8},{8,4},{12,16},{16,12},{20,24},{24,20},{28,0},{1,29},{... | collective-permute-start | bytes 491528 | tf_op jit(solution)/shard_map/ppermute | solution.py:303
  5.7 1.0 %copy-start.7 = (f32[2,2,128]{2,1,0:T(2,128)S(1)}, f32[2,2,128]{2,1,0:T(2,128)}, u32[]{:S(2)}) copy-start(f32[2,2,128]{2,1,0:T(2,128)} %gain_ref.15) | copy-start | bytes 6148
  13.4 12.1 %collective-permute-start.3 = (f32[2,160,128]{2,1,0:T(8,128)S(1)}, f32[2,160,128]{2,1,0:T(8,128)S(1)}, u32[]{:S(2)}, u32[]{:S(2)}) collective-permute-start(f32[2,160,128]{2,1,0:T(8,128)S(1)} %shard_map.106.refs_3_), channel_id=1, source_target_pairs={{0,1},{1,2},{2,3},{3,0},{4,5},{5,6},{6,7},{7,4},{8,9},{9,10},{10,1... | collective-permute-start | bytes 491528 | tf_op jit(solution)/shard_map/ppermute | solution.py:306
  15.2 10.0 %collective-permute-start.4 = (f32[2,1,160,128]{3,2,1,0:T(8,128)S(1)}, f32[2,1,160,128]{3,2,1,0:T(8,128)S(1)}, u32[]{:S(2)}, u32[]{:S(2)}) collective-permute-start(f32[2,1,160,128]{3,2,1,0:T(8,128)S(1)} %get-tuple-element.50.refs_3_), channel_id=1, source_target_pairs={{0,1},{1,2},{2,3},{3,0},{4,5},{5,6},{6,7},{7,4},{8,9},{9,10},{10,1... | collective-permute-start | bytes 491528 | tf_op jit(solution)/shard_map/ppermute | solution.py:306
  18.2 9.7 %collective-permute-start.7 = (f32[2,160,128]{2,1,0:T(8,128)S(1)}, f32[2,160,128]{2,1,0:T(8,128)S(1)}, u32[]{:S(2)}, u32[]{:S(2)}) collective-permute-start(f32[2,160,128]{2,1,0:T(8,128)S(1)} %bitcast.17), channel_id=1, source_target_pairs={{0,4},{4,0},{8,12},{12,8},{16,20},{20,16},{24,28},{28,24},{1,5},{5... | collective-permute-start | bytes 491528 | tf_op jit(solution)/shard_map/ppermute | solution.py:300
  19.2 9.6 %collective-permute-start.8 = (f32[2,160,128]{2,1,0:T(8,128)S(1)}, f32[2,160,128]{2,1,0:T(8,128)S(1)}, u32[]{:S(2)}, u32[]{:S(2)}) collective-permute-start(f32[2,160,128]{2,1,0:T(8,128)S(1)} %get-tuple-element.48.far_ref.refs_1_), channel_id=1, source_target_pairs={{0,28},{4,8},{8,4},{12,16},{16,12},{20,24},{24,20},{28,0},{1,29},{... | collective-permute-start | bytes 491528 | tf_op jit(solution)/shard_map/ppermute | solution.py:303
  25.5 5.4 %collective-permute-start.5 = (f32[2,160,128]{2,1,0:T(8,128)S(1)}, f32[2,160,128]{2,1,0:T(8,128)S(1)}, u32[]{:S(2)}, u32[]{:S(2)}) collective-permute-start(f32[2,160,128]{2,1,0:T(8,128)S(1)} %bitcast.16), channel_id=1, source_target_pairs={{0,4},{4,0},{8,12},{12,8},{16,20},{20,16},{24,28},{28,24},{1,5},{5... | collective-permute-start | bytes 491528 | tf_op jit(solution)/shard_map/ppermute | solution.py:300
  25.8 7.0 %collective-permute-start.6 = (f32[2,160,128]{2,1,0:T(8,128)S(1)}, f32[2,160,128]{2,1,0:T(8,128)S(1)}, u32[]{:S(2)}, u32[]{:S(2)}) collective-permute-start(f32[2,160,128]{2,1,0:T(8,128)S(1)} %shard_map.109.far_ref.refs_0_), channel_id=1, source_target_pairs={{0,28},{4,8},{8,4},{12,16},{16,12},{20,24},{24,20},{28,0},{1,29},{... | collective-permute-start | bytes 491528 | tf_op jit(solution)/shard_map/ppermute | solution.py:303
  27.8 2.8 %copy-start.1 = (f32[3,3,128,256]{3,2,1,0:T(8,128)S(1)}, f32[3,3,128,256]{3,2,1,0:T(8,128)}, u32[]{:S(2)}) copy-start(f32[3,3,128,256]{3,2,1,0:T(8,128)} %down_ref.1) | copy-start | bytes 3538948
  29.3 8.3 %collective-permute-start.9 = (f32[2,160,128]{2,1,0:T(8,128)S(1)}, f32[2,160,128]{2,1,0:T(8,128)S(1)}, u32[]{:S(2)}, u32[]{:S(2)}) collective-permute-start(f32[2,160,128]{2,1,0:T(8,128)S(1)} %shard_map.116.refs_3_), channel_id=1, source_target_pairs={{0,1},{1,2},{2,3},{3,0},{4,5},{5,6},{6,7},{7,4},{8,9},{9,10},{10,1... | collective-permute-start | bytes 491528 | tf_op jit(solution)/shard_map/ppermute | solution.py:306
  29.3 9.9 %collective-permute-start.10 = (f32[2,1,160,128]{3,2,1,0:T(8,128)S(1)}, f32[2,1,160,128]{3,2,1,0:T(8,128)S(1)}, u32[]{:S(2)}, u32[]{:S(2)}) collective-permute-start(f32[2,1,160,128]{3,2,1,0:T(8,128)S(1)} %get-tuple-element.61.refs_3_), channel_id=1, source_target_pairs={{0,1},{1,2},{2,3},{3,0},{4,5},{5,6},{6,7},{7,4},{8,9},{9,10},{10,1... | collective-permute-start | bytes 491528 | tf_op jit(solution)/shard_map/ppermute | solution.py:306
  40.0 12.7 %copy-start.3 = (f32[256,256]{1,0:T(8,128)S(1)}, f32[256,256]{1,0:T(8,128)}, u32[]{:S(2)}) copy-start(f32[256,256]{1,0:T(8,128)} %q_ref.1) | copy-start | bytes 786436
  40.0 12.7 %copy-start.4 = (f32[256,256]{1,0:T(8,128)S(1)}, f32[256,256]{1,0:T(8,128)}, u32[]{:S(2)}) copy-start(f32[256,256]{1,0:T(8,128)} %k_ref.1) | copy-start | bytes 786436
  40.0 12.7 %copy-start.5 = (f32[256,256]{1,0:T(8,128)S(1)}, f32[256,256]{1,0:T(8,128)}, u32[]{:S(2)}) copy-start(f32[256,256]{1,0:T(8,128)} %v_ref.1) | copy-start | bytes 786436
  40.1 12.7 %copy-start.6 = (f32[256,256]{1,0:T(8,128)S(1)}, f32[256,256]{1,0:T(8,128)}, u32[]{:S(2)}) copy-start(f32[256,256]{1,0:T(8,128)} %o_ref.1) | copy-start | bytes 786436
  40.6 13.3 %copy-start.8 = (f32[256]{0:T(256)S(1)}, f32[256]{0:T(256)}, u32[]{:S(2)}) copy-start(f32[256]{0:T(256)} %param.15) | copy-start | bytes 3076
  40.7 7.4 %collective-permute-start.12 = (f32[2,80,256]{2,1,0:T(8,128)S(1)}, f32[2,80,256]{2,1,0:T(8,128)S(1)}, u32[]{:S(2)}, u32[]{:S(2)}) collective-permute-start(f32[2,80,256]{2,1,0:T(8,128)S(1)} %get-tuple-element.68), channel_id=1, source_target_pairs={{0,8},{4,12},{8,0},{12,4},{16,24},{20,28},{24,16},{28,20},{1,9},{5... | collective-permute-start | bytes 491528 | tf_op jit(solution)/shard_map/ppermute | solution.py:431
  43.1 9.2 %collective-permute-start.14 = (f32[2,80,256]{2,1,0:T(8,128)S(1)}, f32[2,80,256]{2,1,0:T(8,128)S(1)}, u32[]{:S(2)}, u32[]{:S(2)}) collective-permute-start(f32[2,80,256]{2,1,0:T(8,128)S(1)} %get-tuple-element.69), channel_id=1, source_target_pairs={{0,16},{4,20},{8,24},{12,28},{16,0},{20,4},{24,8},{28,12},{1,17},{... | collective-permute-start | bytes 491528 | tf_op jit(solution)/shard_map/ppermute | solution.py:431
  43.8 8.4 %collective-permute-start.16 = (f32[2,80,256]{2,1,0:T(8,128)S(1)}, f32[2,80,256]{2,1,0:T(8,128)S(1)}, u32[]{:S(2)}, u32[]{:S(2)}) collective-permute-start(f32[2,80,256]{2,1,0:T(8,128)S(1)} %get-tuple-element.70), channel_id=1, source_target_pairs={{0,24},{4,28},{8,16},{12,20},{16,8},{20,12},{24,0},{28,4},{1,25},{... | collective-permute-start | bytes 491528 | tf_op jit(solution)/shard_map/ppermute | solution.py:431
  44.6 8.6 %collective-permute-start.11 = (f32[1,2,80,256]{3,2,1,0:T(8,128)S(1)}, f32[1,2,80,256]{3,2,1,0:T(8,128)S(1)}, u32[]{:S(2)}, u32[]{:S(2)}) collective-permute-start(f32[1,2,80,256]{3,2,1,0:T(8,128)S(1)} %bitcast.18), channel_id=1, source_target_pairs={{0,4},{4,0},{8,12},{12,8},{16,20},{20,16},{24,28},{28,24},{1,5},{5... | collective-permute-start | bytes 491528 | tf_op jit(solution)/shard_map/ppermute | solution.py:437
  48.1 5.1 %collective-permute-start.13 = (f32[1,2,80,256]{3,2,1,0:T(8,128)S(1)}, f32[1,2,80,256]{3,2,1,0:T(8,128)S(1)}, u32[]{:S(2)}, u32[]{:S(2)}) collective-permute-start(f32[1,2,80,256]{3,2,1,0:T(8,128)S(1)} %bitcast.20), channel_id=1, source_target_pairs={{0,4},{4,0},{8,12},{12,8},{16,20},{20,16},{24,28},{28,24},{1,5},{5... | collective-permute-start | bytes 491528 | tf_op jit(solution)/shard_map/ppermute | solution.py:437
  52.2 1.4 %collective-permute-start.15 = (f32[1,2,80,256]{3,2,1,0:T(8,128)S(1)}, f32[1,2,80,256]{3,2,1,0:T(8,128)S(1)}, u32[]{:S(2)}, u32[]{:S(2)}) collective-permute-start(f32[1,2,80,256]{3,2,1,0:T(8,128)S(1)} %bitcast.22), channel_id=1, source_target_pairs={{0,4},{4,0},{8,12},{12,8},{16,20},{20,16},{24,28},{28,24},{1,5},{5... | collective-permute-start | bytes 491528 | tf_op jit(solution)/shard_map/ppermute | solution.py:437
  52.2 1.6 %collective-permute-start.17 = (f32[1,2,80,256]{3,2,1,0:T(8,128)S(1)}, f32[1,2,80,256]{3,2,1,0:T(8,128)S(1)}, u32[]{:S(2)}, u32[]{:S(2)}) collective-permute-start(f32[1,2,80,256]{3,2,1,0:T(8,128)S(1)} %bitcast.24), channel_id=1, source_target_pairs={{0,4},{4,0},{8,12},{12,8},{16,20},{20,16},{24,28},{28,24},{1,5},{5... | collective-permute-start | bytes 491528 | tf_op jit(solution)/shard_map/ppermute | solution.py:437

commit v4 on v3

--- a/solution.py
+++ b/solution.py
@@ -70,12 +70,12 @@
     return lax.rem(lax.axis_index("tile"), 2) == 0
 
 
-def pack_space(space_ref, pair_ref, above_ref, below_ref):
+def pack_space(block, space_ref, pair_ref, above_ref, below_ref):
     c = space_ref.shape[-1]
     even = is_even()
     for kh in range(3):
         at = jnp.where(even, kh, 2 - kh)
-        high, low = halves(jnp.concatenate([space_ref[at, kw] for kw in range(3)], 0))
+        high, low = halves(jnp.concatenate([space_ref[block, at, kw] for kw in range(3)], 0))
         three = jnp.concatenate([high, high, low], 0)
         for row in range(2):
             to = row + 1 - kh
@@ -193,72 +193,100 @@
     return left_side(jnp.concatenate([before, even, odd], -1))
 
 
-def down_rows(far_ref, near_ref, own_ref, next_ref, out_ref, flat_ref):
+def row_pixels(far_ref, near_ref, flat_ref, row):
     n, rest, w, c = near_ref.shape
-    rows = rest + 1
-    even = is_even()
 
     def held(row):
         return near_ref[:, row - 1] if row else far_ref[...]
 
-    parts = []
-    for row in range(rows):
-        flat_ref[: n * w] = jnp.where(even, held(row), held(rows - 1 - row)).reshape(n * w, c)
-        parts.append(pixels(flat_ref.at[: n * w], n, w))
-    for row in range(rows // 2 + 1):
-        total = mul(parts[2 * row - 1], next_ref[...]) if row else 0.0
-        if row < rows // 2:
-            total = total + mul(jnp.concatenate(parts[2 * row : 2 * row + 2], -1), own_ref[...])
+    flat_ref[...] = jnp.where(is_even(), held(row), held(rest - row)).reshape(n * w, c)
+    return pixels(flat_ref, n, w)
+
+
+def down_next(far_ref, near_ref, next_ref, out_ref, flat_ref):
+    product = mul(row_pixels(far_ref, near_ref, flat_ref, near_ref.shape[1]), next_ref[...])
+    out_ref[...] = product.reshape(out_ref.shape)
+
+
+def down_own(far_ref, near_ref, own_ref, next_ref, out_ref, flat_ref):
+    n, rest, w, _ = near_ref.shape
+    parts = [row_pixels(far_ref, near_ref, flat_ref, row) for row in range(rest + 1)]
+    for row in range((rest + 1) // 2):
+        total = mul(jnp.concatenate(parts[2 * row : 2 * row + 2], -1), own_ref[...])
+        if row:
+            total = total + mul(parts[2 * row - 1], next_ref[...])
         out_ref[:, row] = total.reshape(n, w // 2, -1)
 
 
-def spread_out(refs, out_refs):
+def spread_out(groups, refs, out_refs):
     frames = len(out_refs)
     mine = lax.axis_index("tile") // (lax.axis_size("tile") // frames)
+    even = is_even()
     start = 0
-    for ref in refs:
-        for f in range(ref.shape[0]):
+    for g in range(groups):
+        own_ref, next_ref, got_ref = refs[g], refs[groups + g], refs[2 * groups + g]
+        count, rows, w, _ = own_ref.shape
+        half = w // 2
+        for f in range(count):
             for step in range(frames):
 
                 @pl.when(mine ^ step == start + f)
                 def _():
-                    out_refs[step][...] = ref[f]
-
-        start += ref.shape[0]
-
-
-def attend(count, *refs):
+                    out_ref = out_refs[step]
+                    got = got_ref[f]
+                    out_ref[:w] = own_ref[f, 0] + jnp.where(even, 0.0, got)
+                    for row in range(1, rows):
+                        out_ref[row * w : (row + 1) * w] = own_ref[f, row]
+                    out_ref[rows * w :] = jnp.where(even, got[half:], next_ref[f, :half])
+
+        start += count
+
+
+def attend(count, w, *refs):
     held = refs[:count]
-    gain_ref, qk_ref, vo_ref, out_ref, z_ref, query_ref, k_ref, v_ref = refs[count:]
+    gain_ref, qk_ref, vo_ref, out_ref, next_ref, z_ref, query_ref, k_ref, v_ref = refs[count:]
     places = [(ref, i) for ref in held for i in range(ref.shape[0])]
     count = len(places)
-    _, rows, w, d = held[0].shape
-    rows -= 1
+    half = w // 2
+    size, d = z_ref.shape[1:]
     tile = lax.axis_index("tile")
+    next_ref[0] = jnp.zeros((w, d), F32)
     for m, (ref, i) in enumerate(places):
-        z_ref[tile ^ m] = ref[i, :rows].reshape(rows * w, d)
+        device = tile ^ m
+        odd = lax.rem(device, 2)
+        start = half * (1 - odd)
+        if half % 8 == 0:
+            start = pl.multiple_of(start, 8)
+        next_ref[device - odd + 2, pl.ds(start, half)] = ref[i, size:]
+    gain = gain_ref[0]
     for m, (ref, i) in enumerate(places):
-        at = (tile ^ m) + 1
-        z_ref[at, :w] = z_ref[at, :w] + ref[i, rows]
-    gain = gain_ref[0]
-    size = rows * w
-    step = min(count, 8)
-    for at in range(0, count, step):
-        high, low = halves(norm(z_ref[at : at + step].reshape(step * size, d), gain))
-        tokens = slice(at * size, (at + step) * size)
+        device = tile ^ m
+        odd = lax.rem(device, 2)
+        added = jnp.where(odd == 0, next_ref[device - odd], 0.0)
+        z_ref[m, :w] = ref[i, :w] + added
+        if size > w:
+            z_ref[m, w:] = ref[i, w:size]
+        high, low = halves(norm(z_ref[m], gain))
+        tokens = slice(m * size, (m + 1) * size)
         k_ref[tokens, :d] = high
         k_ref[tokens, d : 2 * d] = high
         k_ref[tokens, 2 * d :] = low
-        v_ref[at * size : (at + step) * size] = high
-        v_ref[(count + at) * size : (count + at + step) * size] = high
-        v_ref[(2 * count + at) * size : (2 * count + at + step) * size] = low
-    part = out_ref.shape[0] // count
-    for block in range(size // part):
-
-        @pl.when(lax.rem(tile, size // part) == block)
-        def _():
-            for b in range(count):
-                query_ref[b * part : (b + 1) * part] = z_ref[b, block * part : (block + 1) * part]
+        for place, values in enumerate((high, high, low)):
+            at = (place * count + m) * size
+            v_ref[at : at + size] = values
+    part = out_ref.shape[1]
+    block = lax.rem(tile, size // part)
+    if part % 8 == 0:
+        at = pl.multiple_of(block * part, 8)
+        for m in range(count):
+            query_ref[m * part : (m + 1) * part] = z_ref[m, pl.ds(at, part)]
+    else:
+        for b in range(size // part):
+
+            @pl.when(block == b)
+            def _():
+                for m in range(count):
+                    query_ref[m * part : (m + 1) * part] = z_ref[m, b * part : (b + 1) * part]
 
     mine = query_ref[...]
     query = mul(left_side(norm(mine, gain)), qk_ref[...])
@@ -268,7 +296,9 @@
     weights = jnp.exp(scores - jnp.max(scores, -1, keepdims=True))
     total = jnp.sum(weights, -1, keepdims=True)
     mixed = mul(left_side(weights), v_ref[...])
-    out_ref[...] = mine + mul(left_side(mixed / total), vo_ref[...])
+    result = mine + mul(left_side(mixed / total), vo_ref[...])
+    for m in range(count):
+        out_ref[tile ^ m] = result[m * part : (m + 1) * part]
 
 
 def local(
@@ -312,10 +342,11 @@
             outs, sem = refs[:-1], refs[-1]
             even = is_even()
             copies = []
-            for out, r, j in zip(outs, ranges, rows_of):
+            for i, (r, j, out) in enumerate(zip(ranges, rows_of, outs)):
                 at = jnp.where(even, j, rows - 1 - j)
-                copies.append(pltpu.make_async_copy(video_ref.at[r, at], out, sem.at[len(copies)]))
-                copies[-1].start()
+                copies.append(pltpu.make_async_copy(video_ref.at[r, at], out, sem.at[i]))
+            for copy in copies:
+                copy.start()
             for copy in copies:
                 copy.wait()
 
@@ -342,7 +373,7 @@
     partner = [partner_all[r] for r in ranges]
 
     wide = [((18 * c, 2 * c), BF16), ((6 * c, 2 * c), BF16), ((6 * c, 2 * c), BF16)]
-    space = [call(pack_space, wide, space_weight[j]) for j in range(2)]
+    space = [call(functools.partial(pack_space, j), wide, space_weight) for j in range(2)]
     times = call(pack_time, [((3 * c, 3 * c), BF16)] * 2, time_weight)
     down = call(pack_down, [((18 * c, outer), BF16), ((9 * c, outer), BF16)], down_weight)
     attention = call(pack_attn, [((3 * outer, outer), BF16)] * 2, w_query, w_key, w_value, w_out)
@@ -396,7 +427,8 @@
                 partner[g] = fold(near[g][:, -1])
                 beyond[g] = cross(far[g])
 
-    piece = (rows // 2 + 1, w // 2, outer)
+    half = w // 2
+    piece = (rows // 2 * half + half // 2, outer)
 
     def staged(body, outs, args, scratch, limit):
         return pl.pallas_call(
@@ -409,23 +441,29 @@
             cost_estimate=pl.CostEstimate(flops=1 << 20, bytes_accessed=1 << 20, transcendentals=0),
         )(*args)
 
-    rowed = []
-    for g in range(groups):
+    own, extra, got = [None] * groups, [None] * groups, [None] * groups
+    for g in reversed(range(groups)):
         count = far[g].shape[0]
-        rowed.append(
-            staged(
-                down_rows,
-                jax.ShapeDtypeStruct((count, *piece), F32),
-                (far[g], near[g], *down),
-                [((count * w, c), F32)],
-                28,
-            )
+        extra[g] = staged(
+            down_next,
+            jax.ShapeDtypeStruct((count, half, outer), F32),
+            (far[g], near[g], down[1]),
+            [((count * w, c), F32)],
+            28,
         )
+        got[g] = fold(extra[g])
+        own[g] = staged(
+            down_own,
+            jax.ShapeDtypeStruct((count, rows // 2, half, outer), F32),
+            (far[g], near[g], *down),
+            [((count * w, c), F32)],
+            28,
+        )
 
     def spread_body(*refs):
-        spread_out(refs[:groups], refs[groups:])
-
-    held = call(spread_body, [(piece, F32)] * n, *rowed)
+        spread_out(groups, refs[: 3 * groups], refs[3 * groups :])
+
+    held = call(spread_body, [(piece, F32)] * n, *own, *extra, *got)
     group = tiles // n
     held = [
         lax.ppermute(x, "tile", [(i, i ^ (step * group)) for i in range(tiles)]) if step else x
@@ -440,20 +478,22 @@
     pieces = []
     for both in zip(held, got):
         pieces += both
-    size = (rows // 2) * (w // 2)
+    size = rows // 2 * half
     total = tiles * size
     result = staged(
-        functools.partial(attend, len(pieces)),
-        jax.ShapeDtypeStruct((total // group, outer), F32),
+        functools.partial(attend, len(pieces), half),
+        jax.ShapeDtypeStruct((tiles, size // group, outer), F32),
         (*pieces, attn_gain.reshape(1, outer), *attention),
         [
-            ((tiles + 1, size, outer), F32),
+            ((tiles + 2, half, outer), F32),
+            ((tiles, size, outer), F32),
             ((total // group, outer), F32),
             ((total, 3 * outer), BF16),
             ((3 * total, outer), BF16),
         ],
         28 if total < 2048 else 60,
     )
+    result = result.reshape(-1, outer)
     return result[None]
 
 

time: 57.3 us -> 57.3 us (level)
  waiting for transfers between devices: 23.7 us -> 22.9 us
  starting transfers between devices: 17.3 us -> 17.9 us
    ppermute x3, waiting for transfers between devices: 7.63 us -> 6.4 us  [local(): lax.ppermute(x, 'tile', [(i, i ^ step * group) for i in range(tiles)])]
    ppermute x3 -> x5, starting transfers between devices: 0.7 us -> 1.33 us  [fold(): return lax.ppermute(x, 'tile', pairs)]
    pallas_call x3 -> x5, Pallas kernels: 4.21 us -> 4.45 us  [staged(): pl.pallas_call(body, out_shape=outs, in_specs=[VM] * len(args), out_specs...]
  transfers between devices with their start and end apart: 18 -> 20, of which waited for: 9 -> 10; matrix products, arithmetic and copies ran while one was open for 0% -> 0% of each run, Pallas kernels for 16% -> 18%
where the time goes in v4:
time: 57.3 us; the launch traced here: 57.1 us
  waiting for transfers between devices  22.9 us (40%)
  starting transfers between devices  17.9 us (31%)
  Pallas kernels  14.5 us (25%)
  local copies, waits for them, and re-layouts  1.42 us (2%)
    pallas_call x22, Pallas kernels, called(): pl.pallas_call(body, out_shape=outs, in_specs=[VM] * len(args), out_specs...  9.76 us
    ppermute x4, waiting for transfers between devices, shift(): return lax.ppermute(x[-2:], 'frame', onward)  8.96 us
    ppermute x4, starting transfers between devices, cross(): return lax.ppermute(x, 'tile', across)  7.45 us
    ppermute x4, waiting for transfers between devices, cross(): return lax.ppermute(x, 'tile', across)  6.87 us
    ppermute x3, waiting for transfers between devices, local(): lax.ppermute(x, 'tile', [(i, i ^ step * group) for i in range(tiles)])  6.4 us
    ppermute x4, starting transfers between devices, shift(): return lax.ppermute(x[-2:], 'frame', onward)  4.73 us
    pallas_call x5, Pallas kernels, staged(): pl.pallas_call(body, out_shape=outs, in_specs=[VM] * len(args), out_specs...  4.45 us
    ppermute x3, starting transfers between devices, local(): lax.ppermute(x, 'tile', [(i, i ^ step * group) for i in range(tiles)])  3.88 us
  transfers between devices with their start and end apart: 20, of which 10 were waited for; matrix products, arithmetic and copies ran while one was open for 0% of the time, Pallas kernels for 18%

profile of v4, /device:TPU:0, one launch (start us, length us, event | category | flops | bytes accessed | tf_op | source)
XLA Modules:
  0.0 57.1 jit_solution(1253209445366555301)
XLA Ops:
  0.0 1.2 %copy-done.1 = f32[4,2,160,128]{3,2,1,0:T(8,128)S(1)} copy-done((f32[4,2,160,128]{3,2,1,0:T(8,128)S(1)}, f32[4,2,160,128]{3,2,1,0:T(8,128)}, u32[]{:S(2)}) %copy-start.1) | copy-done | bytes 655384
  1.2 0.1 shard_map.100
  1.3 0.6 collective-permute-start
  1.9 3.5 %collective-permute-start.1 = (f32[2,160,128]{2,1,0:T(8,128)S(1)}, f32[2,160,128]{2,1,0:T(8,128)S(1)}, u32[]{:S(2)}, u32[]{:S(2)}) collective-permute-start(f32[2,160,128]{2,1,0:T(8,128)S(1)} %get-tuple-element.39.far_ref.refs_0_), channel_id=1, source_target_pairs={{0,28},{4,8},{8,4},{12,16},{16,12},{20,24},{24,20},{28,0},{1,29},{... | collective-permute-start | bytes 491528 | tf_op jit(solution)/shard_map/ppermute | solution.py:333
  5.5 0.1 shard_map.101.far_ref.refs_1_
  5.6 0.0 copy-start.8
  5.6 0.1 collective-permute-start.2
  5.7 0.3 shard_map.102
  5.9 0.1 shard_map.107
  6.1 0.1 copy-done.8
  6.2 0.9 %shard_map.105 = (f32[2,1,160,128]{3,2,1,0:T(8,128)S(1)}, f32[2,160,128]{2,1,0:T(8,128)S(1)}) custom-call(f32[2,160,128]{2,1,0:T(8,128)S(1)} %shard_map.101.far_ref.refs_1_, f32[2,1,160,128]{3,2,1,0:T(8,128)S(1)} %get-tuple-element.75.near_ref.refs_1_, f32[2,160,128]{2,1,0:T(8,128)S(1)} %get-tuple-element.73.partner_ref, f32[2,2,128]{2,1,0:T(2,128)S(1)} %copy-done.8, ...), custom_call_target="tpu_custom_call" | custom-call | bytes 2787328 | tf_op jit(solution)/shard_map/pallas_call | solution.py:23
  7.2 5.9 %collective-permute-done.2.beyond_ref = f32[2,160,128]{2,1,0:T(8,128)S(1)} collective-permute-done((f32[2,160,128]{2,1,0:T(8,128)S(1)}, f32[2,160,128]{2,1,0:T(8,128)S(1)}, u32[]{:S(2)}, u32[]{:S(2)}) %collective-permute-start.2) | collective-permute-done | bytes 163872 | tf_op jit(solution)/shard_map/ppermute | solution.py:333
  13.0 0.5 shard_map.106.refs_3_
  13.5 1.8 %collective-permute-start.3 = (f32[2,160,128]{2,1,0:T(8,128)S(1)}, f32[2,160,128]{2,1,0:T(8,128)S(1)}, u32[]{:S(2)}, u32[]{:S(2)}) collective-permute-start(f32[2,160,128]{2,1,0:T(8,128)S(1)} %shard_map.106.refs_3_), channel_id=1, source_target_pairs={{0,1},{1,2},{2,3},{3,0},{4,5},{5,6},{6,7},{7,4},{8,9},{9,10},{10,1... | collective-permute-start | bytes 491528 | tf_op jit(solution)/shard_map/ppermute | solution.py:336
  15.3 1.6 %collective-permute-start.4 = (f32[2,1,160,128]{3,2,1,0:T(8,128)S(1)}, f32[2,1,160,128]{3,2,1,0:T(8,128)S(1)}, u32[]{:S(2)}, u32[]{:S(2)}) collective-permute-start(f32[2,1,160,128]{3,2,1,0:T(8,128)S(1)} %get-tuple-element.50.refs_3_), channel_id=1, source_target_pairs={{0,1},{1,2},{2,3},{3,0},{4,5},{5,6},{6,7},{7,4},{8,9},{9,10},{10,1... | collective-permute-start | bytes 491528 | tf_op jit(solution)/shard_map/ppermute | solution.py:336
  16.9 0.9 %shard_map.103 = (f32[2,1,160,128]{3,2,1,0:T(8,128)S(1)}, f32[2,160,128]{2,1,0:T(8,128)S(1)}) custom-call(f32[2,160,128]{2,1,0:T(8,128)S(1)} %get-tuple-element.39.far_ref.refs_0_, f32[2,1,160,128]{3,2,1,0:T(8,128)S(1)} %get-tuple-element.76.near_ref.refs_0_, f32[2,160,128]{2,1,0:T(8,128)S(1)} %get-tuple-element.74.partner_ref, f32[2,2,128]{2,1,0:T(2,128)S(1)} %copy-done.8, ...), custom_call_target="tpu_custom_call" | custom-call | bytes 2787328 | tf_op jit(solution)/shard_map/pallas_call | solution.py:23
  17.9 0.4 shard_map.110
  18.3 0.1 collective-permute-start.7
  18.3 0.5 shard_map.104.refs_2_.u_ref
  18.9 0.4 shard_map.108
  19.3 1.8 %collective-permute-start.8 = (f32[2,160,128]{2,1,0:T(8,128)S(1)}, f32[2,160,128]{2,1,0:T(8,128)S(1)}, u32[]{:S(2)}, u32[]{:S(2)}) collective-permute-start(f32[2,160,128]{2,1,0:T(8,128)S(1)} %get-tuple-element.48.far_ref.refs_1_), channel_id=1, source_target_pairs={{0,28},{4,8},{8,4},{12,16},{16,12},{20,24},{24,20},{28,0},{1,29},{... | collective-permute-start | bytes 491528 | tf_op jit(solution)/shard_map/ppermute | solution.py:333
  21.1 0.3 shard_map.112
  21.3 4.0 %collective-permute-done.4.got_ref = f32[2,1,160,128]{3,2,1,0:T(8,128)S(1)} collective-permute-done((f32[2,1,160,128]{3,2,1,0:T(8,128)S(1)}, f32[2,1,160,128]{3,2,1,0:T(8,128)S(1)}, u32[]{:S(2)}, u32[]{:S(2)}) %collective-permute-start.4) | collective-permute-done | bytes 163872 | tf_op jit(solution)/shard_map/ppermute | solution.py:336
  25.4 0.2 shard_map.111.near_ref.refs_0_
  25.6 0.1 collective-permute-start.5
  25.7 0.2 shard_map.109.far_ref.refs_0_
  25.9 2.0 %collective-permute-start.6 = (f32[2,160,128]{2,1,0:T(8,128)S(1)}, f32[2,160,128]{2,1,0:T(8,128)S(1)}, u32[]{:S(2)}, u32[]{:S(2)}) collective-permute-start(f32[2,160,128]{2,1,0:T(8,128)S(1)} %shard_map.109.far_ref.refs_0_), channel_id=1, source_target_pairs={{0,28},{4,8},{8,4},{12,16},{16,12},{20,24},{24,20},{28,0},{1,29},{... | collective-permute-start | bytes 491528 | tf_op jit(solution)/shard_map/ppermute | solution.py:333
  27.9 0.9 %shard_map.115 = (f32[2,1,160,128]{3,2,1,0:T(8,128)S(1)}, f32[2,160,128]{2,1,0:T(8,128)S(1)}) custom-call(f32[2,160,128]{2,1,0:T(8,128)S(1)} %get-tuple-element.48.far_ref.refs_1_, f32[2,1,160,128]{3,2,1,0:T(8,128)S(1)} %get-tuple-element.56.near_ref.refs_1_, f32[2,160,128]{2,1,0:T(8,128)S(1)} %collective-permute-done.7.partner_ref, ...), custom_call_target="tpu_custom_call" | custom-call | bytes 2787328 | tf_op jit(solution)/shard_map/pallas_call | solution.py:23
  28.9 0.5 shard_map.116.refs_3_
  29.4 0.1 collective-permute-start.9
  29.5 1.3 %collective-permute-start.10 = (f32[2,1,160,128]{3,2,1,0:T(8,128)S(1)}, f32[2,1,160,128]{3,2,1,0:T(8,128)S(1)}, u32[]{:S(2)}, u32[]{:S(2)}) collective-permute-start(f32[2,1,160,128]{3,2,1,0:T(8,128)S(1)} %get-tuple-element.61.refs_3_), channel_id=1, source_target_pairs={{0,1},{1,2},{2,3},{3,0},{4,5},{5,6},{6,7},{7,4},{8,9},{9,10},{10,1... | collective-permute-start | bytes 491528 | tf_op jit(solution)/shard_map/ppermute | solution.py:336
  30.7 0.2 shard_map.121
  31.0 0.9 %shard_map.113 = (f32[2,1,160,128]{3,2,1,0:T(8,128)S(1)}, f32[2,160,128]{2,1,0:T(8,128)S(1)}) custom-call(f32[2,160,128]{2,1,0:T(8,128)S(1)} %shard_map.109.far_ref.refs_0_, f32[2,1,160,128]{3,2,1,0:T(8,128)S(1)} %shard_map.111.near_ref.refs_0_, f32[2,160,128]{2,1,0:T(8,128)S(1)} %collective-permute-done.5.partner_ref, f32[2,2,128]{2,1,0:T(2,128)S(1)} %copy-done.8, ...), custom_call_target="tpu_custom_call" | custom-call | bytes 2787328 | tf_op jit(solution)/shard_map/pallas_call | solution.py:23
  31.9 1.0 %collective-permute-done.6.beyond_ref = f32[2,160,128]{2,1,0:T(8,128)S(1)} collective-permute-done((f32[2,160,128]{2,1,0:T(8,128)S(1)}, f32[2,160,128]{2,1,0:T(8,128)S(1)}, u32[]{:S(2)}, u32[]{:S(2)}) %collective-permute-start.6) | collective-permute-done | bytes 163872 | tf_op jit(solution)/shard_map/ppermute | solution.py:333
  32.9 0.5 shard_map.114.refs_2_.u_ref
  33.5 0.4 shard_map.117
  33.9 0.4 shard_map.119
  34.3 3.4 %collective-permute-done.9.got_ref = f32[2,160,128]{2,1,0:T(8,128)S(1)} collective-permute-done((f32[2,160,128]{2,1,0:T(8,128)S(1)}, f32[2,160,128]{2,1,0:T(8,128)S(1)}, u32[]{:S(2)}, u32[]{:S(2)}) %collective-permute-start.9) | collective-permute-done | bytes 163872 | tf_op jit(solution)/shard_map/ppermute | solution.py:336
  37.7 0.2 shard_map.118.far_ref
  37.9 1.5 %collective-permute-done.10.got_ref = f32[2,1,160,128]{3,2,1,0:T(8,128)S(1)} collective-permute-done((f32[2,1,160,128]{3,2,1,0:T(8,128)S(1)}, f32[2,1,160,128]{3,2,1,0:T(8,128)S(1)}, u32[]{:S(2)}, u32[]{:S(2)}) %collective-permute-start.10) | collective-permute-done | bytes 163872 | tf_op jit(solution)/shard_map/ppermute | solution.py:336
  39.4 0.2 shard_map.120.near_ref
  39.7 0.3 shard_map.124.refs_2_
  40.0 0.1 collective-permute-start.11
  40.0 0.3 shard_map.125.refs_3_
  40.3 0.6 collective-permute-start.12
  40.9 0.4 shard_map.122.refs_0_
  41.3 0.0 copy-start.4
  41.3 0.0 copy-start.5
  41.3 0.0 copy-start.6
  41.3 0.0 copy-start.7
  41.4 0.4 shard_map.123.refs_1_
  41.8 0.0 copy-start.9
  41.8 0.1 collective-permute-done.12.refs_5_
  41.9 0.3 shard_map.126
  42.2 2.3 %collective-permute-start.14 = (f32[120,256]{1,0:T(8,128)S(1)}, f32[120,256]{1,0:T(8,128)S(1)}, u32[]{:S(2)}, u32[]{:S(2)}) collective-permute-start(f32[120,256]{1,0:T(8,128)S(1)} %get-tuple-element.68), channel_id=1, source_target_pairs={{0,8},{4,12},{8,0},{12,4},{16,24},{20,28},{24,16},{28,20},{1,9},{5... | collective-permute-start | bytes 368648 | tf_op jit(solution)/shard_map/ppermute | solution.py:469
  44.6 0.8 %collective-permute-start.16 = (f32[120,256]{1,0:T(8,128)S(1)}, f32[120,256]{1,0:T(8,128)S(1)}, u32[]{:S(2)}, u32[]{:S(2)}) collective-permute-start(f32[120,256]{1,0:T(8,128)S(1)} %get-tuple-element.69), channel_id=1, source_target_pairs={{0,16},{4,20},{8,24},{12,28},{16,0},{20,4},{24,8},{28,12},{1,17},{... | collective-permute-start | bytes 368648 | tf_op jit(solution)/shard_map/ppermute | solution.py:469
  45.4 0.8 %collective-permute-start.18 = (f32[120,256]{1,0:T(8,128)S(1)}, f32[120,256]{1,0:T(8,128)S(1)}, u32[]{:S(2)}, u32[]{:S(2)}) collective-permute-start(f32[120,256]{1,0:T(8,128)S(1)} %get-tuple-element.70), channel_id=1, source_target_pairs={{0,24},{4,28},{8,16},{12,20},{16,8},{20,12},{24,0},{28,4},{1,25},{... | collective-permute-start | bytes 368648 | tf_op jit(solution)/shard_map/ppermute | solution.py:469
  46.1 2.3 %collective-permute-done.14 = f32[120,256]{1,0:T(8,128)S(1)} collective-permute-done((f32[120,256]{1,0:T(8,128)S(1)}, f32[120,256]{1,0:T(8,128)S(1)}, u32[]{:S(2)}, u32[]{:S(2)}) %collective-permute-start.14) | collective-permute-done | bytes 122912 | tf_op jit(solution)/shard_map/ppermute | solution.py:469
  48.4 4.1 %collective-permute-done.16 = f32[120,256]{1,0:T(8,128)S(1)} collective-permute-done((f32[120,256]{1,0:T(8,128)S(1)}, f32[120,256]{1,0:T(8,128)S(1)}, u32[]{:S(2)}, u32[]{:S(2)}) %collective-permute-start.16) | collective-permute-done | bytes 122912 | tf_op jit(solution)/shard_map/ppermute | solution.py:469
  52.5 0.5 collective-permute-start.19
  53.1 0.4 shard_map.127
  53.5 0.4 collective-permute-done.17.refs_5_
  53.9 0.2 collective-permute-done.19.refs_7_
  54.0 3.1 %shard_map.128 = f32[8,40,256]{2,1,0:T(8,128)} custom-call(f32[1,120,256]{2,1,0:T(8,128)S(1)} %bitcast.15, f32[1,120,256]{2,1,0:T(8,128)S(1)} %collective-permute-done.13.refs_1_, f32[1,120,256]{2,1,0:T(8,128)S(1)} %bitcast.17, f32[1,120,256]{2,1,0:T(8,128)S(1)} %collective-permute-done.15.refs_3_, f32[1,120,256]{2,1,0:T(8,128)S(1)} %bitcast.19, ...), custom_call_target="tpu_custom_call" | custom-call | flops 1048576 | bytes 1048576 | tf_op jit(solution)/shard_map/pallas_call | solution.py:434
  (27 shorter events, 0.1 us)
Async XLA Ops:
  0.0 5.6 %copy-start = (f32[2,3,3,128,128]{4,3,2,1,0:T(8,128)S(1)}, f32[2,3,3,128,128]{4,3,2,1,0:T(8,128)}, u32[]{:S(2)}) copy-start(f32[2,3,3,128,128]{4,3,2,1,0:T(8,128)} %space_ref.3) | copy-start | bytes 3538948
  0.0 1.2 %copy-start.1 = (f32[4,2,160,128]{3,2,1,0:T(8,128)S(1)}, f32[4,2,160,128]{3,2,1,0:T(8,128)}, u32[]{:S(2)}) copy-start(f32[4,2,160,128]{3,2,1,0:T(8,128)} %video_ref.3) | copy-start | bytes 1966084
  1.2 4.7 %copy-start.3 = (f32[2,3,128,128]{3,2,1,0:T(8,128)S(1)}, f32[2,3,128,128]{3,2,1,0:T(8,128)}, u32[]{:S(2)}) copy-start(f32[2,3,128,128]{3,2,1,0:T(8,128)} %time_ref.1) | copy-start | bytes 1179652
  1.3 4.7 %collective-permute-start = (f32[4,160,128]{2,1,0:T(8,128)S(1)}, f32[4,160,128]{2,1,0:T(8,128)S(1)}, u32[]{:S(2)}, u32[]{:S(2)}) collective-permute-start(f32[4,160,128]{2,1,0:T(8,128)S(1)} %get-tuple-element.40), channel_id=1, source_target_pairs={{0,4},{4,0},{8,12},{12,8},{16,20},{20,16},{24,28},{28,24},{1,5},{5... | collective-permute-start | bytes 983048 | tf_op jit(solution)/shard_map/ppermute | solution.py:330
  1.9 16.4 %collective-permute-start.1 = (f32[2,160,128]{2,1,0:T(8,128)S(1)}, f32[2,160,128]{2,1,0:T(8,128)S(1)}, u32[]{:S(2)}, u32[]{:S(2)}) collective-permute-start(f32[2,160,128]{2,1,0:T(8,128)S(1)} %get-tuple-element.39.far_ref.refs_0_), channel_id=1, source_target_pairs={{0,28},{4,8},{8,4},{12,16},{16,12},{20,24},{24,20},{28,0},{1,29},{... | collective-permute-start | bytes 491528 | tf_op jit(solution)/shard_map/ppermute | solution.py:333
  5.6 0.7 %copy-start.8 = (f32[2,2,128]{2,1,0:T(2,128)S(1)}, f32[2,2,128]{2,1,0:T(2,128)}, u32[]{:S(2)}) copy-start(f32[2,2,128]{2,1,0:T(2,128)} %gain_ref.15) | copy-start | bytes 6148
  5.6 7.5 %collective-permute-start.2 = (f32[2,160,128]{2,1,0:T(8,128)S(1)}, f32[2,160,128]{2,1,0:T(8,128)S(1)}, u32[]{:S(2)}, u32[]{:S(2)}) collective-permute-start(f32[2,160,128]{2,1,0:T(8,128)S(1)} %shard_map.101.far_ref.refs_1_), channel_id=1, source_target_pairs={{0,28},{4,8},{8,4},{12,16},{16,12},{20,24},{24,20},{28,0},{1,29},{... | collective-permute-start | bytes 491528 | tf_op jit(solution)/shard_map/ppermute | solution.py:333
  13.5 12.1 %collective-permute-start.3 = (f32[2,160,128]{2,1,0:T(8,128)S(1)}, f32[2,160,128]{2,1,0:T(8,128)S(1)}, u32[]{:S(2)}, u32[]{:S(2)}) collective-permute-start(f32[2,160,128]{2,1,0:T(8,128)S(1)} %shard_map.106.refs_3_), channel_id=1, source_target_pairs={{0,1},{1,2},{2,3},{3,0},{4,5},{5,6},{6,7},{7,4},{8,9},{9,10},{10,1... | collective-permute-start | bytes 491528 | tf_op jit(solution)/shard_map/ppermute | solution.py:336
  15.3 10.0 %collective-permute-start.4 = (f32[2,1,160,128]{3,2,1,0:T(8,128)S(1)}, f32[2,1,160,128]{3,2,1,0:T(8,128)S(1)}, u32[]{:S(2)}, u32[]{:S(2)}) collective-permute-start(f32[2,1,160,128]{3,2,1,0:T(8,128)S(1)} %get-tuple-element.50.refs_3_), channel_id=1, source_target_pairs={{0,1},{1,2},{2,3},{3,0},{4,5},{5,6},{6,7},{7,4},{8,9},{9,10},{10,1... | collective-permute-start | bytes 491528 | tf_op jit(solution)/shard_map/ppermute | solution.py:336
  18.3 9.7 %collective-permute-start.7 = (f32[2,160,128]{2,1,0:T(8,128)S(1)}, f32[2,160,128]{2,1,0:T(8,128)S(1)}, u32[]{:S(2)}, u32[]{:S(2)}) collective-permute-start(f32[2,160,128]{2,1,0:T(8,128)S(1)} %bitcast.13), channel_id=1, source_target_pairs={{0,4},{4,0},{8,12},{12,8},{16,20},{20,16},{24,28},{28,24},{1,5},{5... | collective-permute-start | bytes 491528 | tf_op jit(solution)/shard_map/ppermute | solution.py:330
  19.3 9.6 %collective-permute-start.8 = (f32[2,160,128]{2,1,0:T(8,128)S(1)}, f32[2,160,128]{2,1,0:T(8,128)S(1)}, u32[]{:S(2)}, u32[]{:S(2)}) collective-permute-start(f32[2,160,128]{2,1,0:T(8,128)S(1)} %get-tuple-element.48.far_ref.refs_1_), channel_id=1, source_target_pairs={{0,28},{4,8},{8,4},{12,16},{16,12},{20,24},{24,20},{28,0},{1,29},{... | collective-permute-start | bytes 491528 | tf_op jit(solution)/shard_map/ppermute | solution.py:333
  25.6 5.4 %collective-permute-start.5 = (f32[2,160,128]{2,1,0:T(8,128)S(1)}, f32[2,160,128]{2,1,0:T(8,128)S(1)}, u32[]{:S(2)}, u32[]{:S(2)}) collective-permute-start(f32[2,160,128]{2,1,0:T(8,128)S(1)} %bitcast.12), channel_id=1, source_target_pairs={{0,4},{4,0},{8,12},{12,8},{16,20},{20,16},{24,28},{28,24},{1,5},{5... | collective-permute-start | bytes 491528 | tf_op jit(solution)/shard_map/ppermute | solution.py:330
  25.9 7.0 %collective-permute-start.6 = (f32[2,160,128]{2,1,0:T(8,128)S(1)}, f32[2,160,128]{2,1,0:T(8,128)S(1)}, u32[]{:S(2)}, u32[]{:S(2)}) collective-permute-start(f32[2,160,128]{2,1,0:T(8,128)S(1)} %shard_map.109.far_ref.refs_0_), channel_id=1, source_target_pairs={{0,28},{4,8},{8,4},{12,16},{16,12},{20,24},{24,20},{28,0},{1,29},{... | collective-permute-start | bytes 491528 | tf_op jit(solution)/shard_map/ppermute | solution.py:333
  27.9 2.8 %copy-start.2 = (f32[3,3,128,256]{3,2,1,0:T(8,128)S(1)}, f32[3,3,128,256]{3,2,1,0:T(8,128)}, u32[]{:S(2)}) copy-start(f32[3,3,128,256]{3,2,1,0:T(8,128)} %down_ref.1) | copy-start | bytes 3538948
  29.4 8.3 %collective-permute-start.9 = (f32[2,160,128]{2,1,0:T(8,128)S(1)}, f32[2,160,128]{2,1,0:T(8,128)S(1)}, u32[]{:S(2)}, u32[]{:S(2)}) collective-permute-start(f32[2,160,128]{2,1,0:T(8,128)S(1)} %shard_map.116.refs_3_), channel_id=1, source_target_pairs={{0,1},{1,2},{2,3},{3,0},{4,5},{5,6},{6,7},{7,4},{8,9},{9,10},{10,1... | collective-permute-start | bytes 491528 | tf_op jit(solution)/shard_map/ppermute | solution.py:336
  29.5 10.0 %collective-permute-start.10 = (f32[2,1,160,128]{3,2,1,0:T(8,128)S(1)}, f32[2,1,160,128]{3,2,1,0:T(8,128)S(1)}, u32[]{:S(2)}, u32[]{:S(2)}) collective-permute-start(f32[2,1,160,128]{3,2,1,0:T(8,128)S(1)} %get-tuple-element.61.refs_3_), channel_id=1, source_target_pairs={{0,1},{1,2},{2,3},{3,0},{4,5},{5,6},{6,7},{7,4},{8,9},{9,10},{10,1... | collective-permute-start | bytes 491528 | tf_op jit(solution)/shard_map/ppermute | solution.py:336
  40.0 1.8 %collective-permute-start.11 = (f32[2,80,256]{2,1,0:T(8,128)S(1)}, f32[2,80,256]{2,1,0:T(8,128)S(1)}, u32[]{:S(2)}, u32[]{:S(2)}) collective-permute-start(f32[2,80,256]{2,1,0:T(8,128)S(1)} %shard_map.124.refs_2_), channel_id=1, source_target_pairs={{0,4},{4,0},{8,12},{12,8},{16,20},{20,16},{24,28},{28,24},{1,5},{5... | collective-permute-start | bytes 491528 | tf_op jit(solution)/shard_map/ppermute | solution.py:330
  40.3 1.6 %collective-permute-start.12 = (f32[2,80,256]{2,1,0:T(8,128)S(1)}, f32[2,80,256]{2,1,0:T(8,128)S(1)}, u32[]{:S(2)}, u32[]{:S(2)}) collective-permute-start(f32[2,80,256]{2,1,0:T(8,128)S(1)} %shard_map.125.refs_3_), channel_id=1, source_target_pairs={{0,4},{4,0},{8,12},{12,8},{16,20},{20,16},{24,28},{28,24},{1,5},{5... | collective-permute-start | bytes 491528 | tf_op jit(solution)/shard_map/ppermute | solution.py:330
  41.3 11.7 %copy-start.4 = (f32[256,256]{1,0:T(8,128)S(1)}, f32[256,256]{1,0:T(8,128)}, u32[]{:S(2)}) copy-start(f32[256,256]{1,0:T(8,128)} %q_ref.1) | copy-start | bytes 786436
  41.3 11.7 %copy-start.5 = (f32[256,256]{1,0:T(8,128)S(1)}, f32[256,256]{1,0:T(8,128)}, u32[]{:S(2)}) copy-start(f32[256,256]{1,0:T(8,128)} %k_ref.1) | copy-start | bytes 786436
  41.3 11.7 %copy-start.6 = (f32[256,256]{1,0:T(8,128)S(1)}, f32[256,256]{1,0:T(8,128)}, u32[]{:S(2)}) copy-start(f32[256,256]{1,0:T(8,128)} %v_ref.1) | copy-start | bytes 786436
  41.3 11.7 %copy-start.7 = (f32[256,256]{1,0:T(8,128)S(1)}, f32[256,256]{1,0:T(8,128)}, u32[]{:S(2)}) copy-start(f32[256,256]{1,0:T(8,128)} %o_ref.1) | copy-start | bytes 786436
  41.8 12.3 %copy-start.9 = (f32[256]{0:T(256)S(1)}, f32[256]{0:T(256)}, u32[]{:S(2)}) copy-start(f32[256]{0:T(256)} %param.15) | copy-start | bytes 3076
  42.2 6.2 %collective-permute-start.14 = (f32[120,256]{1,0:T(8,128)S(1)}, f32[120,256]{1,0:T(8,128)S(1)}, u32[]{:S(2)}, u32[]{:S(2)}) collective-permute-start(f32[120,256]{1,0:T(8,128)S(1)} %get-tuple-element.68), channel_id=1, source_target_pairs={{0,8},{4,12},{8,0},{12,4},{16,24},{20,28},{24,16},{28,20},{1,9},{5... | collective-permute-start | bytes 368648 | tf_op jit(solution)/shard_map/ppermute | solution.py:469
  44.6 7.9 %collective-permute-start.16 = (f32[120,256]{1,0:T(8,128)S(1)}, f32[120,256]{1,0:T(8,128)S(1)}, u32[]{:S(2)}, u32[]{:S(2)}) collective-permute-start(f32[120,256]{1,0:T(8,128)S(1)} %get-tuple-element.69), channel_id=1, source_target_pairs={{0,16},{4,20},{8,24},{12,28},{16,0},{20,4},{24,8},{28,12},{1,17},{... | collective-permute-start | bytes 368648 | tf_op jit(solution)/shard_map/ppermute | solution.py:469
  45.4 7.2 %collective-permute-start.18 = (f32[120,256]{1,0:T(8,128)S(1)}, f32[120,256]{1,0:T(8,128)S(1)}, u32[]{:S(2)}, u32[]{:S(2)}) collective-permute-start(f32[120,256]{1,0:T(8,128)S(1)} %get-tuple-element.70), channel_id=1, source_target_pairs={{0,24},{4,28},{8,16},{12,20},{16,8},{20,12},{24,0},{28,4},{1,25},{... | collective-permute-start | bytes 368648 | tf_op jit(solution)/shard_map/ppermute | solution.py:469
  46.1 7.4 %collective-permute-start.13 = (f32[1,120,256]{2,1,0:T(8,128)S(1)}, f32[1,120,256]{2,1,0:T(8,128)S(1)}, u32[]{:S(2)}, u32[]{:S(2)}) collective-permute-start(f32[1,120,256]{2,1,0:T(8,128)S(1)} %bitcast.14), channel_id=1, source_target_pairs={{0,4},{4,0},{8,12},{12,8},{16,20},{20,16},{24,28},{28,24},{1,5},{5... | collective-permute-start | bytes 368648 | tf_op jit(solution)/shard_map/ppermute | solution.py:475
  48.4 5.1 %collective-permute-start.15 = (f32[1,120,256]{2,1,0:T(8,128)S(1)}, f32[1,120,256]{2,1,0:T(8,128)S(1)}, u32[]{:S(2)}, u32[]{:S(2)}) collective-permute-start(f32[1,120,256]{2,1,0:T(8,128)S(1)} %bitcast.16), channel_id=1, source_target_pairs={{0,4},{4,0},{8,12},{12,8},{16,20},{20,16},{24,28},{28,24},{1,5},{5... | collective-permute-start | bytes 368648 | tf_op jit(solution)/shard_map/ppermute | solution.py:475
  52.5 1.3 %collective-permute-start.17 = (f32[1,120,256]{2,1,0:T(8,128)S(1)}, f32[1,120,256]{2,1,0:T(8,128)S(1)}, u32[]{:S(2)}, u32[]{:S(2)}) collective-permute-start(f32[1,120,256]{2,1,0:T(8,128)S(1)} %bitcast.18), channel_id=1, source_target_pairs={{0,4},{4,0},{8,12},{12,8},{16,20},{20,16},{24,28},{28,24},{1,5},{5... | collective-permute-start | bytes 368648 | tf_op jit(solution)/shard_map/ppermute | solution.py:475
  52.5 1.5 %collective-permute-start.19 = (f32[1,120,256]{2,1,0:T(8,128)S(1)}, f32[1,120,256]{2,1,0:T(8,128)S(1)}, u32[]{:S(2)}, u32[]{:S(2)}) collective-permute-start(f32[1,120,256]{2,1,0:T(8,128)S(1)} %bitcast.20), channel_id=1, source_target_pairs={{0,4},{4,0},{8,12},{12,8},{16,20},{20,16},{24,28},{28,24},{1,5},{5... | collective-permute-start | bytes 368648 | tf_op jit(solution)/shard_map/ppermute | solution.py:475

commit v5 on v4

--- a/solution.py
+++ b/solution.py
@@ -92,8 +92,12 @@
 def pack_time(time_ref, *out_refs):
     c = time_ref.shape[-1]
     for block, out_ref in enumerate(out_refs):
-        for k in range(3):
-            out_ref[:, (2 - k) * c : (3 - k) * c] = right_side(time_ref[block, k])
+        sides = [right_side(time_ref[block, k]) for k in range(3)]
+        for frame in range(4):
+            for to in range(2):
+                k = frame - to
+                side = sides[k] if 0 <= k < 3 else jnp.zeros_like(sides[0])
+                out_ref[frame * 3 * c : (frame + 1) * 3 * c, to * c : (to + 1) * c] = side
 
 
 def pack_down(down_ref, own_ref, next_ref):
@@ -158,28 +162,30 @@
     places = [(g, f) for g in range(groups) for f in range(x_refs[g].shape[0])]
     c = x_refs[0].shape[-1]
     shape = x_refs[0].shape[1:]
-    total = [x_refs[g][f].reshape(-1, c) for g, f in places]
-    for at, (g, f) in enumerate(places):
-        left = left_side(u_refs[g][f].reshape(-1, c))
-        wide = min(3, len(places) - at)
-        product = mul(left, weight_ref[:, : wide * c])
-        for k in range(wide):
-            total[at + k] = total[at + k] + product[:, k * c : (k + 1) * c]
-    for at, (g, f) in enumerate(places):
-        out_refs[g][f] = total[at].reshape(shape)
-
-
-def mix_earlier(x_ref, u_ref, got_ref, weight_ref, out_ref):
+    left = [left_side(u_refs[g][f].reshape(-1, c)) for g, f in places]
+    for at in range(0, len(places), 2):
+        first = max(at - 2, 0)
+        rows = slice((first - at + 2) * 3 * c, 12 * c)
+        both = mul(jnp.concatenate(left[first : at + 2], -1), weight_ref[rows])
+        for to in range(2):
+            g, f = places[at + to]
+            out_refs[g][f] = x_refs[g][f] + both[:, to * c : (to + 1) * c].reshape(shape)
+
+
+def mix_earlier(x_ref, u_ref, *refs):
     c = x_ref.shape[-1]
     shape = x_ref.shape[1:]
-    opening = lax.axis_index("frame") == 0
-    first = u_ref[0].reshape(-1, c)
-    before = jnp.where(opening, first, got_ref[0].reshape(-1, c))
-    last = jnp.where(opening, first, got_ref[1].reshape(-1, c))
-    near = mul(left_side(last), weight_ref[:, c:])
-    far = mul(left_side(before), weight_ref[:, 2 * c :])
-    out_ref[0] = x_ref[0] + (near[:, :c] + far).reshape(shape)
-    out_ref[1] = x_ref[1] + near[:, c:].reshape(shape)
+    *got_refs, weight_ref, out_ref = refs
+    frame = lax.axis_index("frame")
+    left = []
+    for f in range(2):
+        values = got_refs[-1][f]
+        if len(got_refs) > 1:
+            values = jnp.where(lax.rem(frame, 2) == 1, got_refs[0][f], values)
+        left.append(left_side(jnp.where(frame == 0, u_ref[0], values).reshape(-1, c)))
+    both = mul(jnp.concatenate(left, -1), weight_ref[: 6 * c])
+    for f in range(2):
+        out_ref[f] = x_ref[f] + both[:, f * c : (f + 1) * c].reshape(shape)
 
 
 def pixels(ref, n, w):
@@ -263,10 +269,11 @@
         device = tile ^ m
         odd = lax.rem(device, 2)
         added = jnp.where(odd == 0, next_ref[device - odd], 0.0)
-        z_ref[m, :w] = ref[i, :w] + added
+        z = ref[i, :w] + added
         if size > w:
-            z_ref[m, w:] = ref[i, w:size]
-        high, low = halves(norm(z_ref[m], gain))
+            z = jnp.concatenate([z, ref[i, w:size]], 0)
+        z_ref[m] = z
+        high, low = halves(norm(z, gain))
         tokens = slice(m * size, (m + 1) * size)
         k_ref[tokens, :d] = high
         k_ref[tokens, d : 2 * d] = high
@@ -317,10 +324,11 @@
     tiles, spans = lax.axis_size("tile"), lax.axis_size("frame")
     even = lax.rem(lax.axis_index("tile"), 2) == 0
     outer = down_weight.shape[-1]
-    if n == 3:
-        raise ValueError("three frames")
+    if n % 2:
+        raise ValueError("odd frames")
     pairs = [(i, i ^ 1) for i in range(tiles)]
     across = [(i, (i + 1 if i % 2 else i - 1) % tiles) for i in range(tiles)]
+    split = ('far1',)
     onward = [(i, (i + 1) % spans) for i in range(spans)]
     early, late = slice(0, 2), slice(2, n)
     ranges = [early, late] if n > 2 else [early]
@@ -332,8 +340,17 @@
     def cross(x):
         return lax.ppermute(x, "tile", across)
 
-    def shift(x):
-        return lax.ppermute(x[-2:], "frame", onward)
+    def shift(x, tag):
+        x = x[-2:]
+        if tag not in split:
+            return [lax.ppermute(x, "frame", onward)]
+        by_pair = lax.ppermute(x, "frame", [(i, i ^ 1) for i in range(spans)])
+        places = []
+        for i in range(spans):
+            ends = i in (0, spans - 1)
+            to = i if ends else (i + 1 if i % 2 else i - 1)
+            places += [(t * spans + i, (t ^ ends) * spans + to) for t in range(tiles)]
+        return [by_pair, lax.ppermute(x, ("tile", "frame"), places)]
 
     far, near, beyond = [None] * groups, [None] * groups, [None] * groups
 
@@ -374,7 +391,7 @@
 
     wide = [((18 * c, 2 * c), BF16), ((6 * c, 2 * c), BF16), ((6 * c, 2 * c), BF16)]
     space = [call(functools.partial(pack_space, j), wide, space_weight) for j in range(2)]
-    times = call(pack_time, [((3 * c, 3 * c), BF16)] * 2, time_weight)
+    times = call(pack_time, [((12 * c, 2 * c), BF16)] * 2, time_weight)
     down = call(pack_down, [((18 * c, outer), BF16), ((9 * c, outer), BF16)], down_weight)
     attention = call(pack_attn, [((3 * outer, outer), BF16)] * 2, w_query, w_key, w_value, w_out)
 
@@ -401,7 +418,7 @@
         return call(body, [(a.shape, F32) for a in x], *x, *u, times[block])
 
     def mix_in(block, x, u, got):
-        return call(mix_earlier, [(x.shape, F32)], x, u, got, times[block])[0]
+        return call(mix_earlier, [(x.shape, F32)], x, u, *got, times[block])[0]
 
     last = groups - 1
     for block in range(2):
@@ -409,13 +426,13 @@
         for g in reversed(range(groups)):
             u_near[g], part[g] = near_conv(block, far[g], near[g], partner[g])
             if g == last:
-                got_near = shift(u_near[g])
+                got_near = shift(u_near[g], f"near{block}")
         near = list(mix(block, near, u_near))
         u_far = [None] * groups
         for g in reversed(range(groups)):
             u_far[g] = far_conv(block, part[g], beyond[g])
             if g == last:
-                got_far = shift(u_far[g])
+                got_far = shift(u_far[g], f"far{block}")
         far = list(mix(block, far, u_far))
         if block == 0:
             partner, beyond = [None] * groups, [None] * groups

time: 57.3 us -> 55.6 us (0.970)
  waiting for transfers between devices: 22.9 us -> 21.4 us
    ppermute x4 -> x5, waiting for transfers between devices: 8.96 us -> 7.34 us  [the longest x3 7.13 us: shift(): return [lax.ppermute(x, 'frame', onward)]]
    ppermute x4 -> x5, starting transfers between devices: 4.73 us -> 4.79 us  [the longest x3 3.45 us: shift(): return [lax.ppermute(x, 'frame', onward)]]
  transfers between devices with their start and end apart: 20 -> 21, of which waited for: 10 -> 10; matrix products, arithmetic and copies ran while one was open for 0% -> 0% of each run, Pallas kernels for 18% -> 19%
where the time goes in v5:
time: 55.6 us; the launch traced here: 55.4 us
  waiting for transfers between devices  21.4 us (38%)
  starting transfers between devices  18 us (32%)
  Pallas kernels  14.4 us (26%)
  local copies, waits for them, and re-layouts  1.3 us (2%)
    pallas_call x22, Pallas kernels, called(): pl.pallas_call(body, out_shape=outs, in_specs=[VM] * len(args), out_specs...  9.7 us
    ppermute x4, starting transfers between devices, cross(): return lax.ppermute(x, 'tile', across)  7.46 us
    ppermute x3, waiting for transfers between devices, shift(): return [lax.ppermute(x, 'frame', onward)]  7.13 us
    ppermute x4, waiting for transfers between devices, cross(): return lax.ppermute(x, 'tile', across)  6.88 us
    ppermute x3, waiting for transfers between devices, local(): lax.ppermute(x, 'tile', [(i, i ^ step * group) for i in range(tiles)])  6.4 us
    pallas_call x5, Pallas kernels, staged(): pl.pallas_call(body, out_shape=outs, in_specs=[VM] * len(args), out_specs...  4.42 us
    ppermute x3, starting transfers between devices, local(): lax.ppermute(x, 'tile', [(i, i ^ step * group) for i in range(tiles)])  3.88 us
    ppermute x3, starting transfers between devices, shift(): return [lax.ppermute(x, 'frame', onward)]  3.45 us
  transfers between devices with their start and end apart: 21, of which 10 were waited for; matrix products, arithmetic and copies ran while one was open for 0% of the time, Pallas kernels for 19%

profile of v5, /device:TPU:0, one launch (start us, length us, event | category | flops | bytes accessed | tf_op | source)
XLA Modules:
  0.0 55.4 jit_solution(9370062459393804666)
XLA Ops:
  0.0 1.2 %copy-done.1 = f32[4,2,160,128]{3,2,1,0:T(8,128)S(1)} copy-done((f32[4,2,160,128]{3,2,1,0:T(8,128)S(1)}, f32[4,2,160,128]{3,2,1,0:T(8,128)}, u32[]{:S(2)}) %copy-start.1) | copy-done | bytes 655384
  1.2 0.1 shard_map.100
  1.3 0.6 %collective-permute-start = (f32[4,160,128]{2,1,0:T(8,128)S(1)}, f32[4,160,128]{2,1,0:T(8,128)S(1)}, u32[]{:S(2)}, u32[]{:S(2)}) collective-permute-start(f32[4,160,128]{2,1,0:T(8,128)S(1)} %get-tuple-element.40), channel_id=1, source_target_pairs={{0,4},{4,0},{8,12},{12,8},{16,20},{20,16},{24,28},{28,24},{1,5},{5... | collective-permute-start | bytes 983048 | tf_op jit(solution)/shard_map/ppermute | solution.py:338
  1.9 3.5 %collective-permute-start.1 = (f32[2,160,128]{2,1,0:T(8,128)S(1)}, f32[2,160,128]{2,1,0:T(8,128)S(1)}, u32[]{:S(2)}, u32[]{:S(2)}) collective-permute-start(f32[2,160,128]{2,1,0:T(8,128)S(1)} %get-tuple-element.39.far_ref.refs_0_), channel_id=1, source_target_pairs={{0,28},{4,8},{8,4},{12,16},{16,12},{20,24},{24,20},{28,0},{1,29},{... | collective-permute-start | bytes 491528 | tf_op jit(solution)/shard_map/ppermute | solution.py:341
  5.5 0.1 shard_map.101.far_ref.refs_1_
  5.6 0.0 copy-start.8
  5.6 0.1 collective-permute-start.2
  5.7 0.3 shard_map.102
  5.9 0.2 shard_map.107
  6.2 0.0 copy-done.8
  6.2 0.9 %shard_map.105 = (f32[2,1,160,128]{3,2,1,0:T(8,128)S(1)}, f32[2,160,128]{2,1,0:T(8,128)S(1)}) custom-call(f32[2,160,128]{2,1,0:T(8,128)S(1)} %shard_map.101.far_ref.refs_1_, f32[2,1,160,128]{3,2,1,0:T(8,128)S(1)} %get-tuple-element.75.near_ref.refs_1_, f32[2,160,128]{2,1,0:T(8,128)S(1)} %get-tuple-element.73.partner_ref, f32[2,2,128]{2,1,0:T(2,128)S(1)} %copy-done.8, ...), custom_call_target="tpu_custom_call" | custom-call | bytes 2787328 | tf_op jit(solution)/shard_map/pallas_call | solution.py:23
  7.2 5.9 %collective-permute-done.2.beyond_ref = f32[2,160,128]{2,1,0:T(8,128)S(1)} collective-permute-done((f32[2,160,128]{2,1,0:T(8,128)S(1)}, f32[2,160,128]{2,1,0:T(8,128)S(1)}, u32[]{:S(2)}, u32[]{:S(2)}) %collective-permute-start.2) | collective-permute-done | bytes 163872 | tf_op jit(solution)/shard_map/ppermute | solution.py:341
  13.0 0.5 shard_map.106.refs_3_
  13.5 1.8 %collective-permute-start.3 = (f32[2,160,128]{2,1,0:T(8,128)S(1)}, f32[2,160,128]{2,1,0:T(8,128)S(1)}, u32[]{:S(2)}, u32[]{:S(2)}) collective-permute-start(f32[2,160,128]{2,1,0:T(8,128)S(1)} %shard_map.106.refs_3_), channel_id=1, source_target_pairs={{0,1},{1,2},{2,3},{3,0},{4,5},{5,6},{6,7},{7,4},{8,9},{9,10},{10,1... | collective-permute-start | bytes 491528 | tf_op jit(solution)/shard_map/ppermute | solution.py:346
  15.3 1.6 %collective-permute-start.4 = (f32[2,1,160,128]{3,2,1,0:T(8,128)S(1)}, f32[2,1,160,128]{3,2,1,0:T(8,128)S(1)}, u32[]{:S(2)}, u32[]{:S(2)}) collective-permute-start(f32[2,1,160,128]{3,2,1,0:T(8,128)S(1)} %get-tuple-element.50.refs_3_), channel_id=1, source_target_pairs={{0,1},{1,2},{2,3},{3,0},{4,5},{5,6},{6,7},{7,4},{8,9},{9,10},{10,1... | collective-permute-start | bytes 491528 | tf_op jit(solution)/shard_map/ppermute | solution.py:346
  16.9 0.9 %shard_map.103 = (f32[2,1,160,128]{3,2,1,0:T(8,128)S(1)}, f32[2,160,128]{2,1,0:T(8,128)S(1)}) custom-call(f32[2,160,128]{2,1,0:T(8,128)S(1)} %get-tuple-element.39.far_ref.refs_0_, f32[2,1,160,128]{3,2,1,0:T(8,128)S(1)} %get-tuple-element.76.near_ref.refs_0_, f32[2,160,128]{2,1,0:T(8,128)S(1)} %get-tuple-element.74.partner_ref, f32[2,2,128]{2,1,0:T(2,128)S(1)} %copy-done.8, ...), custom_call_target="tpu_custom_call" | custom-call | bytes 2787328 | tf_op jit(solution)/shard_map/pallas_call | solution.py:23
  17.8 0.4 shard_map.110
  18.2 0.1 collective-permute-start.7
  18.3 0.5 shard_map.104.refs_2_.u_ref
  18.8 0.4 shard_map.108
  19.2 1.8 %collective-permute-start.8 = (f32[2,160,128]{2,1,0:T(8,128)S(1)}, f32[2,160,128]{2,1,0:T(8,128)S(1)}, u32[]{:S(2)}, u32[]{:S(2)}) collective-permute-start(f32[2,160,128]{2,1,0:T(8,128)S(1)} %get-tuple-element.48.far_ref.refs_1_), channel_id=1, source_target_pairs={{0,28},{4,8},{8,4},{12,16},{16,12},{20,24},{24,20},{28,0},{1,29},{... | collective-permute-start | bytes 491528 | tf_op jit(solution)/shard_map/ppermute | solution.py:341
  21.0 0.3 shard_map.112
  21.3 4.1 %collective-permute-done.4.refs_0_ = f32[2,1,160,128]{3,2,1,0:T(8,128)S(1)} collective-permute-done((f32[2,1,160,128]{3,2,1,0:T(8,128)S(1)}, f32[2,1,160,128]{3,2,1,0:T(8,128)S(1)}, u32[]{:S(2)}, u32[]{:S(2)}) %collective-permute-start.4) | collective-permute-done | bytes 163872 | tf_op jit(solution)/shard_map/ppermute | solution.py:346
  25.4 0.2 shard_map.111.near_ref.refs_0_
  25.6 0.1 collective-permute-start.5
  25.7 0.2 shard_map.109.far_ref.refs_0_
  25.9 2.0 %collective-permute-start.6 = (f32[2,160,128]{2,1,0:T(8,128)S(1)}, f32[2,160,128]{2,1,0:T(8,128)S(1)}, u32[]{:S(2)}, u32[]{:S(2)}) collective-permute-start(f32[2,160,128]{2,1,0:T(8,128)S(1)} %shard_map.109.far_ref.refs_0_), channel_id=1, source_target_pairs={{0,28},{4,8},{8,4},{12,16},{16,12},{20,24},{24,20},{28,0},{1,29},{... | collective-permute-start | bytes 491528 | tf_op jit(solution)/shard_map/ppermute | solution.py:341
  28.0 0.9 %shard_map.115 = (f32[2,1,160,128]{3,2,1,0:T(8,128)S(1)}, f32[2,160,128]{2,1,0:T(8,128)S(1)}) custom-call(f32[2,160,128]{2,1,0:T(8,128)S(1)} %get-tuple-element.48.far_ref.refs_1_, f32[2,1,160,128]{3,2,1,0:T(8,128)S(1)} %get-tuple-element.56.near_ref.refs_1_, f32[2,160,128]{2,1,0:T(8,128)S(1)} %collective-permute-done.7.partner_ref, ...), custom_call_target="tpu_custom_call" | custom-call | bytes 2787328 | tf_op jit(solution)/shard_map/pallas_call | solution.py:23
  28.9 0.1 collective-permute-start.11
  28.9 0.5 shard_map.116.refs_3_
  29.4 1.3 %collective-permute-start.9 = (f32[2,160,128]{2,1,0:T(8,128)S(1)}, f32[2,160,128]{2,1,0:T(8,128)S(1)}, u32[]{:S(2)}, u32[]{:S(2)}) collective-permute-start(f32[2,160,128]{2,1,0:T(8,128)S(1)} %shard_map.116.refs_3_), channel_id=1, source_target_pairs={{0,1},{1,0},{2,3},{3,2},{4,5},{5,4},{6,7},{7,6},{8,9},{9,8},{10,11... | collective-permute-start | bytes 491528 | tf_op jit(solution)/shard_map/ppermute | solution.py:347
  30.8 0.2 shard_map.121
  31.0 0.9 %shard_map.113 = (f32[2,1,160,128]{3,2,1,0:T(8,128)S(1)}, f32[2,160,128]{2,1,0:T(8,128)S(1)}) custom-call(f32[2,160,128]{2,1,0:T(8,128)S(1)} %shard_map.109.far_ref.refs_0_, f32[2,1,160,128]{3,2,1,0:T(8,128)S(1)} %shard_map.111.near_ref.refs_0_, f32[2,160,128]{2,1,0:T(8,128)S(1)} %collective-permute-done.5.partner_ref, f32[2,2,128]{2,1,0:T(2,128)S(1)} %copy-done.8, ...), custom_call_target="tpu_custom_call" | custom-call | bytes 2787328 | tf_op jit(solution)/shard_map/pallas_call | solution.py:23
  32.0 1.0 %collective-permute-done.6.beyond_ref = f32[2,160,128]{2,1,0:T(8,128)S(1)} collective-permute-done((f32[2,160,128]{2,1,0:T(8,128)S(1)}, f32[2,160,128]{2,1,0:T(8,128)S(1)}, u32[]{:S(2)}, u32[]{:S(2)}) %collective-permute-start.6) | collective-permute-done | bytes 163872 | tf_op jit(solution)/shard_map/ppermute | solution.py:341
  33.0 0.5 shard_map.114.refs_2_.u_ref
  33.5 0.4 shard_map.117
  33.8 0.4 shard_map.119
  34.2 3.0 %collective-permute-done.11.refs_0_ = f32[2,1,160,128]{3,2,1,0:T(8,128)S(1)} collective-permute-done((f32[2,1,160,128]{3,2,1,0:T(8,128)S(1)}, f32[2,1,160,128]{3,2,1,0:T(8,128)S(1)}, u32[]{:S(2)}, u32[]{:S(2)}) %collective-permute-start.11) | collective-permute-done | bytes 163872 | tf_op jit(solution)/shard_map/ppermute | solution.py:346
  37.2 0.2 shard_map.120.near_ref
  37.5 0.2 collective-permute-done.9.refs_0_
  37.7 0.2 shard_map.118.far_ref
  37.9 0.3 shard_map.124.refs_2_
  38.2 0.1 collective-permute-start.12
  38.3 0.3 shard_map.125.refs_3_
  38.6 0.6 collective-permute-start.13
  39.2 0.4 shard_map.122.refs_0_
  39.6 0.0 copy-start.4
  39.6 0.0 copy-start.5
  39.6 0.0 copy-start.6
  39.6 0.0 copy-start.7
  39.6 0.4 shard_map.123.refs_1_
  40.0 0.0 copy-start.9
  40.0 0.2 collective-permute-done.13.refs_5_
  40.2 0.3 shard_map.126
  40.5 2.3 %collective-permute-start.15 = (f32[120,256]{1,0:T(8,128)S(1)}, f32[120,256]{1,0:T(8,128)S(1)}, u32[]{:S(2)}, u32[]{:S(2)}) collective-permute-start(f32[120,256]{1,0:T(8,128)S(1)} %get-tuple-element.68), channel_id=1, source_target_pairs={{0,8},{4,12},{8,0},{12,4},{16,24},{20,28},{24,16},{28,20},{1,9},{5... | collective-permute-start | bytes 368648 | tf_op jit(solution)/shard_map/ppermute | solution.py:486
  42.8 0.8 %collective-permute-start.17 = (f32[120,256]{1,0:T(8,128)S(1)}, f32[120,256]{1,0:T(8,128)S(1)}, u32[]{:S(2)}, u32[]{:S(2)}) collective-permute-start(f32[120,256]{1,0:T(8,128)S(1)} %get-tuple-element.69), channel_id=1, source_target_pairs={{0,16},{4,20},{8,24},{12,28},{16,0},{20,4},{24,8},{28,12},{1,17},{... | collective-permute-start | bytes 368648 | tf_op jit(solution)/shard_map/ppermute | solution.py:486
  43.6 0.7 %collective-permute-start.19 = (f32[120,256]{1,0:T(8,128)S(1)}, f32[120,256]{1,0:T(8,128)S(1)}, u32[]{:S(2)}, u32[]{:S(2)}) collective-permute-start(f32[120,256]{1,0:T(8,128)S(1)} %get-tuple-element.70), channel_id=1, source_target_pairs={{0,24},{4,28},{8,16},{12,20},{16,8},{20,12},{24,0},{28,4},{1,25},{... | collective-permute-start | bytes 368648 | tf_op jit(solution)/shard_map/ppermute | solution.py:486
  44.4 2.3 %collective-permute-done.15 = f32[120,256]{1,0:T(8,128)S(1)} collective-permute-done((f32[120,256]{1,0:T(8,128)S(1)}, f32[120,256]{1,0:T(8,128)S(1)}, u32[]{:S(2)}, u32[]{:S(2)}) %collective-permute-start.15) | collective-permute-done | bytes 122912 | tf_op jit(solution)/shard_map/ppermute | solution.py:486
  46.7 4.1 %collective-permute-done.17 = f32[120,256]{1,0:T(8,128)S(1)} collective-permute-done((f32[120,256]{1,0:T(8,128)S(1)}, f32[120,256]{1,0:T(8,128)S(1)}, u32[]{:S(2)}, u32[]{:S(2)}) %collective-permute-start.17) | collective-permute-done | bytes 122912 | tf_op jit(solution)/shard_map/ppermute | solution.py:486
  50.8 0.5 collective-permute-start.20
  51.3 0.4 shard_map.127
  51.8 0.4 collective-permute-done.18.refs_5_
  52.1 0.2 collective-permute-done.20.refs_7_
  52.3 3.1 %shard_map.128 = f32[8,40,256]{2,1,0:T(8,128)} custom-call(f32[1,120,256]{2,1,0:T(8,128)S(1)} %bitcast.15, f32[1,120,256]{2,1,0:T(8,128)S(1)} %collective-permute-done.14.refs_1_, f32[1,120,256]{2,1,0:T(8,128)S(1)} %bitcast.17, f32[1,120,256]{2,1,0:T(8,128)S(1)} %collective-permute-done.16.refs_3_, f32[1,120,256]{2,1,0:T(8,128)S(1)} %bitcast.19, ...), custom_call_target="tpu_custom_call" | custom-call | flops 1048576 | bytes 1048576 | tf_op jit(solution)/shard_map/pallas_call | solution.py:451
  (29 shorter events, 0.1 us)
Async XLA Ops:
  0.0 5.6 %copy-start = (f32[2,3,3,128,128]{4,3,2,1,0:T(8,128)S(1)}, f32[2,3,3,128,128]{4,3,2,1,0:T(8,128)}, u32[]{:S(2)}) copy-start(f32[2,3,3,128,128]{4,3,2,1,0:T(8,128)} %space_ref.3) | copy-start | bytes 3538948
  0.0 1.2 %copy-start.1 = (f32[4,2,160,128]{3,2,1,0:T(8,128)S(1)}, f32[4,2,160,128]{3,2,1,0:T(8,128)}, u32[]{:S(2)}) copy-start(f32[4,2,160,128]{3,2,1,0:T(8,128)} %video_ref.3) | copy-start | bytes 1966084
  1.2 4.7 %copy-start.3 = (f32[2,3,128,128]{3,2,1,0:T(8,128)S(1)}, f32[2,3,128,128]{3,2,1,0:T(8,128)}, u32[]{:S(2)}) copy-start(f32[2,3,128,128]{3,2,1,0:T(8,128)} %time_ref.1) | copy-start | bytes 1179652
  1.3 4.8 %collective-permute-start = (f32[4,160,128]{2,1,0:T(8,128)S(1)}, f32[4,160,128]{2,1,0:T(8,128)S(1)}, u32[]{:S(2)}, u32[]{:S(2)}) collective-permute-start(f32[4,160,128]{2,1,0:T(8,128)S(1)} %get-tuple-element.40), channel_id=1, source_target_pairs={{0,4},{4,0},{8,12},{12,8},{16,20},{20,16},{24,28},{28,24},{1,5},{5... | collective-permute-start | bytes 983048 | tf_op jit(solution)/shard_map/ppermute | solution.py:338
  1.9 16.4 %collective-permute-start.1 = (f32[2,160,128]{2,1,0:T(8,128)S(1)}, f32[2,160,128]{2,1,0:T(8,128)S(1)}, u32[]{:S(2)}, u32[]{:S(2)}) collective-permute-start(f32[2,160,128]{2,1,0:T(8,128)S(1)} %get-tuple-element.39.far_ref.refs_0_), channel_id=1, source_target_pairs={{0,28},{4,8},{8,4},{12,16},{16,12},{20,24},{24,20},{28,0},{1,29},{... | collective-permute-start | bytes 491528 | tf_op jit(solution)/shard_map/ppermute | solution.py:341
  5.6 0.7 %copy-start.8 = (f32[2,2,128]{2,1,0:T(2,128)S(1)}, f32[2,2,128]{2,1,0:T(2,128)}, u32[]{:S(2)}) copy-start(f32[2,2,128]{2,1,0:T(2,128)} %gain_ref.15) | copy-start | bytes 6148
  5.6 7.5 %collective-permute-start.2 = (f32[2,160,128]{2,1,0:T(8,128)S(1)}, f32[2,160,128]{2,1,0:T(8,128)S(1)}, u32[]{:S(2)}, u32[]{:S(2)}) collective-permute-start(f32[2,160,128]{2,1,0:T(8,128)S(1)} %shard_map.101.far_ref.refs_1_), channel_id=1, source_target_pairs={{0,28},{4,8},{8,4},{12,16},{16,12},{20,24},{24,20},{28,0},{1,29},{... | collective-permute-start | bytes 491528 | tf_op jit(solution)/shard_map/ppermute | solution.py:341
  13.5 12.1 %collective-permute-start.3 = (f32[2,160,128]{2,1,0:T(8,128)S(1)}, f32[2,160,128]{2,1,0:T(8,128)S(1)}, u32[]{:S(2)}, u32[]{:S(2)}) collective-permute-start(f32[2,160,128]{2,1,0:T(8,128)S(1)} %shard_map.106.refs_3_), channel_id=1, source_target_pairs={{0,1},{1,2},{2,3},{3,0},{4,5},{5,6},{6,7},{7,4},{8,9},{9,10},{10,1... | collective-permute-start | bytes 491528 | tf_op jit(solution)/shard_map/ppermute | solution.py:346
  15.3 10.0 %collective-permute-start.4 = (f32[2,1,160,128]{3,2,1,0:T(8,128)S(1)}, f32[2,1,160,128]{3,2,1,0:T(8,128)S(1)}, u32[]{:S(2)}, u32[]{:S(2)}) collective-permute-start(f32[2,1,160,128]{3,2,1,0:T(8,128)S(1)} %get-tuple-element.50.refs_3_), channel_id=1, source_target_pairs={{0,1},{1,2},{2,3},{3,0},{4,5},{5,6},{6,7},{7,4},{8,9},{9,10},{10,1... | collective-permute-start | bytes 491528 | tf_op jit(solution)/shard_map/ppermute | solution.py:346
  18.2 9.7 %collective-permute-start.7 = (f32[2,160,128]{2,1,0:T(8,128)S(1)}, f32[2,160,128]{2,1,0:T(8,128)S(1)}, u32[]{:S(2)}, u32[]{:S(2)}) collective-permute-start(f32[2,160,128]{2,1,0:T(8,128)S(1)} %bitcast.13), channel_id=1, source_target_pairs={{0,4},{4,0},{8,12},{12,8},{16,20},{20,16},{24,28},{28,24},{1,5},{5... | collective-permute-start | bytes 491528 | tf_op jit(solution)/shard_map/ppermute | solution.py:338
  19.2 9.7 %collective-permute-start.8 = (f32[2,160,128]{2,1,0:T(8,128)S(1)}, f32[2,160,128]{2,1,0:T(8,128)S(1)}, u32[]{:S(2)}, u32[]{:S(2)}) collective-permute-start(f32[2,160,128]{2,1,0:T(8,128)S(1)} %get-tuple-element.48.far_ref.refs_1_), channel_id=1, source_target_pairs={{0,28},{4,8},{8,4},{12,16},{16,12},{20,24},{24,20},{28,0},{1,29},{... | collective-permute-start | bytes 491528 | tf_op jit(solution)/shard_map/ppermute | solution.py:341
  25.6 5.4 %collective-permute-start.5 = (f32[2,160,128]{2,1,0:T(8,128)S(1)}, f32[2,160,128]{2,1,0:T(8,128)S(1)}, u32[]{:S(2)}, u32[]{:S(2)}) collective-permute-start(f32[2,160,128]{2,1,0:T(8,128)S(1)} %bitcast.12), channel_id=1, source_target_pairs={{0,4},{4,0},{8,12},{12,8},{16,20},{20,16},{24,28},{28,24},{1,5},{5... | collective-permute-start | bytes 491528 | tf_op jit(solution)/shard_map/ppermute | solution.py:338
  25.9 7.0 %collective-permute-start.6 = (f32[2,160,128]{2,1,0:T(8,128)S(1)}, f32[2,160,128]{2,1,0:T(8,128)S(1)}, u32[]{:S(2)}, u32[]{:S(2)}) collective-permute-start(f32[2,160,128]{2,1,0:T(8,128)S(1)} %shard_map.109.far_ref.refs_0_), channel_id=1, source_target_pairs={{0,28},{4,8},{8,4},{12,16},{16,12},{20,24},{24,20},{28,0},{1,29},{... | collective-permute-start | bytes 491528 | tf_op jit(solution)/shard_map/ppermute | solution.py:341
  28.0 2.8 %copy-start.2 = (f32[3,3,128,256]{3,2,1,0:T(8,128)S(1)}, f32[3,3,128,256]{3,2,1,0:T(8,128)}, u32[]{:S(2)}) copy-start(f32[3,3,128,256]{3,2,1,0:T(8,128)} %down_ref.1) | copy-start | bytes 3538948
  28.9 8.4 %collective-permute-start.11 = (f32[2,1,160,128]{3,2,1,0:T(8,128)S(1)}, f32[2,1,160,128]{3,2,1,0:T(8,128)S(1)}, u32[]{:S(2)}, u32[]{:S(2)}) collective-permute-start(f32[2,1,160,128]{3,2,1,0:T(8,128)S(1)} %get-tuple-element.61.refs_3_), channel_id=1, source_target_pairs={{0,1},{1,2},{2,3},{3,0},{4,5},{5,6},{6,7},{7,4},{8,9},{9,10},{10,1... | collective-permute-start | bytes 491528 | tf_op jit(solution)/shard_map/ppermute | solution.py:346
  29.4 8.3 %collective-permute-start.9 = (f32[2,160,128]{2,1,0:T(8,128)S(1)}, f32[2,160,128]{2,1,0:T(8,128)S(1)}, u32[]{:S(2)}, u32[]{:S(2)}) collective-permute-start(f32[2,160,128]{2,1,0:T(8,128)S(1)} %shard_map.116.refs_3_), channel_id=1, source_target_pairs={{0,1},{1,0},{2,3},{3,2},{4,5},{5,4},{6,7},{7,6},{8,9},{9,8},{10,11... | collective-permute-start | bytes 491528 | tf_op jit(solution)/shard_map/ppermute | solution.py:347
  30.8 6.9 %collective-permute-start.10 = (f32[2,160,128]{2,1,0:T(8,128)S(1)}, f32[2,160,128]{2,1,0:T(8,128)S(1)}, u32[]{:S(2)}, u32[]{:S(2)}) collective-permute-start(f32[2,160,128]{2,1,0:T(8,128)S(1)} %shard_map.116.refs_3_), channel_id=1, source_target_pairs={{0,4},{4,0},{8,12},{12,8},{16,20},{20,16},{24,28},{28,24},{1,2},{5... | collective-permute-start | bytes 491528 | tf_op jit(solution)/shard_map/ppermute | solution.py:353
  38.2 1.8 %collective-permute-start.12 = (f32[2,80,256]{2,1,0:T(8,128)S(1)}, f32[2,80,256]{2,1,0:T(8,128)S(1)}, u32[]{:S(2)}, u32[]{:S(2)}) collective-permute-start(f32[2,80,256]{2,1,0:T(8,128)S(1)} %shard_map.124.refs_2_), channel_id=1, source_target_pairs={{0,4},{4,0},{8,12},{12,8},{16,20},{20,16},{24,28},{28,24},{1,5},{5... | collective-permute-start | bytes 491528 | tf_op jit(solution)/shard_map/ppermute | solution.py:338
  38.6 1.6 %collective-permute-start.13 = (f32[2,80,256]{2,1,0:T(8,128)S(1)}, f32[2,80,256]{2,1,0:T(8,128)S(1)}, u32[]{:S(2)}, u32[]{:S(2)}) collective-permute-start(f32[2,80,256]{2,1,0:T(8,128)S(1)} %shard_map.125.refs_3_), channel_id=1, source_target_pairs={{0,4},{4,0},{8,12},{12,8},{16,20},{20,16},{24,28},{28,24},{1,5},{5... | collective-permute-start | bytes 491528 | tf_op jit(solution)/shard_map/ppermute | solution.py:338
  39.6 11.8 %copy-start.4 = (f32[256,256]{1,0:T(8,128)S(1)}, f32[256,256]{1,0:T(8,128)}, u32[]{:S(2)}) copy-start(f32[256,256]{1,0:T(8,128)} %q_ref.1) | copy-start | bytes 786436
  39.6 11.7 %copy-start.5 = (f32[256,256]{1,0:T(8,128)S(1)}, f32[256,256]{1,0:T(8,128)}, u32[]{:S(2)}) copy-start(f32[256,256]{1,0:T(8,128)} %k_ref.1) | copy-start | bytes 786436
  39.6 11.7 %copy-start.6 = (f32[256,256]{1,0:T(8,128)S(1)}, f32[256,256]{1,0:T(8,128)}, u32[]{:S(2)}) copy-start(f32[256,256]{1,0:T(8,128)} %v_ref.1) | copy-start | bytes 786436
  39.6 11.7 %copy-start.7 = (f32[256,256]{1,0:T(8,128)S(1)}, f32[256,256]{1,0:T(8,128)}, u32[]{:S(2)}) copy-start(f32[256,256]{1,0:T(8,128)} %o_ref.1) | copy-start | bytes 786436
  40.0 12.3 %copy-start.9 = (f32[256]{0:T(256)S(1)}, f32[256]{0:T(256)}, u32[]{:S(2)}) copy-start(f32[256]{0:T(256)} %param.15) | copy-start | bytes 3076
  40.5 6.2 %collective-permute-start.15 = (f32[120,256]{1,0:T(8,128)S(1)}, f32[120,256]{1,0:T(8,128)S(1)}, u32[]{:S(2)}, u32[]{:S(2)}) collective-permute-start(f32[120,256]{1,0:T(8,128)S(1)} %get-tuple-element.68), channel_id=1, source_target_pairs={{0,8},{4,12},{8,0},{12,4},{16,24},{20,28},{24,16},{28,20},{1,9},{5... | collective-permute-start | bytes 368648 | tf_op jit(solution)/shard_map/ppermute | solution.py:486
  42.8 7.9 %collective-permute-start.17 = (f32[120,256]{1,0:T(8,128)S(1)}, f32[120,256]{1,0:T(8,128)S(1)}, u32[]{:S(2)}, u32[]{:S(2)}) collective-permute-start(f32[120,256]{1,0:T(8,128)S(1)} %get-tuple-element.69), channel_id=1, source_target_pairs={{0,16},{4,20},{8,24},{12,28},{16,0},{20,4},{24,8},{28,12},{1,17},{... | collective-permute-start | bytes 368648 | tf_op jit(solution)/shard_map/ppermute | solution.py:486
  43.6 7.2 %collective-permute-start.19 = (f32[120,256]{1,0:T(8,128)S(1)}, f32[120,256]{1,0:T(8,128)S(1)}, u32[]{:S(2)}, u32[]{:S(2)}) collective-permute-start(f32[120,256]{1,0:T(8,128)S(1)} %get-tuple-element.70), channel_id=1, source_target_pairs={{0,24},{4,28},{8,16},{12,20},{16,8},{20,12},{24,0},{28,4},{1,25},{... | collective-permute-start | bytes 368648 | tf_op jit(solution)/shard_map/ppermute | solution.py:486
  44.4 7.4 %collective-permute-start.14 = (f32[1,120,256]{2,1,0:T(8,128)S(1)}, f32[1,120,256]{2,1,0:T(8,128)S(1)}, u32[]{:S(2)}, u32[]{:S(2)}) collective-permute-start(f32[1,120,256]{2,1,0:T(8,128)S(1)} %bitcast.14), channel_id=1, source_target_pairs={{0,4},{4,0},{8,12},{12,8},{16,20},{20,16},{24,28},{28,24},{1,5},{5... | collective-permute-start | bytes 368648 | tf_op jit(solution)/shard_map/ppermute | solution.py:492
  46.7 5.1 %collective-permute-start.16 = (f32[1,120,256]{2,1,0:T(8,128)S(1)}, f32[1,120,256]{2,1,0:T(8,128)S(1)}, u32[]{:S(2)}, u32[]{:S(2)}) collective-permute-start(f32[1,120,256]{2,1,0:T(8,128)S(1)} %bitcast.16), channel_id=1, source_target_pairs={{0,4},{4,0},{8,12},{12,8},{16,20},{20,16},{24,28},{28,24},{1,5},{5... | collective-permute-start | bytes 368648 | tf_op jit(solution)/shard_map/ppermute | solution.py:492
  50.8 1.3 %collective-permute-start.18 = (f32[1,120,256]{2,1,0:T(8,128)S(1)}, f32[1,120,256]{2,1,0:T(8,128)S(1)}, u32[]{:S(2)}, u32[]{:S(2)}) collective-permute-start(f32[1,120,256]{2,1,0:T(8,128)S(1)} %bitcast.18), channel_id=1, source_target_pairs={{0,4},{4,0},{8,12},{12,8},{16,20},{20,16},{24,28},{28,24},{1,5},{5... | collective-permute-start | bytes 368648 | tf_op jit(solution)/shard_map/ppermute | solution.py:492
  50.8 1.5 %collective-permute-start.20 = (f32[1,120,256]{2,1,0:T(8,128)S(1)}, f32[1,120,256]{2,1,0:T(8,128)S(1)}, u32[]{:S(2)}, u32[]{:S(2)}) collective-permute-start(f32[1,120,256]{2,1,0:T(8,128)S(1)} %bitcast.20), channel_id=1, source_target_pairs={{0,4},{4,0},{8,12},{12,8},{16,20},{20,16},{24,28},{28,24},{1,5},{5... | collective-permute-start | bytes 368648 | tf_op jit(solution)/shard_map/ppermute | solution.py:492
